TPU v7x, 32 devices: a whole 2x2x4 slice. The times are simulated.
32 devices in a mesh: shard: 8 (over z, x), tensor: 4 (over y, core).
Axes of the slice: x: 2, y: 2, z: 4, core: 2. Of those that a mesh axis runs over, the one named last changes fastest.
Arguments:
- att_grads: float32 [2, 4, 768, 768], P(None, None, 'shard', 'tensor'), may hold values from -6 to 6
- glu_grads: float32 [2, 4, 768, 1024], P(None, None, 'shard', 'tensor'), may hold values from -6 to 6
- att_weight: float32 [4, 768, 768], P(None, 'shard', 'tensor'), may hold values from -0.21875 to 0.21875
- att_moment: float32 [4, 768, 768], P(None, 'shard', 'tensor'), may hold values from -4 to 4
- att_second: float32 [4, 768, 768], P(None, 'shard', 'tensor'), may hold values from 0.05 to 1
- glu_weight: float32 [4, 768, 1024], P(None, 'shard', 'tensor'), may hold values from -0.21875 to 0.21875
- glu_moment: float32 [4, 768, 1024], P(None, 'shard', 'tensor'), may hold values from -4 to 4
- glu_second: float32 [4, 768, 1024], P(None, 'shard', 'tensor'), may hold values from 0.05 to 1
- att_stats: float32 [8, 2, 768, 768], P('shard', None, 'tensor'), may hold values from -1 to 10
- att_left_root: bfloat16 [8, 768, 768], P('shard', 'tensor'), may hold values from -1 to 2
- att_right_root: bfloat16 [8, 768, 768], P('shard', None, 'tensor'), may hold values from -1 to 2
- glu_left_stat: float32 [8, 768, 768], P('shard', 'tensor'), may hold values from -1 to 10
- glu_right_stat: float32 [8, 1024, 1024], P('shard', 'tensor'), may hold values from -1 to 10
- glu_left_root: bfloat16 [8, 768, 768], P('shard', 'tensor'), may hold values from -1 to 2
- glu_right_root: bfloat16 [8, 1024, 1024], P('shard', None, 'tensor'), may hold values from -1 to 2
- att_owner: int32 [4], replicated, may hold values from 0 to 7, as said below
- glu_owner: int32 [4], replicated, may hold values from 0 to 7, as said below
Outputs:
- att_weight_out: float32 [4, 768, 768], P(None, 'shard', 'tensor')
- att_moment_out: float32 [4, 768, 768], P(None, 'shard', 'tensor')
- att_second_out: float32 [4, 768, 768], P(None, 'shard', 'tensor')
- glu_weight_out: float32 [4, 768, 1024], P(None, 'shard', 'tensor')
- glu_moment_out: float32 [4, 768, 1024], P(None, 'shard', 'tensor')
- glu_second_out: float32 [4, 768, 1024], P(None, 'shard', 'tensor')
- att_stats_out: float32 [8, 2, 768, 768], P('shard', None, 'tensor')
- glu_left_out: float32 [8, 768, 768], P('shard', 'tensor')
- glu_right_out: float32 [8, 1024, 1024], P('shard', 'tensor')
Inputs may be any that keep to these rules, and one draw needn't show every extreme that they name: `att_owner`: distinct owners; no owner holds more than one attention matrix. `glu_owner`: distinct owners; no owner holds more than one GeGLU block; in every draw some owner holds an attention matrix and a GeGLU block.
All inputs are finite; a program needn't handle non-finite values.
Results may differ from a plain program's by a relative error of at most 0.0014.
Values may be sent and summed in bfloat16 or wider, within the bound.
No kernel may reach another device: no remote copies, remote signals or barrier semaphores. Data moves between devices by JAX's collectives and lax.ppermute only.
A program may use at most 128 MiB of HBM per device.

v0:
```python
import jax
import jax.numpy as jnp
from jax import lax
from jax.sharding import PartitionSpec as P

beta_one = 0.9
beta_two = 0.999
beta_stat = 0.999
adam_eps = 1e-08
graft_eps = 1e-06
learn_rate = 0.01
top_precision = lax.Precision.HIGHEST


def adam_part(grads, moment, second):
    summed = jnp.sum(grads, axis=0)
    moment_new = beta_one * moment + (1.0 - beta_one) * summed
    second_new = beta_two * second + (1.0 - beta_two) * summed * summed
    direction = moment_new / (jnp.sqrt(second_new) + adam_eps)
    adam_sq = jnp.sum(direction * direction, axis=(1, 2))
    return (summed, moment_new, second_new, adam_sq)


def owner_table(owner_list, count):
    places = lax.broadcasted_iota(jnp.int32, (count, owner_list.shape[0]), 0)
    unit_ids = lax.broadcasted_iota(jnp.int32, (count, owner_list.shape[0]), 1)
    matched = owner_list[None, :] == places
    present = jnp.any(matched, axis=1)
    unit_index = jnp.sum(jnp.where(matched, unit_ids, 0), axis=1)
    return (present, unit_index)


def owner_rows(values, present, unit_index):
    picked = jnp.take(values, unit_index, axis=0)
    return jnp.where(present[:, None, None], picked, 0.0)


def refresh(operands):
    grad, row_start, col_start, left_stat, right_stat, left_root = operands
    row_block = lax.dynamic_slice_in_dim(grad, row_start, left_stat.shape[0], 0)
    col_block = lax.dynamic_slice_in_dim(grad, col_start, right_stat.shape[0], 1)
    outer_left = lax.dot_general(row_block, grad, (((1,), (1,)), ((), ())), precision=top_precision)
    outer_right = lax.dot_general(
        col_block, grad, (((0,), (0,)), ((), ())), precision=top_precision
    )
    left_new = beta_stat * left_stat + (1.0 - beta_stat) * outer_left
    right_new = beta_stat * right_stat + (1.0 - beta_stat) * outer_right
    halfway = jnp.dot(
        left_root, grad.astype(jnp.bfloat16), preferred_element_type=jnp.float32
    ).astype(jnp.bfloat16)
    return (left_new, right_new, halfway)


def keep_stats(operands):
    grad, row_start, col_start, left_stat, right_stat, left_root = operands
    return (left_stat, right_stat, jnp.zeros((left_root.shape[0], grad.shape[1]), jnp.bfloat16))


def right_product(flag, piece, root):

    def compute(operands):
        return jnp.dot(operands[0], operands[1], preferred_element_type=jnp.float32)

    def nothing(operands):
        return jnp.zeros((operands[0].shape[0], operands[1].shape[1]), jnp.float32)

    return lax.cond(flag, compute, nothing, (piece, root))


def per_device(
    att_grads,
    glu_grads,
    att_weight,
    att_moment,
    att_second,
    glu_weight,
    glu_moment,
    glu_second,
    att_stats,
    att_left_root,
    att_right_root,
    glu_left_stat,
    glu_right_stat,
    glu_left_root,
    glu_right_root,
    att_owner,
    glu_owner,
):
    owners = lax.axis_size("shard")
    my_shard = lax.axis_index("shard")
    my_part = lax.axis_index("tensor")
    att_sum, att_moment_out, att_second_out, att_adam = adam_part(att_grads, att_moment, att_second)
    glu_sum, glu_moment_out, glu_second_out, glu_adam = adam_part(glu_grads, glu_moment, glu_second)
    att_present, att_index = owner_table(att_owner, owners)
    glu_present, glu_index = owner_table(glu_owner, owners)
    att_rows_full, glu_rows_full = (
        lax.all_gather(att_sum.astype(jnp.bfloat16), "tensor", axis=2, tiled=True).astype(
            att_sum.dtype
        ),
        lax.all_gather(glu_sum.astype(jnp.bfloat16), "tensor", axis=2, tiled=True).astype(
            glu_sum.dtype
        ),
    )
    att_send = owner_rows(att_rows_full, att_present, att_index)
    glu_send = owner_rows(glu_rows_full, glu_present, glu_index)
    att_recv, glu_recv = (
        lax.all_to_all(
            att_send.astype(jnp.bfloat16), "shard", split_axis=0, concat_axis=1, tiled=True
        ).astype(att_send.dtype),
        lax.all_to_all(
            glu_send.astype(jnp.bfloat16), "shard", split_axis=0, concat_axis=1, tiled=True
        ).astype(glu_send.dtype),
    )
    att_grad = att_recv[0]
    glu_grad = glu_recv[0]
    att_mine = jnp.any(att_owner == my_shard)
    glu_mine = jnp.any(glu_owner == my_shard)
    att_right_local = att_right_root[0]
    glu_right_local = glu_right_root[0]
    att_operands = (
        att_grad,
        my_part * att_stats.shape[2],
        my_part * att_right_local.shape[1],
        att_stats[0, 0],
        att_stats[0, 1],
        att_left_root[0],
    )
    att_left_new, att_right_new, att_half = lax.cond(att_mine, refresh, keep_stats, att_operands)
    glu_operands = (
        glu_grad,
        my_part * glu_left_stat.shape[1],
        my_part * glu_right_local.shape[1],
        glu_left_stat[0],
        glu_right_stat[0],
        glu_left_root[0],
    )
    glu_left_new, glu_right_new, glu_half = lax.cond(glu_mine, refresh, keep_stats, glu_operands)
    att_done = right_product(
        att_mine, lax.all_gather(att_half, "tensor", axis=0, tiled=True), att_right_local
    )
    glu_done = right_product(
        glu_mine, lax.all_gather(glu_half, "tensor", axis=0, tiled=True), glu_right_local
    )
    att_total, glu_total = lax.psum((att_adam, glu_adam), ("shard", "tensor"))
    att_norm_mine = jnp.sum(jnp.where(att_owner == my_shard, att_total, 0.0))
    glu_norm_mine = jnp.sum(jnp.where(glu_owner == my_shard, glu_total, 0.0))
    att_pnorm, glu_pnorm = lax.psum(
        (jnp.sum(att_done * att_done), jnp.sum(glu_done * glu_done)), "tensor"
    )
    att_out = jnp.sqrt(att_norm_mine / (att_pnorm + graft_eps)) * att_done
    glu_out = jnp.sqrt(glu_norm_mine / (glu_pnorm + graft_eps)) * glu_done
    rows_here = att_grads.shape[2]
    att_back, glu_back = (
        lax.all_to_all(
            att_out.reshape(owners, rows_here, att_out.shape[1]).astype(jnp.bfloat16),
            "shard",
            split_axis=0,
            concat_axis=0,
            tiled=True,
        ).astype(jnp.float32),
        lax.all_to_all(
            glu_out.reshape(owners, rows_here, glu_out.shape[1]).astype(jnp.bfloat16),
            "shard",
            split_axis=0,
            concat_axis=0,
            tiled=True,
        ).astype(jnp.float32),
    )
    att_update = jnp.take(att_back, att_owner, axis=0)
    glu_update = jnp.take(glu_back, glu_owner, axis=0)
    att_weight_out = att_weight - learn_rate * att_update
    glu_weight_out = glu_weight - learn_rate * glu_update
    att_stats_out = jnp.stack([att_left_new, att_right_new])[None]
    return (
        att_weight_out,
        att_moment_out,
        att_second_out,
        glu_weight_out,
        glu_moment_out,
        glu_second_out,
        att_stats_out,
        glu_left_new[None],
        glu_right_new[None],
    )


def solution(mesh):
    placed = (
        P(None, None, "shard", "tensor"),
        P(None, None, "shard", "tensor"),
        P(None, "shard", "tensor"),
        P(None, "shard", "tensor"),
        P(None, "shard", "tensor"),
        P(None, "shard", "tensor"),
        P(None, "shard", "tensor"),
        P(None, "shard", "tensor"),
        P("shard", None, "tensor", None),
        P("shard", "tensor", None),
        P("shard", None, "tensor"),
        P("shard", "tensor", None),
        P("shard", "tensor", None),
        P("shard", "tensor", None),
        P("shard", None, "tensor"),
        P(),
        P(),
    )
    return jax.shard_map(
        per_device,
        mesh=mesh,
        in_specs=placed,
        out_specs=(
            P(None, "shard", "tensor"),
            P(None, "shard", "tensor"),
            P(None, "shard", "tensor"),
            P(None, "shard", "tensor"),
            P(None, "shard", "tensor"),
            P(None, "shard", "tensor"),
            P("shard", None, "tensor", None),
            P("shard", "tensor", None),
            P("shard", "tensor", None),
        ),
        check_vma=False,
    )
```

profile of v0, /device:TPU:0, one launch (start us, length us, event | category | flops | bytes accessed | tf_op | source)
XLA Modules:
  0.0 198.3 jit_solution(5837012286356567686)
XLA Ops:
  7.2 2.0 %copy.73 = f32[1,192,768]{2,1,0:T(8,128)} copy(f32[1,192,768]{2,1,0:T(8,128)} %param.36) | data formatting | bytes 1179648
  10.9 1.1 multiply_reduce_fusion.3
  12.2 10.1 %all_gather.12 = bf16[4,96,768]{1,0,2:T(4,128)(2,1)S(1)} all-gather(bf16[4,96,192]{1,0,2:T(4,128)(2,1)S(1)} %copy.51), channel_id=1, replica_groups=mesh['shard'=8,'tensor'=4] {'tensor'}, dimensions={2}, use_global_device_ids=true | all-gather | bytes 737280 | tf_op jit(solution)/shard_map/all_gather | solution.py:97
  23.5 1.4 select_convert_fusion.1
  24.9 5.9 %all-to-all-start = ((bf16[8,96,768]{2,1,0:T(8,128)(2,1)}), bf16[8,96,768]{2,1,0:T(8,128)(2,1)S(1)}, u32[]{:S(2)}, u32[]{:S(2)}) async-start(bf16[8,96,768]{2,1,0:T(8,128)(2,1)} %select_convert_fusion.1), calls=%async_computation | async-start | bytes 2359296 | tf_op jit(solution)/shard_map/all_to_all | solution.py:107
  33.1 8.4 %all_gather.14 = bf16[4,96,1024]{2,1,0:T(8,128)(2,1)S(1)} all-gather(bf16[4,96,256]{2,1,0:T(8,128)(2,1)S(1)} %get-tuple-element.162), channel_id=1, replica_groups=mesh['shard'=8,'tensor'=4] {'tensor'}, dimensions={2}, use_global_device_ids=true | all-gather | bytes 983040 | tf_op jit(solution)/shard_map/all_gather | solution.py:100
  41.5 1.8 gather_fusion.2
  43.4 3.1 %select_convert_fusion = bf16[8,96,1024]{2,1,0:T(8,128)(2,1)} fusion(bf16[8,96,1024]{2,1,0:T(8,128)(2,1)} %gather_fusion.2, pred[8]{0:T(512)(128)(4,1)S(1)} %compare_and_fusion, pred[8]{0:T(512)(128)(4,1)S(1)} %fusion.20), kind=kLoop, calls=%fused_computation.28 | loop fusion | flops 1572864 | bytes 3145744 | tf_op jit(solution)/shard_map/convert_element_type | solution.py:111
  46.5 13.4 %all-to-all-done = bf16[8,96,768]{2,1,0:T(8,128)(2,1)S(1)} async-done(((bf16[8,96,768]{2,1,0:T(8,128)(2,1)}), bf16[8,96,768]{2,1,0:T(8,128)(2,1)S(1)}, u32[]{:S(2)}, u32[]{:S(2)}) %all-to-all-start) | async-done | bytes 1179680 | tf_op jit(solution)/shard_map/all_to_all | solution.py:107
  59.9 3.6 %all-to-all-start.2 = ((bf16[8,96,1024]{2,1,0:T(8,128)(2,1)}), bf16[8,96,1024]{2,1,0:T(8,128)(2,1)S(1)}, u32[]{:S(2)}, u32[]{:S(2)}) async-start(bf16[8,96,1024]{2,1,0:T(8,128)(2,1)} %select_convert_fusion), calls=%async_computation.2 | async-start | bytes 3145728 | tf_op jit(solution)/shard_map/all_to_all | solution.py:110
  64.9 2.1 %slice_bitcast_fusion = (f32[192,768]{1,0:T(8,128)S(1)}, f32[192,768]{1,0:T(8,128)}) fusion(f32[1,2,192,768]{3,2,1,0:T(8,128)} %param.33), kind=kLoop, calls=%fused_computation.37 | loop fusion | bytes 2359296 | tf_op jit(solution)/shard_map/squeeze | solution.py:125
  67.0 4.5 %conditional.4 = (f32[192,768]{1,0:T(8,128)}, f32[192,768]{1,0:T(8,128)S(1)}, bf16[192,768]{1,0:T(8,128)(2,1)}) conditional(s32[]{:T(128)} %convert_element_type.69, (f32[192,768]{1,0:T(8,128)}, f32[192,768]{1,0:T(8,128)S(1)}) %tuple.40, (f32[192,768]{1,0:T(8,128)}, bf16[8,96,768]{2,1,0:T(8,128)(2,1)S(1)}, s32[]{:T(128)}, f32[192,768]{1,0:T(8,128)S(1)}, ...), branch_computations={%region_7.8_spmd, %region_8.9_spmd} | conditional | flops 680509440 | bytes 8355934 | solution.py:128
  67.0 2.5 %fusion = f32[192,768]{1,0:T(8,128)} fusion(bf16[768,768]{1,0:T(8,128)(2,1)S(1)} %bitcast.48, f32[192,768]{1,0:T(8,128)} %get-tuple-element.69, s32[]{:T(128)S(6)} %select_n.72), kind=kOutput, calls=%fused_computation.6 | convolution fusion | flops 226934784 | bytes 2654212 | tf_op jit(solution)/shard_map/cond/branch_1_fun/dot_general | solution.py:42
  70.4 1.1 convolution_convert_fusion
  72.9 27.8 %all-to-all-done.2 = bf16[8,96,1024]{2,1,0:T(8,128)(2,1)S(1)} async-done(((bf16[8,96,1024]{2,1,0:T(8,128)(2,1)}), bf16[8,96,1024]{2,1,0:T(8,128)(2,1)S(1)}, u32[]{:S(2)}, u32[]{:S(2)}) %all-to-all-start.2) | async-done | bytes 1572896 | tf_op jit(solution)/shard_map/all_to_all | solution.py:110
  101.6 41.7 %all-reduce = (f32[4]{0:T(128)S(1)}, f32[4]{0:T(128)S(1)}) all-reduce(f32[4]{0:T(128)S(1)} %get-tuple-element.157, f32[4]{0:T(128)S(1)} %get-tuple-element.154), channel_id=1, replica_groups=mesh['shard'=8,'tensor'=4] {'shard','tensor'}, use_global_device_ids=true, to_apply=%region_2.0 | all-reduce | flops 8 | bytes 64 | tf_op jit(solution)/shard_map/psum | solution.py:144
  143.3 1.9 conditional.5
  143.3 1.9 fusion.7
  147.4 6.5 %all-reduce.1 = (f32[]{:T(128)}, f32[]{:T(128)}) all-reduce(f32[]{:T(128)} %multiply_reduce_fusion.1, f32[]{:T(128)} %multiply_reduce_fusion), channel_id=1, replica_groups=mesh['shard'=8,'tensor'=4] {'tensor'}, use_global_device_ids=true, to_apply=%region_12.13 | all-reduce | flops 2 | bytes 16 | tf_op jit(solution)/shard_map/psum | solution.py:147
  156.3 6.2 %all-to-all-start.1 = ((bf16[8,96,192]{2,1,0:T(8,128)(2,1)}), bf16[8,96,192]{2,1,0:T(8,128)(2,1)S(1)}, u32[]{:S(2)}, u32[]{:S(2)}) async-start(bf16[8,96,192]{2,1,0:T(8,128)(2,1)} %bitcast.10), calls=%async_computation.1 | async-start | bytes 786432 | tf_op jit(solution)/shard_map/all_to_all | solution.py:154
  165.2 9.2 %all-to-all-done.1 = bf16[8,96,192]{2,1,0:T(8,128)(2,1)S(1)} async-done(((bf16[8,96,192]{2,1,0:T(8,128)(2,1)}), bf16[8,96,192]{2,1,0:T(8,128)(2,1)S(1)}, u32[]{:S(2)}, u32[]{:S(2)}) %all-to-all-start.1) | async-done | bytes 294944 | tf_op jit(solution)/shard_map/all_to_all | solution.py:154
  174.4 3.6 %all-to-all-start.3 = ((bf16[8,96,256]{2,1,0:T(8,128)(2,1)}), bf16[8,96,256]{2,1,0:T(8,128)(2,1)S(1)}, u32[]{:S(2)}, u32[]{:S(2)}) async-start(bf16[8,96,256]{2,1,0:T(8,128)(2,1)} %bitcast.15), calls=%async_computation.3 | async-start | bytes 786432 | tf_op jit(solution)/shard_map/all_to_all | solution.py:161
  178.1 2.2 %maximum_bitcast_fusion = f32[1,2,192,768]{3,2,1,0:T(8,128)} fusion(f32[1,192,768]{2,1,0:T(8,128)S(1)} %bitcast.51, f32[1,192,768]{2,1,0:T(8,128)} %bitcast.16), kind=kLoop, calls=%fused_computation.30 | loop fusion | flops 294912 | bytes 2359296 | tf_op jit(solution)/shard_map/broadcast_in_dim | solution.py:173
  182.1 7.8 %all-to-all-done.3 = bf16[8,96,256]{2,1,0:T(8,128)(2,1)S(1)} async-done(((bf16[8,96,256]{2,1,0:T(8,128)(2,1)}), bf16[8,96,256]{2,1,0:T(8,128)(2,1)S(1)}, u32[]{:S(2)}, u32[]{:S(2)}) %all-to-all-start.3) | async-done | bytes 393248 | tf_op jit(solution)/shard_map/all_to_all | solution.py:161
  (73 shorter events, 17.3 us)
Async XLA Ops:
  7.2 2.0 %copy-start.2 = (f32[1,256,1024]{2,1,0:T(8,128)S(1)}, f32[1,256,1024]{2,1,0:T(8,128)}, u32[]{:S(2)}) copy-start(f32[1,256,1024]{2,1,0:T(8,128)} %param.37) | copy-start | bytes 3145732
  9.2 1.0 copy-start.15
  9.2 1.5 copy-start.3
  9.2 1.6 copy-start.6
  9.2 1.7 copy-start.7
  24.9 5.9 %copy-start.4 = (f32[2,4,96,256]{3,2,1,0:T(8,128)S(1)}, f32[2,4,96,256]{3,2,1,0:T(8,128)}, u32[]{:S(2)}) copy-start(f32[2,4,96,256]{3,2,1,0:T(8,128)} %param.26) | copy-start | bytes 2359300
  24.9 35.0 %all-to-all-start = ((bf16[8,96,768]{2,1,0:T(8,128)(2,1)}), bf16[8,96,768]{2,1,0:T(8,128)(2,1)S(1)}, u32[]{:S(2)}, u32[]{:S(2)}) async-start(bf16[8,96,768]{2,1,0:T(8,128)(2,1)} %select_convert_fusion.1), calls=%async_computation | async-start | bytes 2359296 | tf_op jit(solution)/shard_map/all_to_all | solution.py:107
  30.8 0.7 copy-start.14
  30.8 1.0 copy-start.8
  30.8 1.1 copy-start.9
  59.9 40.8 %all-to-all-start.2 = ((bf16[8,96,1024]{2,1,0:T(8,128)(2,1)}), bf16[8,96,1024]{2,1,0:T(8,128)(2,1)S(1)}, u32[]{:S(2)}, u32[]{:S(2)}) async-start(bf16[8,96,1024]{2,1,0:T(8,128)(2,1)} %select_convert_fusion), calls=%async_computation.2 | async-start | bytes 3145728 | tf_op jit(solution)/shard_map/all_to_all | solution.py:110
  63.5 79.7 %all-gather.3.cloned.1.call-start = ((), (), s32[]{:S(2)}) async-start(), calls=%async_computation.4 | async-start | bytes 1474560 | tf_op jit(solution)/shard_map/all_gather | solution.py:139
  69.5 1.0 copy-start.13
  71.6 74.4 %all-gather.5.cloned.1.call-start = ((), (), s32[]{:S(2)}) async-start(), calls=%async_computation.5 | async-start | bytes 1966080 | tf_op jit(solution)/shard_map/all_gather | solution.py:142
  143.3 2.7 %copy-start.5 = (bf16[1,1024,256]{2,1,0:T(8,128)(2,1)S(1)}, bf16[1,1024,256]{2,1,0:T(8,128)(2,1)}, u32[]{:S(2)}) copy-start(bf16[1,1024,256]{2,1,0:T(8,128)(2,1)} %param.39) | copy-start | bytes 1572868
  156.3 18.2 %all-to-all-start.1 = ((bf16[8,96,192]{2,1,0:T(8,128)(2,1)}), bf16[8,96,192]{2,1,0:T(8,128)(2,1)S(1)}, u32[]{:S(2)}, u32[]{:S(2)}) async-start(bf16[8,96,192]{2,1,0:T(8,128)(2,1)} %bitcast.10), calls=%async_computation.1 | async-start | bytes 786432 | tf_op jit(solution)/shard_map/all_to_all | solution.py:154
  174.4 15.5 %all-to-all-start.3 = ((bf16[8,96,256]{2,1,0:T(8,128)(2,1)}), bf16[8,96,256]{2,1,0:T(8,128)(2,1)S(1)}, u32[]{:S(2)}, u32[]{:S(2)}) async-start(bf16[8,96,256]{2,1,0:T(8,128)(2,1)} %bitcast.15), calls=%async_computation.3 | async-start | bytes 786432 | tf_op jit(solution)/shard_map/all_to_all | solution.py:161
  180.2 1.0 copy-start.10
  182.1 8.5 %copy-start.11 = (f32[4,96,256]{2,1,0:T(8,128)S(1)}, f32[4,96,256]{2,1,0:T(8,128)}, u32[]{:S(2)}) copy-start(f32[4,96,256]{2,1,0:T(8,128)} %param.30) | copy-start | bytes 1179652
Sparse Core Ops, SparseCore 0:
  71.7 17.5 all-gather.2
  101.7 22.5 all-gather.4
where the time goes:
time: 200 us; the launch traced here: 198 us
  blocking collectives  66.8 us (33%)
  waiting for transfers between devices  58.3 us (29%)
  starting transfers between devices  19.5 us (10%)
  between operations  18.2 us (9%)
  other arithmetic  16.1 us (8%)
  local copies, waits for them, and re-layouts  13.2 us (7%)
  matrix products  6.18 us (3%)
    psum x1, blocking collectives, per_device(): att_total, glu_total = lax.psum((att_adam, glu_adam), ('shard', 'tensor'))  41.7 us
    all_to_all x1, waiting for transfers between devices, per_device(): lax.all_to_all(glu_send.astype(jnp.bfloat16), 'shard', split_axis=0, conc...  27.8 us
    all_to_all x1, waiting for transfers between devices, per_device(): lax.all_to_all(att_send.astype(jnp.bfloat16), 'shard', split_axis=0, conc...  13.4 us
    all_gather x1, blocking collectives, per_device(): lax.all_gather(att_sum.astype(jnp.bfloat16), 'tensor', axis=2, tiled=True)  10.1 us
    all_to_all x1, waiting for transfers between devices, per_device(): lax.all_to_all(att_out.reshape(owners, rows_here, att_out.shape[1]).astyp...  9.22 us
    all_gather x1, blocking collectives, per_device(): lax.all_gather(glu_sum.astype(jnp.bfloat16), 'tensor', axis=2, tiled=True)  8.43 us
    all_to_all x1, waiting for transfers between devices, per_device(): lax.all_to_all(glu_out.reshape(owners, rows_here, glu_out.shape[1]).astyp...  7.82 us
    psum x1, blocking collectives, per_device(): lax.psum((jnp.sum(att_done * att_done), jnp.sum(glu_done * glu_done)), 't...  6.54 us
  transfers between devices with their start and end apart: 6, of which 4 were waited for; matrix products, arithmetic and copies ran while one was open for 11% of the time, Pallas kernels for 0%

commit v1 on v0

v1 whole, which is shorter than its diff:
```python
import functools

import jax
import jax.numpy as jnp
from jax import lax
from jax.experimental import pallas as pl
from jax.experimental.pallas import tpu as pltpu
from jax.sharding import PartitionSpec as P

beta_one = 0.9
beta_two = 0.999
beta_stat = 0.999
adam_eps = 1e-08
graft_eps = 1e-06
learn_rate = 0.01

bf16 = jnp.bfloat16
f32 = jnp.float32
LANES = 128
VMEM = pl.BlockSpec(memory_space=pltpu.VMEM)
SMEM = pl.BlockSpec(memory_space=pltpu.SMEM)


def round_up(value, step):
    return -(-value // step) * step


def packed_shape(rows, cols):
    lanes = round_up(cols, LANES)
    return (rows, lanes) if lanes > cols else (round_up(rows + 3, 8), cols)


def pieces(total, shape):
    full = jnp.full(shape, total, f32)
    high = full.astype(bf16).astype(f32)
    middle = (full - high).astype(bf16).astype(f32)
    low = full - high - middle
    row = lax.broadcasted_iota(jnp.int32, shape, 0)
    column = lax.broadcasted_iota(jnp.int32, shape, 1)
    value = jnp.where(row == 0, high, jnp.where(row == 1, middle, jnp.where(row == 2, low, 0.0)))
    return jnp.where(column == 0, value, 0.0).astype(bf16)


def adam_kernel(owner, grads, moment, second, packed, moment_out, second_out):
    rows, cols = moment.shape[1:]
    packed_rows, packed_cols = packed.shape[1:]
    packed[...] = jnp.zeros_like(packed)

    def unit(u, carry):
        summed = grads[0, u]
        for micro in range(1, grads.shape[0]):
            summed = summed + grads[micro, u]
        moment_new = beta_one * moment[u] + (1.0 - beta_one) * summed
        second_new = beta_two * second[u] + (1.0 - beta_two) * summed * summed
        direction = moment_new / (jnp.sqrt(second_new) + adam_eps)
        moment_out[u] = moment_new
        second_out[u] = second_new
        total = jnp.sum(direction * direction)
        slot = owner[u]
        if packed_cols > cols:
            packed[slot, :, :cols] = summed.astype(bf16)
            packed[slot, :, cols:] = pieces(total, (packed_rows, packed_cols - cols))
        else:
            packed[slot, :rows, :] = summed.astype(bf16)
            packed[slot, rows:, :] = pieces(total, (packed_rows - rows, packed_cols))
        return carry

    lax.fori_loop(0, moment.shape[0], unit, 0, unroll=moment.shape[0] <= 4)


def adam_part(owner, grads, moment, second, owners):
    rows, cols = moment.shape[1:]
    packed = jax.ShapeDtypeStruct((owners, *packed_shape(rows, cols)), bf16)
    return pl.pallas_call(
        adam_kernel,
        out_shape=(
            packed,
            jax.ShapeDtypeStruct(moment.shape, f32),
            jax.ShapeDtypeStruct(second.shape, f32),
        ),
        in_specs=[SMEM, VMEM, VMEM, VMEM],
        out_specs=(VMEM, VMEM, VMEM),
        cost_estimate=pl.CostEstimate(
            flops=20 * moment.size, bytes_accessed=32 * moment.size, transcendentals=moment.size
        ),
    )(owner, grads, moment, second)


def holds(owner):
    me = lax.axis_index("shard")
    found = owner[0] == me
    for unit in range(1, owner.shape[0]):
        found = jnp.logical_or(found, owner[unit] == me)
    return found


def block(ref, rows, cols, start=0, count=None):
    count = ref.shape[0] if count is None else count
    return ref[pl.ds(start, count), :rows, :cols].reshape(count * rows, cols)


def shampoo_kernel(rows, cols, owner, *refs):
    tensor = lax.axis_size("tensor")
    left, grad, (root, out, norm, adam, half) = refs[:tensor], refs[tensor : 2 * tensor], refs[2 * tensor :]
    part = lax.axis_index("tensor")

    @pl.when(holds(owner))
    def _():
        depth = left[0].shape[0]
        total = jnp.zeros(out.shape, f32)
        adam_sq = jnp.zeros((), f32)
        for k in range(tensor):
            columns = block(grad[k], rows, cols)
            for i in range(tensor):
                product = jnp.dot(left[i][...], columns, preferred_element_type=f32)
                place = pl.multiple_of((part ^ i) * depth, depth)
                half[k, pl.ds(place, depth), :] = product.astype(bf16)
            if grad[k].shape[2] > cols:
                extra = grad[k][:, :, cols:]
            else:
                extra = grad[k][:, rows:, :]
            adam_sq = adam_sq + jnp.sum(extra.astype(f32))
        for k in range(tensor):
            place = pl.multiple_of((part ^ k) * cols, cols)
            total = total + jnp.dot(
                half[k], root[0, pl.ds(place, cols), :], preferred_element_type=f32
            )
        out[...] = total
        norm[...] = jnp.full(norm.shape, jnp.sum(total * total), f32)
        adam[...] = jnp.full(adam.shape, adam_sq, f32)

    @pl.when(jnp.logical_not(holds(owner)))
    def _():
        out[...] = jnp.zeros_like(out)
        norm[...] = jnp.zeros_like(norm)
        adam[...] = jnp.zeros_like(adam)


def shampoo_part(owner, left, grad, root, rows):
    cols = root.shape[2]
    depth = left[0].shape[1]
    tensor = len(left)
    small = jax.ShapeDtypeStruct((8, LANES), f32)
    return pl.pallas_call(
        functools.partial(shampoo_kernel, rows, cols),
        out_shape=(jax.ShapeDtypeStruct((depth, cols), f32), small, small),
        in_specs=[SMEM] + [VMEM] * (2 * tensor + 1),
        out_specs=(VMEM, VMEM, VMEM),
        scratch_shapes=[pltpu.VMEM((tensor, depth, cols), bf16)],
        cost_estimate=pl.CostEstimate(
            flops=2 * depth * cols * tensor * (depth + cols),
            bytes_accessed=2 * depth * depth + 2 * depth * cols * tensor + 6 * depth * cols,
            transcendentals=0,
        ),
    )(owner, *left, *grad, root)


def stats_kernel(rows, cols, paired, owner, *refs):
    tensor = lax.axis_size("tensor")
    grad = refs[:tensor]
    if paired:
        stats, stats_out, square = refs[tensor:]
        left, right = stats.at[0, 0], stats.at[0, 1]
        left_out, right_out = stats_out.at[0, 0], stats_out.at[0, 1]
    else:
        left, right, left_out, right_out, square = refs[tensor:]
        left, right, left_out, right_out = left.at[0], right.at[0], left_out.at[0], right_out.at[0]
    part = lax.axis_index("tensor")

    @pl.when(holds(owner))
    def _():
        high = left.shape[0]
        total = jnp.zeros(left.shape, f32)
        mine = block(grad[0], rows, cols)
        for k in range(tensor):
            columns = block(grad[k], rows, cols)
            slots = high // rows
            band = block(grad[k], rows, cols, part * slots, slots)
            total = total + lax.dot_general(
                band, columns, (((1,), (1,)), ((), ())), preferred_element_type=f32
            )
            square[part ^ k] = lax.dot_general(
                mine, columns, (((0,), (0,)), ((), ())), preferred_element_type=f32
            )
        left_out[...] = beta_stat * left[...] + (1.0 - beta_stat) * total
        for k in range(tensor):
            span = slice(k * cols, (k + 1) * cols)
            right_out[:, span] = beta_stat * right[:, span] + (1.0 - beta_stat) * square[k]

    @pl.when(jnp.logical_not(holds(owner)))
    def _():
        left_out[...] = left[...]
        right_out[...] = right[...]


def stats_part(owner, grad, stats, rows, cols):
    tensor = len(grad)
    shapes = tuple(jax.ShapeDtypeStruct(s.shape, f32) for s in stats)
    depth = tensor * cols
    return pl.pallas_call(
        functools.partial(stats_kernel, rows, cols, len(stats) == 1),
        out_shape=shapes,
        in_specs=[SMEM] + [VMEM] * (tensor + len(stats)),
        out_specs=(VMEM,) * len(stats),
        scratch_shapes=[pltpu.VMEM((tensor, cols, cols), f32)],
        cost_estimate=pl.CostEstimate(
            flops=4 * depth * depth * cols,
            bytes_accessed=8 * sum(s.size for s in stats) + 2 * depth * depth,
            transcendentals=0,
        ),
    )(owner, *grad, *stats)


def weight_kernel(owner, weight, back, out):
    def unit(u, carry):
        out[u] = weight[u] - learn_rate * back[owner[u]].astype(f32)
        return carry

    lax.fori_loop(0, weight.shape[0], unit, 0, unroll=weight.shape[0] <= 4)


def weight_part(owner, weight, back):
    return pl.pallas_call(
        weight_kernel,
        out_shape=jax.ShapeDtypeStruct(weight.shape, f32),
        in_specs=[SMEM, VMEM, VMEM],
        out_specs=VMEM,
    )(owner, weight, back)


def flip(value, bits):
    size = lax.axis_size("tensor")
    return lax.ppermute(value, "tensor", [(i, i ^ bits) for i in range(size)])


def spread(value):
    blocks = [value]
    bit = lax.axis_size("tensor") // 2
    held = {0: value}
    while bit:
        for k in sorted(held):
            held[k | bit] = flip(held[k], bit)
        bit //= 2
    return [held[k] for k in range(len(held))]


def over_shard(value):
    return lax.all_to_all(value, "shard", split_axis=0, concat_axis=0, tiled=True)


def grafted(done, norm, adam, owners):
    bit = 1
    while bit < lax.axis_size("tensor"):
        norm = norm + flip(norm, bit)
        bit *= 2
    scale = jnp.sqrt(adam[0, 0] / (norm[0, 0] + graft_eps))
    return (scale * done).astype(bf16).reshape(owners, -1, done.shape[1])


def per_device(
    att_grads,
    glu_grads,
    att_weight,
    att_moment,
    att_second,
    glu_weight,
    glu_moment,
    glu_second,
    att_stats,
    att_left_root,
    att_right_root,
    glu_left_stat,
    glu_right_stat,
    glu_left_root,
    glu_right_root,
    att_owner,
    glu_owner,
):
    owners = lax.axis_size("shard")
    rows = att_weight.shape[1]
    att_packed, att_moment_out, att_second_out = adam_part(
        att_owner, att_grads, att_moment, att_second, owners
    )
    glu_packed, glu_moment_out, glu_second_out = adam_part(
        glu_owner, glu_grads, glu_moment, glu_second, owners
    )
    att_left = spread(att_left_root[0])
    glu_left = spread(glu_left_root[0])
    att_grad = spread(over_shard(att_packed))
    att_done, att_norm, att_adam = shampoo_part(att_owner, att_left, att_grad, att_right_root, rows)
    glu_grad = spread(over_shard(glu_packed))
    glu_done, glu_norm, glu_adam = shampoo_part(glu_owner, glu_left, glu_grad, glu_right_root, rows)
    att_back = over_shard(grafted(att_done, att_norm, att_adam, owners))
    glu_back = over_shard(grafted(glu_done, glu_norm, glu_adam, owners))
    (att_stats_out,) = stats_part(att_owner, att_grad, (att_stats,), rows, att_weight.shape[2])
    glu_left_out, glu_right_out = stats_part(
        glu_owner, glu_grad, (glu_left_stat, glu_right_stat), rows, glu_weight.shape[2]
    )
    att_weight_out = weight_part(att_owner, att_weight, att_back)
    glu_weight_out = weight_part(glu_owner, glu_weight, glu_back)
    return (
        att_weight_out,
        att_moment_out,
        att_second_out,
        glu_weight_out,
        glu_moment_out,
        glu_second_out,
        att_stats_out,
        glu_left_out,
        glu_right_out,
    )


def solution(mesh):
    placed = (
        P(None, None, "shard", "tensor"),
        P(None, None, "shard", "tensor"),
        P(None, "shard", "tensor"),
        P(None, "shard", "tensor"),
        P(None, "shard", "tensor"),
        P(None, "shard", "tensor"),
        P(None, "shard", "tensor"),
        P(None, "shard", "tensor"),
        P("shard", None, "tensor", None),
        P("shard", "tensor", None),
        P("shard", None, "tensor"),
        P("shard", "tensor", None),
        P("shard", "tensor", None),
        P("shard", "tensor", None),
        P("shard", None, "tensor"),
        P(),
        P(),
    )
    return jax.shard_map(
        per_device,
        mesh=mesh,
        in_specs=placed,
        out_specs=(
            P(None, "shard", "tensor"),
            P(None, "shard", "tensor"),
            P(None, "shard", "tensor"),
            P(None, "shard", "tensor"),
            P(None, "shard", "tensor"),
            P(None, "shard", "tensor"),
            P("shard", None, "tensor", None),
            P("shard", "tensor", None),
            P("shard", "tensor", None),
        ),
        check_vma=False,
    )
```

time: 200 us -> 111 us (0.56)
  blocking collectives: 66.8 us -> 0 us
  waiting for transfers between devices: 58.3 us -> 36.3 us
  Pallas kernels: 0 us -> 20.9 us
  starting transfers between devices: 19.5 us -> 36.8 us
  between operations: 18.2 us -> 3.36 us
  other arithmetic: 16.1 us -> 5.27 us
  matrix products: 6.18 us -> 0 us
  local copies, waits for them, and re-layouts: 13.2 us -> 7.54 us
    psum x2 -> x0, blocking collectives: 48.3 us -> none  [the longest x1 41.7 us: per_device(): att_total, glu_total = lax.psum((att_adam, glu_adam), ('shard', 'tensor'))]
    all_to_all x4, waiting for transfers between devices: 58.3 us -> 22.1 us  [over_shard(): lax.all_to_all(value, 'shard', split_axis=0, concat_axis=0, tiled=True)]
    pallas_call x0 -> x8, Pallas kernels: none -> 20.9 us  [the longest x2 6.1 us: stats_part(): pl.pallas_call(functools.partial(stats_kernel, rows, cols, len(stats) ==...]
    all_gather x2 -> x0, blocking collectives: 18.5 us -> none  [the longest x1 10.1 us: per_device(): lax.all_gather(att_sum.astype(jnp.bfloat16), 'tensor', axis=2, tiled=True)]
    ppermute x0 -> x16, waiting for transfers between devices: none -> 14.2 us  [flip(): return lax.ppermute(value, 'tensor', [(i, i ^ bits) for i in range(size)])]
    ppermute x0 -> x16, starting transfers between devices: none -> 9.82 us  [flip(): return lax.ppermute(value, 'tensor', [(i, i ^ bits) for i in range(size)])]
    all_to_all x4, starting transfers between devices: 19.4 us -> 26.9 us  [over_shard(): lax.all_to_all(value, 'shard', split_axis=0, concat_axis=0, tiled=True)]
    dot_general x4 -> x0, matrix products: 6.18 us -> none  [the longest x1 2.45 us: refresh(): lax.dot_general(row_block, grad, (((1,), (1,)), ((), ())), precision=top_...]
  transfers between devices with their start and end apart: 6 -> 20, of which waited for: 4 -> 9; matrix products, arithmetic and copies ran while one was open for 11% -> 9% of each run, Pallas kernels for 0% -> 15%
where the time goes in v1:
time: 111 us; the launch traced here: 110 us
  starting transfers between devices  36.8 us (33%)
  waiting for transfers between devices  36.3 us (33%)
  Pallas kernels  20.9 us (19%)
  local copies, waits for them, and re-layouts  7.54 us (7%)
  other arithmetic  5.27 us (5%)
  between operations  3.36 us (3%)
    all_to_all x4, starting transfers between devices, over_shard(): lax.all_to_all(value, 'shard', split_axis=0, concat_axis=0, tiled=True)  26.9 us
    all_to_all x4, waiting for transfers between devices, over_shard(): lax.all_to_all(value, 'shard', split_axis=0, concat_axis=0, tiled=True)  22.1 us
    ppermute x16, waiting for transfers between devices, flip(): return lax.ppermute(value, 'tensor', [(i, i ^ bits) for i in range(size)])  14.2 us
    ppermute x16, starting transfers between devices, flip(): return lax.ppermute(value, 'tensor', [(i, i ^ bits) for i in range(size)])  9.82 us
    pallas_call x2, Pallas kernels, stats_part(): pl.pallas_call(functools.partial(stats_kernel, rows, cols, len(stats) ==...  6.1 us
    pallas_call x2, Pallas kernels, shampoo_part(): pl.pallas_call(functools.partial(shampoo_kernel, rows, cols), out_shape=(...  5.68 us
    pallas_call x2, Pallas kernels, adam_part(): pl.pallas_call(adam_kernel, out_shape=(packed, jax.ShapeDtypeStruct(momen...  5.33 us
    unnamed x31, local copies, waits for them, and re-layouts  4.08 us
  transfers between devices with their start and end apart: 20, of which 9 were waited for; matrix products, arithmetic and copies ran while one was open for 9% of the time, Pallas kernels for 15%

profile of v1, /device:TPU:0, one launch (start us, length us, event | category | flops | bytes accessed | tf_op | source)
XLA Modules:
  0.0 110.1 jit_solution(3647008394732639653)
XLA Ops:
  0.6 2.6 %shard_map.232 = (bf16[8,96,256]{2,1,0:T(8,128)(2,1)}, f32[4,96,192]{2,1,0:T(8,128)}, f32[4,96,192]{2,1,0:T(8,128)}) custom-call(s32[4]{0:T(128)} %owner.14, f32[2,4,96,192]{3,2,1,0:T(8,128)} %grads.2, f32[4,96,192]{2,1,0:T(8,128)} %moment.2, f32[4,96,192]{2,1,0:T(8,128)} %second.2), custom_call_target="tpu_custom_call" | custom-call | flops 1474560 | bytes 2359296 | tf_op jit(solution)/shard_map/pallas_call | solution.py:74
  3.3 7.3 %all-to-all-start = ((bf16[8,96,256]{2,1,0:T(8,128)(2,1)}), bf16[8,96,256]{2,1,0:T(8,128)(2,1)S(1)}, u32[]{:S(2)}, u32[]{:S(2)}) async-start(bf16[8,96,256]{2,1,0:T(8,128)(2,1)} %get-tuple-element.23), calls=%async_computation | async-start | bytes 786432 | tf_op jit(solution)/shard_map/all_to_all | solution.py:248
  10.6 2.7 %shard_map.235 = (bf16[8,104,256]{2,1,0:T(8,128)(2,1)}, f32[4,96,256]{2,1,0:T(8,128)}, f32[4,96,256]{2,1,0:T(8,128)}) custom-call(s32[4]{0:T(128)} %owner.15, f32[2,4,96,256]{3,2,1,0:T(8,128)} %grads.3, f32[4,96,256]{2,1,0:T(8,128)} %moment.3, f32[4,96,256]{2,1,0:T(8,128)} %second.3), custom_call_target="tpu_custom_call" | custom-call | flops 1966080 | bytes 3145728 | tf_op jit(solution)/shard_map/pallas_call | solution.py:74
  13.2 9.0 %all-to-all-done.refs_4_.refs_0_ = bf16[8,96,256]{2,1,0:T(8,128)(2,1)S(1)} async-done(((bf16[8,96,256]{2,1,0:T(8,128)(2,1)}), bf16[8,96,256]{2,1,0:T(8,128)(2,1)S(1)}, u32[]{:S(2)}, u32[]{:S(2)}) %all-to-all-start) | async-done | bytes 393248 | tf_op jit(solution)/shard_map/all_to_all | solution.py:248
  22.2 3.6 %all-to-all-start.2 = ((bf16[8,104,256]{2,1,0:T(8,128)(2,1)}), bf16[8,104,256]{2,1,0:T(8,128)(2,1)S(1)}, u32[]{:S(2)}, u32[]{:S(2)}) async-start(bf16[8,104,256]{2,1,0:T(8,128)(2,1)} %get-tuple-element.29), calls=%async_computation.2 | async-start | bytes 851968 | tf_op jit(solution)/shard_map/all_to_all | solution.py:248
  25.9 1.5 %collective-permute-start.4 = (bf16[8,96,256]{2,1,0:T(8,128)(2,1)S(1)}, bf16[8,96,256]{2,1,0:T(8,128)(2,1)S(1)}, u32[]{:S(2)}, u32[]{:S(2)}) collective-permute-start(bf16[8,96,256]{2,1,0:T(8,128)(2,1)S(1)} %all-to-all-done.refs_4_.refs_0_), channel_id=1, source_target_pairs={{0,2},{1,3},{2,0},{3,1},{4,6},{5,7},{6,4},{7,5},{8,10},{9,11},{10,... | collective-permute-start | bytes 1179656 | tf_op jit(solution)/shard_map/ppermute | solution.py:233
  27.9 10.3 %all-to-all-done.2.refs_4_.refs_0_ = bf16[8,104,256]{2,1,0:T(8,128)(2,1)S(1)} async-done(((bf16[8,104,256]{2,1,0:T(8,128)(2,1)}), bf16[8,104,256]{2,1,0:T(8,128)(2,1)S(1)}, u32[]{:S(2)}, u32[]{:S(2)}) %all-to-all-start.2) | async-done | bytes 426016 | tf_op jit(solution)/shard_map/all_to_all | solution.py:248
  38.1 1.5 %collective-permute-start.12 = (bf16[8,104,256]{2,1,0:T(8,128)(2,1)S(1)}, bf16[8,104,256]{2,1,0:T(8,128)(2,1)S(1)}, u32[]{:S(2)}, u32[]{:S(2)}) collective-permute-start(bf16[8,104,256]{2,1,0:T(8,128)(2,1)S(1)} %all-to-all-done.2.refs_4_.refs_0_), channel_id=1, source_target_pairs={{0,2},{1,3},{2,0},{3,1},{4,6},{5,7},{6,4},{7,5},{8,10},{9,11},{10,... | collective-permute-start | bytes 1277960 | tf_op jit(solution)/shard_map/ppermute | solution.py:233
  40.2 4.0 %collective-permute-done.1.refs_2_ = bf16[192,768]{1,0:T(8,128)(2,1)S(1)} collective-permute-done((bf16[192,768]{1,0:T(8,128)(2,1)S(1)}, bf16[192,768]{1,0:T(8,128)(2,1)S(1)}, u32[]{:S(2)}, u32[]{:S(2)}) %collective-permute-start.1) | collective-permute-done | bytes 294944 | tf_op jit(solution)/shard_map/ppermute | solution.py:233
  44.2 1.6 %collective-permute-start.9 = (bf16[192,768]{1,0:T(8,128)(2,1)}, bf16[192,768]{1,0:T(8,128)(2,1)S(1)}, u32[]{:S(2)}, u32[]{:S(2)}) collective-permute-start(bf16[192,768]{1,0:T(8,128)(2,1)} %bitcast.3.refs_0_), channel_id=1, source_target_pairs={{0,2},{1,3},{2,0},{3,1},{4,6},{5,7},{6,4},{7,5},{8,10},{9,11},{10,... | collective-permute-start | bytes 884744 | tf_op jit(solution)/shard_map/ppermute | solution.py:233
  46.9 6.4 %collective-permute-done.12.refs_6_.refs_2_ = bf16[8,104,256]{2,1,0:T(8,128)(2,1)S(1)} collective-permute-done((bf16[8,104,256]{2,1,0:T(8,128)(2,1)S(1)}, bf16[8,104,256]{2,1,0:T(8,128)(2,1)S(1)}, u32[]{:S(2)}, u32[]{:S(2)}) %collective-permute-start.12) | collective-permute-done | bytes 426016 | tf_op jit(solution)/shard_map/ppermute | solution.py:233
  54.9 2.8 %shard_map.233 = (f32[768,192]{1,0:T(8,128)}, f32[8,128]{1,0:T(8,128)}, f32[8,128]{1,0:T(8,128)}) custom-call(s32[4]{0:T(128)} %owner.14, bf16[192,768]{1,0:T(8,128)(2,1)} %bitcast.6, bf16[192,768]{1,0:T(8,128)(2,1)} %collective-permute-done.refs_1_, bf16[192,768]{1,0:T(8,128)(2,1)} %copy-done.12, bf16[192,768]{1,0:T(8,128)(2,1)} %collective-permute-done.2.refs_3_, ...), custom_call_target="tpu_custom_call" | custom-call | flops 1132462080 | bytes 3244032 | tf_op jit(solution)/shard_map/pallas_call | solution.py:144
  59.9 1.5 %collective-permute-start.7 = (f32[8,128]{1,0:T(8,128)S(1)}, f32[8,128]{1,0:T(8,128)S(1)}, u32[]{:S(2)}, u32[]{:S(2)}) collective-permute-start(f32[8,128]{1,0:T(8,128)S(1)} %add.20), channel_id=1, source_target_pairs={{0,2},{1,3},{2,0},{3,1},{4,6},{5,7},{6,4},{7,5},{8,10},{9,11},{10,... | collective-permute-start | bytes 12296 | tf_op jit(solution)/shard_map/ppermute | solution.py:233
  65.4 1.9 %multiply_convert_fusion.1 = bf16[768,192]{1,0:T(8,128)(2,1)} fusion(f32[768,192]{1,0:T(8,128)} %get-tuple-element.26, f32[]{:T(128)} %bitcast.1), kind=kLoop, calls=%fused_computation.1 | loop fusion | flops 294912 | bytes 884740 | tf_op jit(solution)/shard_map/convert_element_type | solution.py:257
  67.3 8.1 %all-to-all-start.1 = ((bf16[8,96,192]{2,1,0:T(8,128)(2,1)}), bf16[8,96,192]{2,1,0:T(8,128)(2,1)S(1)}, u32[]{:S(2)}, u32[]{:S(2)}) async-start(bf16[8,96,192]{2,1,0:T(8,128)(2,1)} %bitcast.2), calls=%async_computation.1 | async-start | bytes 786432 | tf_op jit(solution)/shard_map/all_to_all | solution.py:248
  76.3 2.9 %shard_map.236 = (f32[768,256]{1,0:T(8,128)}, f32[8,128]{1,0:T(8,128)}, f32[8,128]{1,0:T(8,128)}) custom-call(s32[4]{0:T(128)} %owner.15, bf16[192,768]{1,0:T(8,128)(2,1)} %bitcast.3.refs_0_, bf16[192,768]{1,0:T(8,128)(2,1)} %copy-done.13, bf16[192,768]{1,0:T(8,128)(2,1)} %copy-done.11, bf16[192,768]{1,0:T(8,128)(2,1)} %copy-done.14, ...), custom_call_target="tpu_custom_call" | custom-call | flops 1610612736 | bytes 3932160 | tf_op jit(solution)/shard_map/pallas_call | solution.py:144
  81.3 1.5 %collective-permute-start.15 = (f32[8,128]{1,0:T(8,128)S(1)}, f32[8,128]{1,0:T(8,128)S(1)}, u32[]{:S(2)}, u32[]{:S(2)}) collective-permute-start(f32[8,128]{1,0:T(8,128)S(1)} %add.23), channel_id=1, source_target_pairs={{0,2},{1,3},{2,0},{3,1},{4,6},{5,7},{6,4},{7,5},{8,10},{9,11},{10,... | collective-permute-start | bytes 12296 | tf_op jit(solution)/shard_map/ppermute | solution.py:233
  86.6 2.0 %multiply_convert_fusion = bf16[768,256]{1,0:T(8,128)(2,1)} fusion(f32[768,256]{1,0:T(8,128)} %get-tuple-element.32, f32[]{:T(128)} %bitcast.4), kind=kLoop, calls=%fused_computation | loop fusion | flops 393216 | bytes 1179652 | tf_op jit(solution)/shard_map/convert_element_type | solution.py:257
  88.6 8.0 %all-to-all-start.3 = ((bf16[8,96,256]{2,1,0:T(8,128)(2,1)}), bf16[8,96,256]{2,1,0:T(8,128)(2,1)S(1)}, u32[]{:S(2)}, u32[]{:S(2)}) async-start(bf16[8,96,256]{2,1,0:T(8,128)(2,1)} %bitcast.5), calls=%async_computation.3 | async-start | bytes 786432 | tf_op jit(solution)/shard_map/all_to_all | solution.py:248
  96.6 2.9 %shard_map.238 = f32[1,2,192,768]{3,2,1,0:T(8,128)} custom-call(s32[4]{0:T(128)} %owner.14, bf16[8,96,256]{2,1,0:T(8,128)(2,1)} %copy-done, bf16[8,96,256]{2,1,0:T(8,128)(2,1)} %copy-done.5, bf16[8,96,256]{2,1,0:T(8,128)(2,1)} %copy-done.4, bf16[8,96,256]{2,1,0:T(8,128)(2,1)} %copy-done.6, f32[1,2,192,768]{3,2,1,0:T(8,128)} %refs_4_.2), custom_call_target="tpu_custom_call" | custom-call | flops 452984832 | bytes 3538944 | tf_op jit(solution)/shard_map/pallas_call | solution.py:200
  99.5 3.2 %shard_map.239 = (f32[1,192,768]{2,1,0:T(8,128)}, f32[1,256,1024]{2,1,0:T(8,128)}) custom-call(s32[4]{0:T(128)} %owner.15, bf16[8,104,256]{2,1,0:T(8,128)(2,1)} %copy-done.3, bf16[8,104,256]{2,1,0:T(8,128)(2,1)} %copy-done.9, bf16[8,104,256]{2,1,0:T(8,128)(2,1)} %copy-done.8, bf16[8,104,256]{2,1,0:T(8,128)(2,1)} %collective-permute-done.13.refs_7_.refs_3_, ...), custom_call_target="tpu_custom_call" | custom-call | flops 1073741824 | bytes 5373952 | tf_op jit(solution)/shard_map/pallas_call | solution.py:200
  102.7 1.9 %shard_map.234 = f32[4,96,192]{2,1,0:T(8,128)} custom-call(s32[4]{0:T(128)} %owner.14, f32[4,96,192]{2,1,0:T(8,128)} %weight.2, bf16[8,96,192]{2,1,0:T(8,128)(2,1)} %copy-done.1), custom_call_target="tpu_custom_call" | custom-call | tf_op jit(solution)/shard_map/pallas_call | solution.py:223
  104.6 2.8 %all-to-all-done.3.back = bf16[8,96,256]{2,1,0:T(8,128)(2,1)S(1)} async-done(((bf16[8,96,256]{2,1,0:T(8,128)(2,1)}), bf16[8,96,256]{2,1,0:T(8,128)(2,1)S(1)}, u32[]{:S(2)}, u32[]{:S(2)}) %all-to-all-start.3) | async-done | bytes 393248 | tf_op jit(solution)/shard_map/all_to_all | solution.py:248
  108.2 1.9 %shard_map.237 = f32[4,96,256]{2,1,0:T(8,128)} custom-call(s32[4]{0:T(128)} %owner.15, f32[4,96,256]{2,1,0:T(8,128)} %weight.3, bf16[8,96,256]{2,1,0:T(8,128)(2,1)} %copy-done.2), custom_call_target="tpu_custom_call" | custom-call | tf_op jit(solution)/shard_map/pallas_call | solution.py:223
  (65 shorter events, 14.8 us)
Async XLA Ops:
  3.3 18.9 %all-to-all-start = ((bf16[8,96,256]{2,1,0:T(8,128)(2,1)}), bf16[8,96,256]{2,1,0:T(8,128)(2,1)S(1)}, u32[]{:S(2)}, u32[]{:S(2)}) async-start(bf16[8,96,256]{2,1,0:T(8,128)(2,1)} %get-tuple-element.23), calls=%async_computation | async-start | bytes 786432 | tf_op jit(solution)/shard_map/all_to_all | solution.py:248
  10.5 35.3 %copy-start.7 = (bf16[1,768,192]{1,2,0:T(8,128)(2,1)S(1)}, bf16[1,768,192]{1,2,0:T(8,128)(2,1)}, u32[]{:S(2)}) copy-start(bf16[1,768,192]{1,2,0:T(8,128)(2,1)} %param.27) | copy-start | bytes 884740
  22.2 31.2 %copy-start = (bf16[8,96,256]{2,1,0:T(8,128)(2,1)}, bf16[8,96,256]{2,1,0:T(8,128)(2,1)S(1)}, u32[]{:S(2)}) copy-start(bf16[8,96,256]{2,1,0:T(8,128)(2,1)S(1)} %all-to-all-done.refs_4_.refs_0_) | copy-start | bytes 1179652
  22.2 15.9 %all-to-all-start.2 = ((bf16[8,104,256]{2,1,0:T(8,128)(2,1)}), bf16[8,104,256]{2,1,0:T(8,128)(2,1)S(1)}, u32[]{:S(2)}, u32[]{:S(2)}) async-start(bf16[8,104,256]{2,1,0:T(8,128)(2,1)} %get-tuple-element.29), calls=%async_computation.2 | async-start | bytes 851968 | tf_op jit(solution)/shard_map/all_to_all | solution.py:248
  25.9 13.8 %collective-permute-start.4 = (bf16[8,96,256]{2,1,0:T(8,128)(2,1)S(1)}, bf16[8,96,256]{2,1,0:T(8,128)(2,1)S(1)}, u32[]{:S(2)}, u32[]{:S(2)}) collective-permute-start(bf16[8,96,256]{2,1,0:T(8,128)(2,1)S(1)} %all-to-all-done.refs_4_.refs_0_), channel_id=1, source_target_pairs={{0,2},{1,3},{2,0},{3,1},{4,6},{5,7},{6,4},{7,5},{8,10},{9,11},{10,... | collective-permute-start | bytes 1179656 | tf_op jit(solution)/shard_map/ppermute | solution.py:233
  27.4 16.8 %collective-permute-start.1 = (bf16[192,768]{1,0:T(8,128)(2,1)S(1)}, bf16[192,768]{1,0:T(8,128)(2,1)S(1)}, u32[]{:S(2)}, u32[]{:S(2)}) collective-permute-start(bf16[192,768]{1,0:T(8,128)(2,1)S(1)} %bitcast.7), channel_id=1, source_target_pairs={{0,2},{1,3},{2,0},{3,1},{4,6},{5,7},{6,4},{7,5},{8,10},{9,11},{10,... | collective-permute-start | bytes 884744 | tf_op jit(solution)/shard_map/ppermute | solution.py:233
  27.9 16.4 %collective-permute-start = (bf16[192,768]{1,0:T(8,128)(2,1)S(1)}, bf16[192,768]{1,0:T(8,128)(2,1)}, u32[]{:S(2)}, u32[]{:S(2)}) collective-permute-start(bf16[192,768]{1,0:T(8,128)(2,1)S(1)} %bitcast.8), channel_id=1, source_target_pairs={{0,1},{1,0},{2,3},{3,2},{4,5},{5,4},{6,7},{7,6},{8,9},{9,8},{10,11... | collective-permute-start | bytes 884744 | tf_op jit(solution)/shard_map/ppermute | solution.py:233
  38.1 19.5 %copy-start.3 = (bf16[8,104,256]{2,1,0:T(8,128)(2,1)}, bf16[8,104,256]{2,1,0:T(8,128)(2,1)S(1)}, u32[]{:S(2)}) copy-start(bf16[8,104,256]{2,1,0:T(8,128)(2,1)S(1)} %all-to-all-done.2.refs_4_.refs_0_) | copy-start | bytes 1277956
  38.1 15.2 %collective-permute-start.12 = (bf16[8,104,256]{2,1,0:T(8,128)(2,1)S(1)}, bf16[8,104,256]{2,1,0:T(8,128)(2,1)S(1)}, u32[]{:S(2)}, u32[]{:S(2)}) collective-permute-start(bf16[8,104,256]{2,1,0:T(8,128)(2,1)S(1)} %all-to-all-done.2.refs_4_.refs_0_), channel_id=1, source_target_pairs={{0,2},{1,3},{2,0},{3,1},{4,6},{5,7},{6,4},{7,5},{8,10},{9,11},{10,... | collective-permute-start | bytes 1277960 | tf_op jit(solution)/shard_map/ppermute | solution.py:233
  39.7 13.7 %collective-permute-start.3 = (bf16[8,96,256]{2,1,0:T(8,128)(2,1)S(1)}, bf16[8,96,256]{2,1,0:T(8,128)(2,1)S(1)}, u32[]{:S(2)}, u32[]{:S(2)}) collective-permute-start(bf16[8,96,256]{2,1,0:T(8,128)(2,1)S(1)} %all-to-all-done.refs_4_.refs_0_), channel_id=1, source_target_pairs={{0,1},{1,0},{2,3},{3,2},{4,5},{5,4},{6,7},{7,6},{8,9},{9,8},{10,11... | collective-permute-start | bytes 1179656 | tf_op jit(solution)/shard_map/ppermute | solution.py:233
  39.7 13.7 %collective-permute-start.5 = (bf16[8,96,256]{2,1,0:T(8,128)(2,1)S(1)}, bf16[8,96,256]{2,1,0:T(8,128)(2,1)S(1)}, u32[]{:S(2)}, u32[]{:S(2)}) collective-permute-start(bf16[8,96,256]{2,1,0:T(8,128)(2,1)S(1)} %collective-permute-done.4.refs_6_.refs_2_), channel_id=1, source_target_pairs={{0,1},{1,0},{2,3},{3,2},{4,5},{5,4},{6,7},{7,6},{8,9},{9,8},{10,11... | collective-permute-start | bytes 1179656 | tf_op jit(solution)/shard_map/ppermute | solution.py:233
  44.2 2.5 %collective-permute-start.2 = (bf16[192,768]{1,0:T(8,128)(2,1)S(1)}, bf16[192,768]{1,0:T(8,128)(2,1)}, u32[]{:S(2)}, u32[]{:S(2)}) collective-permute-start(bf16[192,768]{1,0:T(8,128)(2,1)S(1)} %collective-permute-done.1.refs_2_), channel_id=1, source_target_pairs={{0,1},{1,0},{2,3},{3,2},{4,5},{5,4},{6,7},{7,6},{8,9},{9,8},{10,11... | collective-permute-start | bytes 884744 | tf_op jit(solution)/shard_map/ppermute | solution.py:233
  44.2 17.2 %collective-permute-start.9 = (bf16[192,768]{1,0:T(8,128)(2,1)}, bf16[192,768]{1,0:T(8,128)(2,1)S(1)}, u32[]{:S(2)}, u32[]{:S(2)}) collective-permute-start(bf16[192,768]{1,0:T(8,128)(2,1)} %bitcast.3.refs_0_), channel_id=1, source_target_pairs={{0,2},{1,3},{2,0},{3,1},{4,6},{5,7},{6,4},{7,5},{8,10},{9,11},{10,... | collective-permute-start | bytes 884744 | tf_op jit(solution)/shard_map/ppermute | solution.py:233
  46.8 28.6 %collective-permute-start.11 = (bf16[8,104,256]{2,1,0:T(8,128)(2,1)S(1)}, bf16[8,104,256]{2,1,0:T(8,128)(2,1)S(1)}, u32[]{:S(2)}, u32[]{:S(2)}) collective-permute-start(bf16[8,104,256]{2,1,0:T(8,128)(2,1)S(1)} %all-to-all-done.2.refs_4_.refs_0_), channel_id=1, source_target_pairs={{0,1},{1,0},{2,3},{3,2},{4,5},{5,4},{6,7},{7,6},{8,9},{9,8},{10,11... | collective-permute-start | bytes 1277960 | tf_op jit(solution)/shard_map/ppermute | solution.py:233
  53.4 22.1 %copy-start.8 = (bf16[8,104,256]{2,1,0:T(8,128)(2,1)}, bf16[8,104,256]{2,1,0:T(8,128)(2,1)S(1)}, u32[]{:S(2)}) copy-start(bf16[8,104,256]{2,1,0:T(8,128)(2,1)S(1)} %collective-permute-done.12.refs_6_.refs_2_) | copy-start | bytes 1277956
  53.4 22.0 %collective-permute-start.13 = (bf16[8,104,256]{2,1,0:T(8,128)(2,1)S(1)}, bf16[8,104,256]{2,1,0:T(8,128)(2,1)}, u32[]{:S(2)}, u32[]{:S(2)}) collective-permute-start(bf16[8,104,256]{2,1,0:T(8,128)(2,1)S(1)} %collective-permute-done.12.refs_6_.refs_2_), channel_id=1, source_target_pairs={{0,1},{1,0},{2,3},{3,2},{4,5},{5,4},{6,7},{7,6},{8,9},{9,8},{10,11... | collective-permute-start | bytes 1277960 | tf_op jit(solution)/shard_map/ppermute | solution.py:233
  57.7 1.5 %collective-permute-start.6 = (f32[8,128]{1,0:T(8,128)}, f32[8,128]{1,0:T(8,128)S(1)}, u32[]{:S(2)}, u32[]{:S(2)}) collective-permute-start(f32[8,128]{1,0:T(8,128)} %get-tuple-element.25), channel_id=1, source_target_pairs={{0,1},{1,0},{2,3},{3,2},{4,5},{5,4},{6,7},{7,6},{8,9},{9,8},{10,11... | collective-permute-start | bytes 12296 | tf_op jit(solution)/shard_map/ppermute | solution.py:233
  59.9 3.6 %collective-permute-start.7 = (f32[8,128]{1,0:T(8,128)S(1)}, f32[8,128]{1,0:T(8,128)S(1)}, u32[]{:S(2)}, u32[]{:S(2)}) collective-permute-start(f32[8,128]{1,0:T(8,128)S(1)} %add.20), channel_id=1, source_target_pairs={{0,2},{1,3},{2,0},{3,1},{4,6},{5,7},{6,4},{7,5},{8,10},{9,11},{10,... | collective-permute-start | bytes 12296 | tf_op jit(solution)/shard_map/ppermute | solution.py:233
  61.4 14.0 %collective-permute-start.8 = (bf16[192,768]{1,0:T(8,128)(2,1)}, bf16[192,768]{1,0:T(8,128)(2,1)S(1)}, u32[]{:S(2)}, u32[]{:S(2)}) collective-permute-start(bf16[192,768]{1,0:T(8,128)(2,1)} %bitcast.3.refs_0_), channel_id=1, source_target_pairs={{0,1},{1,0},{2,3},{3,2},{4,5},{5,4},{6,7},{7,6},{8,9},{9,8},{10,11... | collective-permute-start | bytes 884744 | tf_op jit(solution)/shard_map/ppermute | solution.py:233
  61.5 13.9 %collective-permute-start.10 = (bf16[192,768]{1,0:T(8,128)(2,1)S(1)}, bf16[192,768]{1,0:T(8,128)(2,1)S(1)}, u32[]{:S(2)}, u32[]{:S(2)}) collective-permute-start(bf16[192,768]{1,0:T(8,128)(2,1)S(1)} %collective-permute-done.9.refs_2_), channel_id=1, source_target_pairs={{0,1},{1,0},{2,3},{3,2},{4,5},{5,4},{6,7},{7,6},{8,9},{9,8},{10,11... | collective-permute-start | bytes 884744 | tf_op jit(solution)/shard_map/ppermute | solution.py:233
  67.3 21.3 %all-to-all-start.1 = ((bf16[8,96,192]{2,1,0:T(8,128)(2,1)}), bf16[8,96,192]{2,1,0:T(8,128)(2,1)S(1)}, u32[]{:S(2)}, u32[]{:S(2)}) async-start(bf16[8,96,192]{2,1,0:T(8,128)(2,1)} %bitcast.2), calls=%async_computation.1 | async-start | bytes 786432 | tf_op jit(solution)/shard_map/all_to_all | solution.py:248
  79.2 1.4 %collective-permute-start.14 = (f32[8,128]{1,0:T(8,128)}, f32[8,128]{1,0:T(8,128)S(1)}, u32[]{:S(2)}, u32[]{:S(2)}) collective-permute-start(f32[8,128]{1,0:T(8,128)} %get-tuple-element.31), channel_id=1, source_target_pairs={{0,1},{1,0},{2,3},{3,2},{4,5},{5,4},{6,7},{7,6},{8,9},{9,8},{10,11... | collective-permute-start | bytes 12296 | tf_op jit(solution)/shard_map/ppermute | solution.py:233
  81.3 3.6 %collective-permute-start.15 = (f32[8,128]{1,0:T(8,128)S(1)}, f32[8,128]{1,0:T(8,128)S(1)}, u32[]{:S(2)}, u32[]{:S(2)}) collective-permute-start(f32[8,128]{1,0:T(8,128)S(1)} %add.23), channel_id=1, source_target_pairs={{0,2},{1,3},{2,0},{3,1},{4,6},{5,7},{6,4},{7,5},{8,10},{9,11},{10,... | collective-permute-start | bytes 12296 | tf_op jit(solution)/shard_map/ppermute | solution.py:233
  88.6 18.9 %all-to-all-start.3 = ((bf16[8,96,256]{2,1,0:T(8,128)(2,1)}), bf16[8,96,256]{2,1,0:T(8,128)(2,1)S(1)}, u32[]{:S(2)}, u32[]{:S(2)}) async-start(bf16[8,96,256]{2,1,0:T(8,128)(2,1)} %bitcast.5), calls=%async_computation.3 | async-start | bytes 786432 | tf_op jit(solution)/shard_map/all_to_all | solution.py:248
  (11 other events, 62.7 us)

commit v2 on v1

--- a/solution.py
+++ b/solution.py
@@ -41,57 +41,132 @@
     return jnp.where(column == 0, value, 0.0).astype(bf16)
 
 
-def adam_kernel(owner, grads, moment, second, packed, moment_out, second_out):
-    rows, cols = moment.shape[1:]
-    packed_rows, packed_cols = packed.shape[1:]
-    packed[...] = jnp.zeros_like(packed)
-
-    def unit(u, carry):
+def adam_kernel(direct, owner, grads, moment, second, *refs):
+    packed, (moment_out, second_out, total) = refs[:-3], refs[-3:]
+    units, rows, cols = moment.shape
+    packed_rows, packed_cols = packed[0].shape[-2:]
+
+    def block_sum(u):
         summed = grads[0, u]
         for micro in range(1, grads.shape[0]):
             summed = summed + grads[micro, u]
+        return summed
+
+    def unit(u, carry):
+        summed = block_sum(u)
         moment_new = beta_one * moment[u] + (1.0 - beta_one) * summed
         second_new = beta_two * second[u] + (1.0 - beta_two) * summed * summed
         direction = moment_new / (jnp.sqrt(second_new) + adam_eps)
         moment_out[u] = moment_new
         second_out[u] = second_new
-        total = jnp.sum(direction * direction)
-        slot = owner[u]
+        total[u] = jnp.sum(direction * direction)
+        return carry
+
+    lax.fori_loop(0, units, unit, 0, unroll=units <= 4)
+
+    def fill(target, u):
         if packed_cols > cols:
-            packed[slot, :, :cols] = summed.astype(bf16)
-            packed[slot, :, cols:] = pieces(total, (packed_rows, packed_cols - cols))
+            target[:, :cols] = block_sum(u).astype(bf16)
+            target[:, cols:] = pieces(total[u], (packed_rows, packed_cols - cols))
         else:
-            packed[slot, :rows, :] = summed.astype(bf16)
-            packed[slot, rows:, :] = pieces(total, (packed_rows - rows, packed_cols))
-        return carry
-
-    lax.fori_loop(0, moment.shape[0], unit, 0, unroll=moment.shape[0] <= 4)
+            target[:rows, :] = block_sum(u).astype(bf16)
+            target[rows:, :] = pieces(total[u], (packed_rows - rows, packed_cols))
+
+    if direct:
+        me = lax.axis_index("shard")
+        for k in range(len(packed)):
+            found, index = held_by(owner, me ^ k)
+
+            @pl.when(found)
+            def _():
+                fill(packed[k], index)
+
+            @pl.when(jnp.logical_not(found))
+            def _():
+                packed[k][...] = jnp.zeros_like(packed[k])
+    else:
+        packed[0][...] = jnp.zeros_like(packed[0])
+
+        def place(u, carry):
+            fill(packed[0].at[owner[u]], u)
+            return carry
+
+        lax.fori_loop(0, units, place, 0)
 
 
 def adam_part(owner, grads, moment, second, owners):
     rows, cols = moment.shape[1:]
-    packed = jax.ShapeDtypeStruct((owners, *packed_shape(rows, cols)), bf16)
-    return pl.pallas_call(
-        adam_kernel,
+    shape = packed_shape(rows, cols)
+    if by_permutes(owners, rows):
+        packed = [jax.ShapeDtypeStruct(shape, bf16)] * owners
+    else:
+        packed = [jax.ShapeDtypeStruct((owners, *shape), bf16)]
+    *packed, moment_out, second_out = pl.pallas_call(
+        functools.partial(adam_kernel, len(packed) > 1),
         out_shape=(
-            packed,
+            *packed,
             jax.ShapeDtypeStruct(moment.shape, f32),
             jax.ShapeDtypeStruct(second.shape, f32),
         ),
         in_specs=[SMEM, VMEM, VMEM, VMEM],
-        out_specs=(VMEM, VMEM, VMEM),
+        out_specs=(VMEM,) * (len(packed) + 2),
+        scratch_shapes=[pltpu.SMEM((moment.shape[0],), f32)],
         cost_estimate=pl.CostEstimate(
             flops=20 * moment.size, bytes_accessed=32 * moment.size, transcendentals=moment.size
         ),
     )(owner, grads, moment, second)
+    return packed, moment_out, second_out
+
+
+def by_permutes(owners, rows):
+    return owners <= 8 and owners & (owners - 1) == 0 and rows % 8 == 0
+
+
+def cross(value, bits):
+    size = lax.axis_size("shard")
+    return lax.ppermute(value, "shard", [(i, i ^ bits) for i in range(size)])
+
+
+def order_kernel(*refs):
+    out = refs[-1]
+    me = lax.axis_index("shard")
+    for k, ref in enumerate(refs[:-1]):
+        out[me ^ k] = ref[...]
+
+
+def after(value, *others):
+    return lax.optimization_barrier((value, *others))[0]
+
+
+def gathered(packed, *others):
+    packed = [after(packed[0], *others)] + list(packed[1:])
+    if len(packed) == 1:
+        return lax.all_to_all(packed[0], "shard", split_axis=0, concat_axis=0, tiled=True)
+    arrived = [packed[0]] + [cross(packed[k], k) for k in range(1, len(packed))]
+    shape = (len(packed), *packed[0].shape)
+    return pl.pallas_call(
+        order_kernel,
+        out_shape=jax.ShapeDtypeStruct(shape, bf16),
+        in_specs=[VMEM] * len(packed),
+        out_specs=VMEM,
+        cost_estimate=pl.CostEstimate(
+            flops=0, bytes_accessed=4 * packed[0].size * len(packed), transcendentals=0
+        ),
+    )(*arrived)
+
+
+def held_by(owner, place):
+    found = owner[0] == place
+    index = jnp.int32(0)
+    for unit in range(1, owner.shape[0]):
+        here = owner[unit] == place
+        found = jnp.logical_or(found, here)
+        index = jnp.where(here, unit, index)
+    return found, index
 
 
 def holds(owner):
-    me = lax.axis_index("shard")
-    found = owner[0] == me
-    for unit in range(1, owner.shape[0]):
-        found = jnp.logical_or(found, owner[unit] == me)
-    return found
+    return held_by(owner, lax.axis_index("shard"))[0]
 
 
 def block(ref, rows, cols, start=0, count=None):
@@ -101,20 +176,16 @@
 
 def shampoo_kernel(rows, cols, owner, *refs):
     tensor = lax.axis_size("tensor")
-    left, grad, (root, out, norm, adam, half) = refs[:tensor], refs[tensor : 2 * tensor], refs[2 * tensor :]
+    left, grad, (root, out, norm, adam, half) = refs[0], refs[1 : tensor + 1], refs[tensor + 1 :]
     part = lax.axis_index("tensor")
 
     @pl.when(holds(owner))
     def _():
-        depth = left[0].shape[0]
         total = jnp.zeros(out.shape, f32)
         adam_sq = jnp.zeros((), f32)
         for k in range(tensor):
             columns = block(grad[k], rows, cols)
-            for i in range(tensor):
-                product = jnp.dot(left[i][...], columns, preferred_element_type=f32)
-                place = pl.multiple_of((part ^ i) * depth, depth)
-                half[k, pl.ds(place, depth), :] = product.astype(bf16)
+            half[k] = jnp.dot(left[...], columns, preferred_element_type=f32).astype(bf16)
             if grad[k].shape[2] > cols:
                 extra = grad[k][:, :, cols:]
             else:
@@ -138,13 +209,13 @@
 
 def shampoo_part(owner, left, grad, root, rows):
     cols = root.shape[2]
-    depth = left[0].shape[1]
-    tensor = len(left)
+    depth = left.shape[1]
+    tensor = len(grad)
     small = jax.ShapeDtypeStruct((8, LANES), f32)
     return pl.pallas_call(
         functools.partial(shampoo_kernel, rows, cols),
         out_shape=(jax.ShapeDtypeStruct((depth, cols), f32), small, small),
-        in_specs=[SMEM] + [VMEM] * (2 * tensor + 1),
+        in_specs=[SMEM] + [VMEM] * (tensor + 2),
         out_specs=(VMEM, VMEM, VMEM),
         scratch_shapes=[pltpu.VMEM((tensor, depth, cols), bf16)],
         cost_estimate=pl.CostEstimate(
@@ -152,7 +223,7 @@
             bytes_accessed=2 * depth * depth + 2 * depth * cols * tensor + 6 * depth * cols,
             transcendentals=0,
         ),
-    )(owner, *left, *grad, root)
+    )(owner, left, *grad, root)
 
 
 def stats_kernel(rows, cols, paired, owner, *refs):
@@ -211,21 +282,35 @@
     )(owner, *grad, *stats)
 
 
-def weight_kernel(owner, weight, back, out):
-    def unit(u, carry):
-        out[u] = weight[u] - learn_rate * back[owner[u]].astype(f32)
-        return carry
-
-    lax.fori_loop(0, weight.shape[0], unit, 0, unroll=weight.shape[0] <= 4)
+def weight_kernel(owner, weight, *refs):
+    back, out = refs[:-1], refs[-1]
+    if len(back) == 1:
+
+        def unit(u, carry):
+            out[u] = weight[u] - learn_rate * back[0][owner[u]].astype(f32)
+            return carry
+
+        lax.fori_loop(0, weight.shape[0], unit, 0)
+        return
+    me = lax.axis_index("shard")
+    for k, ref in enumerate(back):
+        found, index = held_by(owner, me ^ k)
+
+        @pl.when(found)
+        def _():
+            out[index] = weight[index] - learn_rate * ref[...].astype(f32)
 
 
 def weight_part(owner, weight, back):
     return pl.pallas_call(
         weight_kernel,
         out_shape=jax.ShapeDtypeStruct(weight.shape, f32),
-        in_specs=[SMEM, VMEM, VMEM],
+        in_specs=[SMEM] + [VMEM] * (1 + len(back)),
         out_specs=VMEM,
-    )(owner, weight, back)
+        cost_estimate=pl.CostEstimate(
+            flops=2 * weight.size, bytes_accessed=12 * weight.size, transcendentals=0
+        ),
+    )(owner, weight, *back)
 
 
 def flip(value, bits):
@@ -234,9 +319,17 @@
 
 
 def spread(value):
-    blocks = [value]
+    return spread_rest(*spread_first(value))
+
+
+def spread_first(value):
+    return value, flip(value, lax.axis_size("tensor") // 2)
+
+
+def spread_rest(value, far):
     bit = lax.axis_size("tensor") // 2
-    held = {0: value}
+    held = {0: value, bit: far}
+    bit //= 2
     while bit:
         for k in sorted(held):
             held[k | bit] = flip(held[k], bit)
@@ -244,17 +337,65 @@
     return [held[k] for k in range(len(held))]
 
 
-def over_shard(value):
-    return lax.all_to_all(value, "shard", split_axis=0, concat_axis=0, tiled=True)
+def rows_kernel(*refs):
+    out, part = refs[-1], lax.axis_index("tensor")
+    depth = refs[0].shape[0]
+    for k, ref in enumerate(refs[:-1]):
+        out[pl.ds(pl.multiple_of((part ^ k) * depth, depth), depth), :] = ref[...]
+
+
+def whole_root(rows, far):
+    parts = spread_rest(rows, far)
+    shape = (rows.shape[0] * len(parts), rows.shape[1])
+    return pl.pallas_call(
+        rows_kernel,
+        out_shape=jax.ShapeDtypeStruct(shape, bf16),
+        in_specs=[VMEM] * len(parts),
+        out_specs=VMEM,
+        cost_estimate=pl.CostEstimate(
+            flops=0, bytes_accessed=4 * rows.size * len(parts), transcendentals=0
+        ),
+    )(*parts)
+
+
+def scale_kernel(direct, done, adam, *refs):
+    tensor = lax.axis_size("tensor")
+    norm, out = refs[:tensor], refs[tensor:]
+    total = norm[0][...]
+    for other in norm[1:]:
+        total = total + other[...]
+    scale = jnp.sqrt(adam[...] / (total + graft_eps))[0, 0]
+    if not direct:
+        out[0][...] = (scale * done[...]).astype(bf16)
+        return
+    me = lax.axis_index("shard")
+    for k, ref in enumerate(out):
+        rows = ref.shape[0]
+        ref[...] = (scale * done[pl.ds(pl.multiple_of((me ^ k) * rows, rows), rows), :]).astype(bf16)
 
 
 def grafted(done, norm, adam, owners):
-    bit = 1
-    while bit < lax.axis_size("tensor"):
-        norm = norm + flip(norm, bit)
-        bit *= 2
-    scale = jnp.sqrt(adam[0, 0] / (norm[0, 0] + graft_eps))
-    return (scale * done).astype(bf16).reshape(owners, -1, done.shape[1])
+    depth, cols = done.shape
+    rows = depth // owners
+    norms = [norm] + [flip(norm, k) for k in range(1, lax.axis_size("tensor"))]
+    direct = by_permutes(owners, rows)
+    shapes = [(rows, cols)] * owners if direct else [done.shape]
+    out = pl.pallas_call(
+        functools.partial(scale_kernel, direct),
+        out_shape=tuple(jax.ShapeDtypeStruct(shape, bf16) for shape in shapes),
+        in_specs=[VMEM] * (2 + len(norms)),
+        out_specs=(VMEM,) * len(shapes),
+        cost_estimate=pl.CostEstimate(
+            flops=done.size, bytes_accessed=6 * done.size, transcendentals=0
+        ),
+    )(done, adam, *norms)
+    return out if direct else [out[0].reshape(owners, rows, cols)]
+
+
+def returned(out):
+    if len(out) > 1:
+        return [out[0]] + [cross(out[k], k) for k in range(1, len(out))]
+    return [lax.all_to_all(out[0], "shard", split_axis=0, concat_axis=0, tiled=True)]
 
 
 def per_device(
@@ -284,14 +425,19 @@
     glu_packed, glu_moment_out, glu_second_out = adam_part(
         glu_owner, glu_grads, glu_moment, glu_second, owners
     )
-    att_left = spread(att_left_root[0])
-    glu_left = spread(glu_left_root[0])
-    att_grad = spread(over_shard(att_packed))
+    att_root, att_root_far = spread_first(att_left_root[0])
+    glu_root, glu_root_far = spread_first(glu_left_root[0])
+    att_near, att_far = spread_first(gathered(att_packed, att_root_far, glu_root_far))
+    att_left = whole_root(att_root, att_root_far)
+    att_grad = spread_rest(att_near, att_far)
     att_done, att_norm, att_adam = shampoo_part(att_owner, att_left, att_grad, att_right_root, rows)
-    glu_grad = spread(over_shard(glu_packed))
+    glu_left = whole_root(glu_root, glu_root_far)
+    glu_near, glu_far = spread_first(gathered(glu_packed, att_far))
+    att_send = grafted(att_done, att_norm, att_adam, owners)
+    glu_grad = spread_rest(glu_near, after(glu_far, att_send[0]))
+    att_back = returned(att_send)
     glu_done, glu_norm, glu_adam = shampoo_part(glu_owner, glu_left, glu_grad, glu_right_root, rows)
-    att_back = over_shard(grafted(att_done, att_norm, att_adam, owners))
-    glu_back = over_shard(grafted(glu_done, glu_norm, glu_adam, owners))
+    glu_back = returned(grafted(glu_done, glu_norm, glu_adam, owners))
     (att_stats_out,) = stats_part(att_owner, att_grad, (att_stats,), rows, att_weight.shape[2])
     glu_left_out, glu_right_out = stats_part(
         glu_owner, glu_grad, (glu_left_stat, glu_right_stat), rows, glu_weight.shape[2]

time: 111 us -> 130 us (1.17)
  starting transfers between devices: 36.8 us -> 56.7 us
  Pallas kernels: 20.9 us -> 37.3 us
  waiting for transfers between devices: 36.3 us -> 24.2 us
  other arithmetic: 5.27 us -> 0 us
  local copies, waits for them, and re-layouts: 7.54 us -> 10.1 us
  between operations: 3.36 us -> 1.09 us
    ppermute x0 -> x28, starting transfers between devices: none -> 46.8 us  [cross(): return lax.ppermute(value, 'shard', [(i, i ^ bits) for i in range(size)])]
    all_to_all x4 -> x0, starting transfers between devices: 26.9 us -> none  [over_shard(): lax.all_to_all(value, 'shard', split_axis=0, concat_axis=0, tiled=True)]
    all_to_all x4 -> x0, waiting for transfers between devices: 22.1 us -> none  [over_shard(): lax.all_to_all(value, 'shard', split_axis=0, concat_axis=0, tiled=True)]
    pallas_call x2 -> x8, Pallas kernels: 5.33 us -> 18.3 us  [the longest x2 6.12 us: adam_part(): pl.pallas_call(functools.partial(adam_kernel, len(packed) > 1), out_shape...]
    ppermute x0 -> x28, waiting for transfers between devices: none -> 11.3 us  [cross(): return lax.ppermute(value, 'shard', [(i, i ^ bits) for i in range(size)])]
    unnamed x31 -> x125, local copies, waits for them, and re-layouts: 4.08 us -> 10.1 us
    convert_element_type x2 -> x0, other arithmetic: 3.91 us -> none  [grafted(): return (scale * done).astype(bf16).reshape(owners, -1, done.shape[1])]
    slice x4 -> x0, local copies, waits for them, and re-layouts: 3.47 us -> none  [grafted(): scale = jnp.sqrt(adam[0, 0] / (norm[0, 0] + graft_eps))]
  transfers between devices with their start and end apart: 20 -> 46, of which waited for: 9 -> 16; matrix products, arithmetic and copies ran while one was open for 9% -> 1% of each run, Pallas kernels for 15% -> 26%
where the time goes in v2:
time: 130 us; the launch traced here: 129 us
  starting transfers between devices  56.7 us (44%)
  Pallas kernels  37.3 us (29%)
  waiting for transfers between devices  24.2 us (19%)
  local copies, waits for them, and re-layouts  10.1 us (8%)
    ppermute x28, starting transfers between devices, cross(): return lax.ppermute(value, 'shard', [(i, i ^ bits) for i in range(size)])  46.8 us
    ppermute x18, waiting for transfers between devices, flip(): return lax.ppermute(value, 'tensor', [(i, i ^ bits) for i in range(size)])  12.9 us
    ppermute x28, waiting for transfers between devices, cross(): return lax.ppermute(value, 'shard', [(i, i ^ bits) for i in range(size)])  11.3 us
    unnamed x125, local copies, waits for them, and re-layouts  10.1 us
    ppermute x18, starting transfers between devices, flip(): return lax.ppermute(value, 'tensor', [(i, i ^ bits) for i in range(size)])  9.88 us
    pallas_call x2, Pallas kernels, shampoo_part(): pl.pallas_call(functools.partial(shampoo_kernel, rows, cols), out_shape=(...  7.8 us
    pallas_call x2, Pallas kernels, stats_part(): pl.pallas_call(functools.partial(stats_kernel, rows, cols, len(stats) ==...  7.14 us
    pallas_call x2, Pallas kernels, adam_part(): pl.pallas_call(functools.partial(adam_kernel, len(packed) > 1), out_shape...  6.12 us
  transfers between devices with their start and end apart: 46, of which 16 were waited for; matrix products, arithmetic and copies ran while one was open for 1% of the time, Pallas kernels for 26%

profile of v2, /device:TPU:0, one launch (start us, length us, event | category | flops | bytes accessed | tf_op | source)
XLA Modules:
  0.0 129.4 jit_solution(764828896500768428)
XLA Ops:
  0.6 3.0 %collective-permute-start.1 = (bf16[192,768]{1,0:T(8,128)(2,1)}, bf16[192,768]{1,0:T(8,128)(2,1)S(1)}, u32[]{:S(2)}, u32[]{:S(2)}) collective-permute-start(bf16[192,768]{1,0:T(8,128)(2,1)} %bitcast.2), channel_id=1, source_target_pairs={{0,2},{1,3},{2,0},{3,1},{4,6},{5,7},{6,4},{7,5},{8,10},{9,11},{10,... | collective-permute-start | bytes 884744 | tf_op jit(solution)/shard_map/ppermute | solution.py:318
  3.8 3.2 %shard_map.233 = (bf16[96,256]{1,0:T(8,128)(2,1)}, bf16[96,256]{1,0:T(8,128)(2,1)}, bf16[96,256]{1,0:T(8,128)(2,1)}, bf16[96,256]{1,0:T(8,128)(2,1)}, bf16[96,25...) custom-call(s32[4]{0:T(128)} %owner.14, ...), custom_call_target="tpu_custom_call" | custom-call | flops 1474560 | bytes 2359296 | tf_op jit(solution)/shard_map/pallas_call | solution.py:104
  11.2 3.0 %collective-permute-start.7 = (bf16[96,256]{1,0:T(8,128)(2,1)}, bf16[96,256]{1,0:T(8,128)(2,1)S(1)}, u32[]{:S(2)}, u32[]{:S(2)}) collective-permute-start(bf16[96,256]{1,0:T(8,128)(2,1)} %get-tuple-element.61), channel_id=1, source_target_pairs={{0,16},{4,20},{8,24},{12,28},{16,0},{20,4},{24,8},{28,12},{1,17},{... | collective-permute-start | bytes 147464 | tf_op jit(solution)/shard_map/ppermute | solution.py:127
  16.0 3.6 %collective-permute-start.9 = (bf16[96,256]{1,0:T(8,128)(2,1)}, bf16[96,256]{1,0:T(8,128)(2,1)S(1)}, u32[]{:S(2)}, u32[]{:S(2)}) collective-permute-start(bf16[96,256]{1,0:T(8,128)(2,1)} %get-tuple-element.63), channel_id=1, source_target_pairs={{0,24},{4,28},{8,16},{12,20},{16,8},{20,12},{24,0},{28,4},{1,25},{... | collective-permute-start | bytes 147464 | tf_op jit(solution)/shard_map/ppermute | solution.py:127
  19.6 2.3 %collective-permute-start.10 = (bf16[96,256]{1,0:T(8,128)(2,1)}, bf16[96,256]{1,0:T(8,128)(2,1)S(1)}, u32[]{:S(2)}, u32[]{:S(2)}) collective-permute-start(bf16[96,256]{1,0:T(8,128)(2,1)} %get-tuple-element.64), channel_id=1, source_target_pairs={{0,28},{4,24},{8,20},{12,16},{16,12},{20,8},{24,4},{28,0},{1,29},{... | collective-permute-start | bytes 147464 | tf_op jit(solution)/shard_map/ppermute | solution.py:127
  23.1 3.6 %collective-permute-done.10.refs_7_ = bf16[96,256]{1,0:T(8,128)(2,1)S(1)} collective-permute-done((bf16[96,256]{1,0:T(8,128)(2,1)}, bf16[96,256]{1,0:T(8,128)(2,1)S(1)}, u32[]{:S(2)}, u32[]{:S(2)}) %collective-permute-start.10) | collective-permute-done | bytes 49184 | tf_op jit(solution)/shard_map/ppermute | solution.py:127
  30.6 2.9 %shard_map.239 = (bf16[104,256]{1,0:T(8,128)(2,1)}, bf16[104,256]{1,0:T(8,128)(2,1)}, bf16[104,256]{1,0:T(8,128)(2,1)}, bf16[104,256]{1,0:T(8,128)(2,1)}, bf16[1...) custom-call(s32[4]{0:T(128)} %owner.15, ...), custom_call_target="tpu_custom_call" | custom-call | flops 1966080 | bytes 3145728 | tf_op jit(solution)/shard_map/pallas_call | solution.py:104
  33.6 3.4 %collective-permute-start.28 = (bf16[104,256]{1,0:T(8,128)(2,1)}, bf16[104,256]{1,0:T(8,128)(2,1)S(1)}, u32[]{:S(2)}, u32[]{:S(2)}) collective-permute-start(bf16[104,256]{1,0:T(8,128)(2,1)} %get-tuple-element.82), channel_id=1, source_target_pairs={{0,12},{4,8},{8,4},{12,0},{16,28},{20,24},{24,20},{28,16},{1,13},{... | collective-permute-start | bytes 159752 | tf_op jit(solution)/shard_map/ppermute | solution.py:127
  40.1 2.8 %collective-permute-start.31 = (bf16[104,256]{1,0:T(8,128)(2,1)}, bf16[104,256]{1,0:T(8,128)(2,1)S(1)}, u32[]{:S(2)}, u32[]{:S(2)}) collective-permute-start(bf16[104,256]{1,0:T(8,128)(2,1)} %get-tuple-element.85), channel_id=1, source_target_pairs={{0,24},{4,28},{8,16},{12,20},{16,8},{20,12},{24,0},{28,4},{1,25},{... | collective-permute-start | bytes 159752 | tf_op jit(solution)/shard_map/ppermute | solution.py:127
  42.9 2.4 %collective-permute-start.32 = (bf16[104,256]{1,0:T(8,128)(2,1)}, bf16[104,256]{1,0:T(8,128)(2,1)S(1)}, u32[]{:S(2)}, u32[]{:S(2)}) collective-permute-start(bf16[104,256]{1,0:T(8,128)(2,1)} %get-tuple-element.86), channel_id=1, source_target_pairs={{0,28},{4,24},{8,20},{12,16},{16,12},{20,8},{24,4},{28,0},{1,29},{... | collective-permute-start | bytes 159752 | tf_op jit(solution)/shard_map/ppermute | solution.py:127
  46.7 3.3 %collective-permute-done.32.refs_7_ = bf16[104,256]{1,0:T(8,128)(2,1)S(1)} collective-permute-done((bf16[104,256]{1,0:T(8,128)(2,1)}, bf16[104,256]{1,0:T(8,128)(2,1)S(1)}, u32[]{:S(2)}, u32[]{:S(2)}) %collective-permute-start.32) | collective-permute-done | bytes 53280 | tf_op jit(solution)/shard_map/ppermute | solution.py:127
  56.1 2.3 %shard_map.232.refs_0_ = bf16[768,768]{1,0:T(8,128)(2,1)} custom-call(bf16[192,768]{1,0:T(8,128)(2,1)} %bitcast.3, bf16[192,768]{1,0:T(8,128)(2,1)} %copy-done.9, bf16[192,768]{1,0:T(8,128)(2,1)} %copy-done.8, bf16[192,768]{1,0:T(8,128)(2,1)} %copy-done.11), custom_call_target="tpu_custom_call" | custom-call | bytes 2359296 | tf_op jit(solution)/shard_map/pallas_call | solution.py:350
  59.9 4.9 %shard_map.235 = (f32[768,192]{1,0:T(8,128)}, f32[8,128]{1,0:T(8,128)}, f32[8,128]{1,0:T(8,128)}) custom-call(s32[4]{0:T(128)} %owner.14, bf16[768,768]{1,0:T(8,128)(2,1)} %shard_map.232.refs_0_, bf16[8,96,256]{2,1,0:T(8,128)(2,1)} %shard_map.234.refs_1_.refs_0_, bf16[8,96,256]{2,1,0:T(8,128)(2,1)} %copy-done.3, bf16[8,96,256]{2,1,0:T(8,128)(2,1)} %copy-done.2, ...), custom_call_target="tpu_custom_call" | custom-call | flops 1132462080 | bytes 3244032 | tf_op jit(solution)/shard_map/pallas_call | solution.py:215
  76.0 2.3 %shard_map.238.refs_0_ = bf16[768,768]{1,0:T(8,128)(2,1)} custom-call(bf16[192,768]{1,0:T(8,128)(2,1)} %bitcast.6, bf16[192,768]{1,0:T(8,128)(2,1)} %copy-done.10, bf16[192,768]{1,0:T(8,128)(2,1)} %copy-done.7, bf16[192,768]{1,0:T(8,128)(2,1)} %copy-done.12), custom_call_target="tpu_custom_call" | custom-call | bytes 2359296 | tf_op jit(solution)/shard_map/pallas_call | solution.py:350
  78.3 2.1 %collective-permute-start.18 = (bf16[96,192]{1,0:T(8,128)(2,1)S(1)}, bf16[96,192]{1,0:T(8,128)(2,1)S(1)}, u32[]{:S(2)}, u32[]{:S(2)}) collective-permute-start(bf16[96,192]{1,0:T(8,128)(2,1)S(1)} %copy-done.58), channel_id=1, source_target_pairs={{0,8},{4,12},{8,0},{12,4},{16,24},{20,28},{24,16},{28,20},{1,9},{5... | collective-permute-start | bytes 110600 | tf_op jit(solution)/shard_map/ppermute | solution.py:127
  83.3 2.9 %shard_map.241 = (f32[768,256]{1,0:T(8,128)}, f32[8,128]{1,0:T(8,128)}, f32[8,128]{1,0:T(8,128)}) custom-call(s32[4]{0:T(128)} %owner.15, bf16[768,768]{1,0:T(8,128)(2,1)} %shard_map.238.refs_0_, bf16[8,104,256]{2,1,0:T(8,128)(2,1)} %shard_map.240.refs_1_.refs_0_, bf16[8,104,256]{2,1,0:T(8,128)(2,1)} %copy-done.48, ...), custom_call_target="tpu_custom_call" | custom-call | flops 1610612736 | bytes 3932160 | tf_op jit(solution)/shard_map/pallas_call | solution.py:215
  88.2 3.2 %collective-permute-done.37.refs_2_ = f32[8,128]{1,0:T(8,128)S(1)} collective-permute-done((f32[8,128]{1,0:T(8,128)}, f32[8,128]{1,0:T(8,128)S(1)}, u32[]{:S(2)}, u32[]{:S(2)}) %collective-permute-start.37) | collective-permute-done | bytes 4128 | tf_op jit(solution)/shard_map/ppermute | solution.py:318
  91.4 3.2 %collective-permute-done.38.refs_3_ = f32[8,128]{1,0:T(8,128)S(1)} collective-permute-done((f32[8,128]{1,0:T(8,128)}, f32[8,128]{1,0:T(8,128)S(1)}, u32[]{:S(2)}, u32[]{:S(2)}) %collective-permute-start.38) | collective-permute-done | bytes 4128 | tf_op jit(solution)/shard_map/ppermute | solution.py:318
  98.2 3.9 %collective-permute-start.40 = (bf16[96,256]{1,0:T(8,128)(2,1)}, bf16[96,256]{1,0:T(8,128)(2,1)S(1)}, u32[]{:S(2)}, u32[]{:S(2)}) collective-permute-start(bf16[96,256]{1,0:T(8,128)(2,1)} %get-tuple-element.93), channel_id=1, source_target_pairs={{0,8},{4,12},{8,0},{12,4},{16,24},{20,28},{24,16},{28,20},{1,9},{5... | collective-permute-start | bytes 147464 | tf_op jit(solution)/shard_map/ppermute | solution.py:127
  104.3 2.9 %collective-permute-start.23 = (bf16[96,192]{1,0:T(8,128)(2,1)S(1)}, bf16[96,192]{1,0:T(8,128)(2,1)S(1)}, u32[]{:S(2)}, u32[]{:S(2)}) collective-permute-start(bf16[96,192]{1,0:T(8,128)(2,1)S(1)} %copy-done.50), channel_id=1, source_target_pairs={{0,28},{4,24},{8,20},{12,16},{16,12},{20,8},{24,4},{28,0},{1,29},{... | collective-permute-start | bytes 110600 | tf_op jit(solution)/shard_map/ppermute | solution.py:127
  107.2 3.9 %shard_map.244 = f32[1,2,192,768]{3,2,1,0:T(8,128)} custom-call(s32[4]{0:T(128)} %owner.14, bf16[8,96,256]{2,1,0:T(8,128)(2,1)} %shard_map.234.refs_1_.refs_0_, bf16[8,96,256]{2,1,0:T(8,128)(2,1)} %copy-done.3, bf16[8,96,256]{2,1,0:T(8,128)(2,1)} %copy-done.2, bf16[8,96,256]{2,1,0:T(8,128)(2,1)} %copy-done.4, f32[1,2,192,768]{3,2,1,0:T(8,128)} %refs_4_.2), custom_call_target="tpu_custom_call" | custom-call | flops 452984832 | bytes 3538944 | tf_op jit(solution)/shard_map/pallas_call | solution.py:271
  112.4 2.0 %shard_map.237 = f32[4,96,192]{2,1,0:T(8,128)} custom-call(s32[4]{0:T(128)} %owner.14, f32[4,96,192]{2,1,0:T(8,128)} %weight.2, bf16[96,192]{1,0:T(8,128)(2,1)} %get-tuple-element.68.refs_0_, bf16[96,192]{1,0:T(8,128)(2,1)} %copy-done.22, bf16[96,192]{1,0:T(8,128)(2,1)} %copy-done.23, bf16[96,192]{1,0:T(8,128)(2,1)} %copy-done.24, ...), custom_call_target="tpu_custom_call" | custom-call | flops 147456 | bytes 884736 | tf_op jit(solution)/shard_map/pallas_call | solution.py:305
  119.9 3.3 %collective-permute-start.45 = (bf16[96,256]{1,0:T(8,128)(2,1)S(1)}, bf16[96,256]{1,0:T(8,128)(2,1)S(1)}, u32[]{:S(2)}, u32[]{:S(2)}) collective-permute-start(bf16[96,256]{1,0:T(8,128)(2,1)S(1)} %copy-done.54), channel_id=1, source_target_pairs={{0,28},{4,24},{8,20},{12,16},{16,12},{20,8},{24,4},{28,0},{1,29},{... | collective-permute-start | bytes 147464 | tf_op jit(solution)/shard_map/ppermute | solution.py:127
  123.2 3.2 %shard_map.245 = (f32[1,192,768]{2,1,0:T(8,128)}, f32[1,256,1024]{2,1,0:T(8,128)}) custom-call(s32[4]{0:T(128)} %owner.15, bf16[8,104,256]{2,1,0:T(8,128)(2,1)} %shard_map.240.refs_1_.refs_0_, bf16[8,104,256]{2,1,0:T(8,128)(2,1)} %copy-done.48, bf16[8,104,256]{2,1,0:T(8,128)(2,1)} %collective-permute-done.34.refs_3_.refs_2_, ...), custom_call_target="tpu_custom_call" | custom-call | flops 1073741824 | bytes 5373952 | tf_op jit(solution)/shard_map/pallas_call | solution.py:271
  (207 shorter events, 54.4 us)
Async XLA Ops:
  0.6 15.4 %collective-permute-start.1 = (bf16[192,768]{1,0:T(8,128)(2,1)}, bf16[192,768]{1,0:T(8,128)(2,1)S(1)}, u32[]{:S(2)}, u32[]{:S(2)}) collective-permute-start(bf16[192,768]{1,0:T(8,128)(2,1)} %bitcast.2), channel_id=1, source_target_pairs={{0,2},{1,3},{2,0},{3,1},{4,6},{5,7},{6,4},{7,5},{8,10},{9,11},{10,... | collective-permute-start | bytes 884744 | tf_op jit(solution)/shard_map/ppermute | solution.py:318
  3.7 16.0 %collective-permute-start.3 = (bf16[192,768]{1,0:T(8,128)(2,1)}, bf16[192,768]{1,0:T(8,128)(2,1)S(1)}, u32[]{:S(2)}, u32[]{:S(2)}) collective-permute-start(bf16[192,768]{1,0:T(8,128)(2,1)} %bitcast.5), channel_id=1, source_target_pairs={{0,2},{1,3},{2,0},{3,1},{4,6},{5,7},{6,4},{7,5},{8,10},{9,11},{10,... | collective-permute-start | bytes 884744 | tf_op jit(solution)/shard_map/ppermute | solution.py:318
  10.4 11.5 %collective-permute-start.6 = (bf16[96,256]{1,0:T(8,128)(2,1)}, bf16[96,256]{1,0:T(8,128)(2,1)S(1)}, u32[]{:S(2)}, u32[]{:S(2)}) collective-permute-start(bf16[96,256]{1,0:T(8,128)(2,1)} %get-tuple-element.60), channel_id=1, source_target_pairs={{0,12},{4,8},{8,4},{12,0},{16,28},{20,24},{24,20},{28,16},{1,13},{... | collective-permute-start | bytes 147464 | tf_op jit(solution)/shard_map/ppermute | solution.py:127
  11.2 10.7 %collective-permute-start.7 = (bf16[96,256]{1,0:T(8,128)(2,1)}, bf16[96,256]{1,0:T(8,128)(2,1)S(1)}, u32[]{:S(2)}, u32[]{:S(2)}) collective-permute-start(bf16[96,256]{1,0:T(8,128)(2,1)} %get-tuple-element.61), channel_id=1, source_target_pairs={{0,16},{4,20},{8,24},{12,28},{16,0},{20,4},{24,8},{28,12},{1,17},{... | collective-permute-start | bytes 147464 | tf_op jit(solution)/shard_map/ppermute | solution.py:127
  14.3 7.7 %collective-permute-start.8 = (bf16[96,256]{1,0:T(8,128)(2,1)}, bf16[96,256]{1,0:T(8,128)(2,1)S(1)}, u32[]{:S(2)}, u32[]{:S(2)}) collective-permute-start(bf16[96,256]{1,0:T(8,128)(2,1)} %get-tuple-element.62), channel_id=1, source_target_pairs={{0,20},{4,16},{8,28},{12,24},{16,4},{20,0},{24,12},{28,8},{1,21},{... | collective-permute-start | bytes 147464 | tf_op jit(solution)/shard_map/ppermute | solution.py:127
  29.0 8.9 %collective-permute-start.12 = (bf16[8,96,256]{2,1,0:T(8,128)(2,1)}, bf16[8,96,256]{2,1,0:T(8,128)(2,1)S(1)}, u32[]{:S(2)}, u32[]{:S(2)}) collective-permute-start(bf16[8,96,256]{2,1,0:T(8,128)(2,1)} %shard_map.234.refs_1_.refs_0_), channel_id=1, source_target_pairs={{0,2},{1,3},{2,0},{3,1},{4,6},{5,7},{6,4},{7,5},{8,10},{9,11},{10,... | collective-permute-start | bytes 1179656 | tf_op jit(solution)/shard_map/ppermute | solution.py:318
  37.9 20.5 %collective-permute-start.11 = (bf16[8,96,256]{2,1,0:T(8,128)(2,1)S(1)}, bf16[8,96,256]{2,1,0:T(8,128)(2,1)S(1)}, u32[]{:S(2)}, u32[]{:S(2)}) collective-permute-start(bf16[8,96,256]{2,1,0:T(8,128)(2,1)S(1)} %copy-done), channel_id=1, source_target_pairs={{0,1},{1,0},{2,3},{3,2},{4,5},{5,4},{6,7},{7,6},{8,9},{9,8},{10,11... | collective-permute-start | bytes 1179656 | tf_op jit(solution)/shard_map/ppermute | solution.py:318
  38.0 20.5 %collective-permute-start.13 = (bf16[8,96,256]{2,1,0:T(8,128)(2,1)S(1)}, bf16[8,96,256]{2,1,0:T(8,128)(2,1)S(1)}, u32[]{:S(2)}, u32[]{:S(2)}) collective-permute-start(bf16[8,96,256]{2,1,0:T(8,128)(2,1)S(1)} %collective-permute-done.12.refs_3_.refs_2_), channel_id=1, source_target_pairs={{0,1},{1,0},{2,3},{3,2},{4,5},{5,4},{6,7},{7,6},{8,9},{9,8},{10,11... | collective-permute-start | bytes 1179656 | tf_op jit(solution)/shard_map/ppermute | solution.py:318
  38.5 8.2 %collective-permute-start.30 = (bf16[104,256]{1,0:T(8,128)(2,1)}, bf16[104,256]{1,0:T(8,128)(2,1)S(1)}, u32[]{:S(2)}, u32[]{:S(2)}) collective-permute-start(bf16[104,256]{1,0:T(8,128)(2,1)} %get-tuple-element.84), channel_id=1, source_target_pairs={{0,20},{4,16},{8,28},{12,24},{16,4},{20,0},{24,12},{28,8},{1,21},{... | collective-permute-start | bytes 159752 | tf_op jit(solution)/shard_map/ppermute | solution.py:127
  52.5 19.8 %collective-permute-start.34 = (bf16[8,104,256]{2,1,0:T(8,128)(2,1)}, bf16[8,104,256]{2,1,0:T(8,128)(2,1)}, u32[]{:S(2)}, u32[]{:S(2)}) collective-permute-start(bf16[8,104,256]{2,1,0:T(8,128)(2,1)} %shard_map.240.refs_1_.refs_0_), channel_id=1, source_target_pairs={{0,2},{1,3},{2,0},{3,1},{4,6},{5,7},{6,4},{7,5},{8,10},{9,11},{10,... | collective-permute-start | bytes 1277960 | tf_op jit(solution)/shard_map/ppermute | solution.py:318
  66.7 15.1 %collective-permute-start.33 = (bf16[8,104,256]{2,1,0:T(8,128)(2,1)S(1)}, bf16[8,104,256]{2,1,0:T(8,128)(2,1)S(1)}, u32[]{:S(2)}, u32[]{:S(2)}) collective-permute-start(bf16[8,104,256]{2,1,0:T(8,128)(2,1)S(1)} %copy-done.1), channel_id=1, source_target_pairs={{0,1},{1,0},{2,3},{3,2},{4,5},{5,4},{6,7},{7,6},{8,9},{9,8},{10,11... | collective-permute-start | bytes 1277960 | tf_op jit(solution)/shard_map/ppermute | solution.py:318
  72.3 9.8 %collective-permute-start.35 = (bf16[8,104,256]{2,1,0:T(8,128)(2,1)}, bf16[8,104,256]{2,1,0:T(8,128)(2,1)S(1)}, u32[]{:S(2)}, u32[]{:S(2)}) collective-permute-start(bf16[8,104,256]{2,1,0:T(8,128)(2,1)} %collective-permute-done.34.refs_3_.refs_2_), channel_id=1, source_target_pairs={{0,1},{1,0},{2,3},{3,2},{4,5},{5,4},{6,7},{7,6},{8,9},{9,8},{10,11... | collective-permute-start | bytes 1277960 | tf_op jit(solution)/shard_map/ppermute | solution.py:318
  78.3 19.9 %collective-permute-start.17 = (bf16[96,192]{1,0:T(8,128)(2,1)S(1)}, bf16[96,192]{1,0:T(8,128)(2,1)S(1)}, u32[]{:S(2)}, u32[]{:S(2)}) collective-permute-start(bf16[96,192]{1,0:T(8,128)(2,1)S(1)} %copy-done.61), channel_id=1, source_target_pairs={{0,4},{4,0},{8,12},{12,8},{16,20},{20,16},{24,28},{28,24},{1,5},{5... | collective-permute-start | bytes 110600 | tf_op jit(solution)/shard_map/ppermute | solution.py:127
  78.3 23.9 %collective-permute-start.18 = (bf16[96,192]{1,0:T(8,128)(2,1)S(1)}, bf16[96,192]{1,0:T(8,128)(2,1)S(1)}, u32[]{:S(2)}, u32[]{:S(2)}) collective-permute-start(bf16[96,192]{1,0:T(8,128)(2,1)S(1)} %copy-done.58), channel_id=1, source_target_pairs={{0,8},{4,12},{8,0},{12,4},{16,24},{20,28},{24,16},{28,20},{1,9},{5... | collective-permute-start | bytes 110600 | tf_op jit(solution)/shard_map/ppermute | solution.py:127
  80.4 23.2 %collective-permute-start.19 = (bf16[96,192]{1,0:T(8,128)(2,1)S(1)}, bf16[96,192]{1,0:T(8,128)(2,1)S(1)}, u32[]{:S(2)}, u32[]{:S(2)}) collective-permute-start(bf16[96,192]{1,0:T(8,128)(2,1)S(1)} %copy-done.55), channel_id=1, source_target_pairs={{0,12},{4,8},{8,4},{12,0},{16,28},{20,24},{24,20},{28,16},{1,13},{... | collective-permute-start | bytes 110600 | tf_op jit(solution)/shard_map/ppermute | solution.py:127
  81.8 22.4 %collective-permute-start.20 = (bf16[96,192]{1,0:T(8,128)(2,1)S(1)}, bf16[96,192]{1,0:T(8,128)(2,1)S(1)}, u32[]{:S(2)}, u32[]{:S(2)}) collective-permute-start(bf16[96,192]{1,0:T(8,128)(2,1)S(1)} %copy-done.53), channel_id=1, source_target_pairs={{0,16},{4,20},{8,24},{12,28},{16,0},{20,4},{24,8},{28,12},{1,17},{... | collective-permute-start | bytes 110600 | tf_op jit(solution)/shard_map/ppermute | solution.py:127
  97.3 21.3 %collective-permute-start.39 = (bf16[96,256]{1,0:T(8,128)(2,1)}, bf16[96,256]{1,0:T(8,128)(2,1)S(1)}, u32[]{:S(2)}, u32[]{:S(2)}) collective-permute-start(bf16[96,256]{1,0:T(8,128)(2,1)} %get-tuple-element.92), channel_id=1, source_target_pairs={{0,4},{4,0},{8,12},{12,8},{16,20},{20,16},{24,28},{28,24},{1,5},{5... | collective-permute-start | bytes 147464 | tf_op jit(solution)/shard_map/ppermute | solution.py:127
  98.2 21.6 %collective-permute-start.40 = (bf16[96,256]{1,0:T(8,128)(2,1)}, bf16[96,256]{1,0:T(8,128)(2,1)S(1)}, u32[]{:S(2)}, u32[]{:S(2)}) collective-permute-start(bf16[96,256]{1,0:T(8,128)(2,1)} %get-tuple-element.93), channel_id=1, source_target_pairs={{0,8},{4,12},{8,0},{12,4},{16,24},{20,28},{24,16},{28,20},{1,9},{5... | collective-permute-start | bytes 147464 | tf_op jit(solution)/shard_map/ppermute | solution.py:127
  102.2 9.0 %collective-permute-start.21 = (bf16[96,192]{1,0:T(8,128)(2,1)S(1)}, bf16[96,192]{1,0:T(8,128)(2,1)S(1)}, u32[]{:S(2)}, u32[]{:S(2)}) collective-permute-start(bf16[96,192]{1,0:T(8,128)(2,1)S(1)} %copy-done.52), channel_id=1, source_target_pairs={{0,20},{4,16},{8,28},{12,24},{16,4},{20,0},{24,12},{28,8},{1,21},{... | collective-permute-start | bytes 110600 | tf_op jit(solution)/shard_map/ppermute | solution.py:127
  103.7 7.5 %collective-permute-start.22 = (bf16[96,192]{1,0:T(8,128)(2,1)S(1)}, bf16[96,192]{1,0:T(8,128)(2,1)S(1)}, u32[]{:S(2)}, u32[]{:S(2)}) collective-permute-start(bf16[96,192]{1,0:T(8,128)(2,1)S(1)} %copy-done.51), channel_id=1, source_target_pairs={{0,24},{4,28},{8,16},{12,20},{16,8},{20,12},{24,0},{28,4},{1,25},{... | collective-permute-start | bytes 110600 | tf_op jit(solution)/shard_map/ppermute | solution.py:127
  114.4 12.0 %collective-permute-start.41 = (bf16[96,256]{1,0:T(8,128)(2,1)S(1)}, bf16[96,256]{1,0:T(8,128)(2,1)S(1)}, u32[]{:S(2)}, u32[]{:S(2)}) collective-permute-start(bf16[96,256]{1,0:T(8,128)(2,1)S(1)} %copy-done.60), channel_id=1, source_target_pairs={{0,12},{4,8},{8,4},{12,0},{16,28},{20,24},{24,20},{28,16},{1,13},{... | collective-permute-start | bytes 147464 | tf_op jit(solution)/shard_map/ppermute | solution.py:127
  115.4 11.0 %collective-permute-start.42 = (bf16[96,256]{1,0:T(8,128)(2,1)S(1)}, bf16[96,256]{1,0:T(8,128)(2,1)S(1)}, u32[]{:S(2)}, u32[]{:S(2)}) collective-permute-start(bf16[96,256]{1,0:T(8,128)(2,1)S(1)} %copy-done.59), channel_id=1, source_target_pairs={{0,16},{4,20},{8,24},{12,28},{16,0},{20,4},{24,8},{28,12},{1,17},{... | collective-permute-start | bytes 147464 | tf_op jit(solution)/shard_map/ppermute | solution.py:127
  117.1 9.3 %collective-permute-start.43 = (bf16[96,256]{1,0:T(8,128)(2,1)S(1)}, bf16[96,256]{1,0:T(8,128)(2,1)S(1)}, u32[]{:S(2)}, u32[]{:S(2)}) collective-permute-start(bf16[96,256]{1,0:T(8,128)(2,1)S(1)} %copy-done.57), channel_id=1, source_target_pairs={{0,20},{4,16},{8,28},{12,24},{16,4},{20,0},{24,12},{28,8},{1,21},{... | collective-permute-start | bytes 147464 | tf_op jit(solution)/shard_map/ppermute | solution.py:127
  118.6 7.9 %collective-permute-start.44 = (bf16[96,256]{1,0:T(8,128)(2,1)S(1)}, bf16[96,256]{1,0:T(8,128)(2,1)S(1)}, u32[]{:S(2)}, u32[]{:S(2)}) collective-permute-start(bf16[96,256]{1,0:T(8,128)(2,1)S(1)} %copy-done.56), channel_id=1, source_target_pairs={{0,24},{4,28},{8,16},{12,20},{16,8},{20,12},{24,0},{28,4},{1,25},{... | collective-permute-start | bytes 147464 | tf_op jit(solution)/shard_map/ppermute | solution.py:127
  (84 other events, 583.1 us)

commit v3 on v1

--- a/solution.py
+++ b/solution.py
@@ -18,6 +18,7 @@
 f32 = jnp.float32
 LANES = 128
 VMEM = pl.BlockSpec(memory_space=pltpu.VMEM)
+LIMIT = pltpu.CompilerParams(vmem_limit_bytes=16 << 20)
 SMEM = pl.BlockSpec(memory_space=pltpu.SMEM)
 
 
@@ -31,7 +32,7 @@
 
 
 def pieces(total, shape):
-    full = jnp.full(shape, total, f32)
+    full = jnp.broadcast_to(total, shape)
     high = full.astype(bf16).astype(f32)
     middle = (full - high).astype(bf16).astype(f32)
     low = full - high - middle
@@ -55,7 +56,7 @@
         direction = moment_new / (jnp.sqrt(second_new) + adam_eps)
         moment_out[u] = moment_new
         second_out[u] = second_new
-        total = jnp.sum(direction * direction)
+        total = jnp.sum(direction * direction, axis=(0, 1), keepdims=True)
         slot = owner[u]
         if packed_cols > cols:
             packed[slot, :, :cols] = summed.astype(bf16)
@@ -80,6 +81,7 @@
         ),
         in_specs=[SMEM, VMEM, VMEM, VMEM],
         out_specs=(VMEM, VMEM, VMEM),
+        compiler_params=LIMIT,
         cost_estimate=pl.CostEstimate(
             flops=20 * moment.size, bytes_accessed=32 * moment.size, transcendentals=moment.size
         ),
@@ -101,20 +103,20 @@
 
 def shampoo_kernel(rows, cols, owner, *refs):
     tensor = lax.axis_size("tensor")
-    left, grad, (root, out, norm, adam, half) = refs[:tensor], refs[tensor : 2 * tensor], refs[2 * tensor :]
+    left, grad, (root, out, norm, adam, whole, half) = refs[:tensor], refs[tensor : 2 * tensor], refs[2 * tensor :]
     part = lax.axis_index("tensor")
 
     @pl.when(holds(owner))
     def _():
         depth = left[0].shape[0]
+        for i in range(tensor):
+            place = pl.multiple_of((part ^ i) * depth, depth)
+            whole[pl.ds(place, depth), :] = left[i][...]
         total = jnp.zeros(out.shape, f32)
         adam_sq = jnp.zeros((), f32)
         for k in range(tensor):
             columns = block(grad[k], rows, cols)
-            for i in range(tensor):
-                product = jnp.dot(left[i][...], columns, preferred_element_type=f32)
-                place = pl.multiple_of((part ^ i) * depth, depth)
-                half[k, pl.ds(place, depth), :] = product.astype(bf16)
+            half[k] = jnp.dot(whole[...], columns, preferred_element_type=f32).astype(bf16)
             if grad[k].shape[2] > cols:
                 extra = grad[k][:, :, cols:]
             else:
@@ -146,7 +148,8 @@
         out_shape=(jax.ShapeDtypeStruct((depth, cols), f32), small, small),
         in_specs=[SMEM] + [VMEM] * (2 * tensor + 1),
         out_specs=(VMEM, VMEM, VMEM),
-        scratch_shapes=[pltpu.VMEM((tensor, depth, cols), bf16)],
+        scratch_shapes=[pltpu.VMEM((depth, depth), bf16), pltpu.VMEM((tensor, depth, cols), bf16)],
+        compiler_params=LIMIT,
         cost_estimate=pl.CostEstimate(
             flops=2 * depth * cols * tensor * (depth + cols),
             bytes_accessed=2 * depth * depth + 2 * depth * cols * tensor + 6 * depth * cols,
@@ -203,6 +206,7 @@
         in_specs=[SMEM] + [VMEM] * (tensor + len(stats)),
         out_specs=(VMEM,) * len(stats),
         scratch_shapes=[pltpu.VMEM((tensor, cols, cols), f32)],
+        compiler_params=LIMIT,
         cost_estimate=pl.CostEstimate(
             flops=4 * depth * depth * cols,
             bytes_accessed=8 * sum(s.size for s in stats) + 2 * depth * depth,
@@ -225,6 +229,10 @@
         out_shape=jax.ShapeDtypeStruct(weight.shape, f32),
         in_specs=[SMEM, VMEM, VMEM],
         out_specs=VMEM,
+        compiler_params=LIMIT,
+        cost_estimate=pl.CostEstimate(
+            flops=2 * weight.size, bytes_accessed=12 * weight.size, transcendentals=0
+        ),
     )(owner, weight, back)
 
 
@@ -233,10 +241,14 @@
     return lax.ppermute(value, "tensor", [(i, i ^ bits) for i in range(size)])
 
 
-def spread(value):
-    blocks = [value]
+def spread_first(value):
+    return value, flip(value, lax.axis_size("tensor") // 2)
+
+
+def spread_rest(value, far):
     bit = lax.axis_size("tensor") // 2
-    held = {0: value}
+    held = {0: value, bit: far}
+    bit //= 2
     while bit:
         for k in sorted(held):
             held[k | bit] = flip(held[k], bit)
@@ -244,17 +256,36 @@
     return [held[k] for k in range(len(held))]
 
 
+def after(value, *others):
+    return lax.optimization_barrier((value, *others))[0]
+
+
 def over_shard(value):
     return lax.all_to_all(value, "shard", split_axis=0, concat_axis=0, tiled=True)
 
 
+def scale_kernel(done, adam, *refs):
+    norm, out = refs[:-1], refs[-1]
+    total = norm[0][...]
+    for other in norm[1:]:
+        total = total + other[...]
+    scale = jnp.sqrt(adam[...] / (total + graft_eps))[:1, :1]
+    out[...] = (scale * done[...]).astype(bf16)
+
+
 def grafted(done, norm, adam, owners):
-    bit = 1
-    while bit < lax.axis_size("tensor"):
-        norm = norm + flip(norm, bit)
-        bit *= 2
-    scale = jnp.sqrt(adam[0, 0] / (norm[0, 0] + graft_eps))
-    return (scale * done).astype(bf16).reshape(owners, -1, done.shape[1])
+    norms = [norm] + [flip(norm, k) for k in range(1, lax.axis_size("tensor"))]
+    out = pl.pallas_call(
+        scale_kernel,
+        out_shape=jax.ShapeDtypeStruct(done.shape, bf16),
+        in_specs=[VMEM] * (2 + len(norms)),
+        out_specs=VMEM,
+        compiler_params=LIMIT,
+        cost_estimate=pl.CostEstimate(
+            flops=done.size, bytes_accessed=6 * done.size, transcendentals=0
+        ),
+    )(done, adam, *norms)
+    return out.reshape(owners, -1, done.shape[1])
 
 
 def per_device(
@@ -284,13 +315,20 @@
     glu_packed, glu_moment_out, glu_second_out = adam_part(
         glu_owner, glu_grads, glu_moment, glu_second, owners
     )
-    att_left = spread(att_left_root[0])
-    glu_left = spread(glu_left_root[0])
-    att_grad = spread(over_shard(att_packed))
+    att_root, att_root_far = spread_first(att_left_root[0])
+    glu_root, glu_root_far = spread_first(glu_left_root[0])
+    att_left = spread_rest(att_root, att_root_far)
+    glu_left = spread_rest(glu_root, glu_root_far)
+    att_near, att_far = spread_first(
+        after(over_shard(att_packed), *att_left[1:], glu_root_far, glu_packed)
+    )
+    att_grad = spread_rest(att_near, att_far)
     att_done, att_norm, att_adam = shampoo_part(att_owner, att_left, att_grad, att_right_root, rows)
-    glu_grad = spread(over_shard(glu_packed))
+    glu_near, glu_far = spread_first(after(over_shard(glu_packed), att_done, *glu_left[1:]))
+    att_send = grafted(att_done, att_norm, att_adam, owners)
+    glu_grad = spread_rest(glu_near, after(glu_far, att_send))
+    att_back = over_shard(att_send)
     glu_done, glu_norm, glu_adam = shampoo_part(glu_owner, glu_left, glu_grad, glu_right_root, rows)
-    att_back = over_shard(grafted(att_done, att_norm, att_adam, owners))
     glu_back = over_shard(grafted(glu_done, glu_norm, glu_adam, owners))
     (att_stats_out,) = stats_part(att_owner, att_grad, (att_stats,), rows, att_weight.shape[2])
     glu_left_out, glu_right_out = stats_part(

time: 111 us -> 95.1 us (0.86)
  Pallas kernels: 20.9 us -> 14.6 us
  other arithmetic: 5.27 us -> 0 us
  starting transfers between devices: 36.8 us -> 32 us
  local copies, waits for them, and re-layouts: 7.54 us -> 11.4 us
  between operations: 3.36 us -> 0.85 us
  waiting for transfers between devices: 36.3 us -> 35 us
    all_to_all x4, waiting for transfers between devices: 22.1 us -> 11.6 us  [over_shard(): lax.all_to_all(value, 'shard', split_axis=0, concat_axis=0, tiled=True)]
    ppermute x16 -> x18, waiting for transfers between devices: 14.2 us -> 23.4 us  [flip(): return lax.ppermute(value, 'tensor', [(i, i ^ bits) for i in range(size)])]
    unnamed x31 -> x57, local copies, waits for them, and re-layouts: 4.08 us -> 11.4 us
    convert_element_type x2 -> x0, other arithmetic: 3.91 us -> none  [grafted(): return (scale * done).astype(bf16).reshape(owners, -1, done.shape[1])]
    all_to_all x4, starting transfers between devices: 26.9 us -> 23.1 us  [over_shard(): lax.all_to_all(value, 'shard', split_axis=0, concat_axis=0, tiled=True)]
    pallas_call x2, Pallas kernels: 5.68 us -> 2.19 us  [shampoo_part(): pl.pallas_call(functools.partial(shampoo_kernel, rows, cols), out_shape=(...]
    slice x4 -> x0, local copies, waits for them, and re-layouts: 3.47 us -> none  [grafted(): scale = jnp.sqrt(adam[0, 0] / (norm[0, 0] + graft_eps))]
    pallas_call x2, Pallas kernels: 6.1 us -> 4.14 us  [stats_part(): pl.pallas_call(functools.partial(stats_kernel, rows, cols, len(stats) ==...]
  transfers between devices with their start and end apart: 20 -> 22, of which waited for: 9 -> 10; matrix products, arithmetic and copies ran while one was open for 9% -> 1% of each run, Pallas kernels for 15% -> 12%
where the time goes in v3:
time: 95.1 us; the launch traced here: 93.8 us
  waiting for transfers between devices  35 us (37%)
  starting transfers between devices  32 us (34%)
  Pallas kernels  14.6 us (15%)
  local copies, waits for them, and re-layouts  11.4 us (12%)
    ppermute x18, waiting for transfers between devices, flip(): return lax.ppermute(value, 'tensor', [(i, i ^ bits) for i in range(size)])  23.4 us
    all_to_all x4, starting transfers between devices, over_shard(): lax.all_to_all(value, 'shard', split_axis=0, concat_axis=0, tiled=True)  23.1 us
    all_to_all x4, waiting for transfers between devices, over_shard(): lax.all_to_all(value, 'shard', split_axis=0, concat_axis=0, tiled=True)  11.6 us
    unnamed x57, local copies, waits for them, and re-layouts  11.4 us
    ppermute x18, starting transfers between devices, flip(): return lax.ppermute(value, 'tensor', [(i, i ^ bits) for i in range(size)])  8.82 us
    pallas_call x2, Pallas kernels, stats_part(): pl.pallas_call(functools.partial(stats_kernel, rows, cols, len(stats) ==...  4.14 us
    pallas_call x2, Pallas kernels, adam_part(): pl.pallas_call(adam_kernel, out_shape=(packed, jax.ShapeDtypeStruct(momen...  3.82 us
    pallas_call x2, Pallas kernels, weight_part(): pl.pallas_call(weight_kernel, out_shape=jax.ShapeDtypeStruct(weight.shape...  2.66 us
  transfers between devices with their start and end apart: 22, of which 10 were waited for; matrix products, arithmetic and copies ran while one was open for 1% of the time, Pallas kernels for 12%

profile of v3, /device:TPU:0, one launch (start us, length us, event | category | flops | bytes accessed | tf_op | source)
XLA Modules:
  0.0 93.8 jit_solution(5839826382809748405)
XLA Ops:
  4.4 2.0 %shard_map.232 = (bf16[8,96,256]{2,1,0:T(8,128)(2,1)}, f32[4,96,192]{2,1,0:T(8,128)}, f32[4,96,192]{2,1,0:T(8,128)}) custom-call(s32[4]{0:T(128)S(1)} %copy-done.13, f32[2,4,96,192]{3,2,1,0:T(8,128)S(1)} %copy-done.1, f32[4,96,192]{2,1,0:T(8,128)S(1)} %copy-done.7, f32[4,96,192]{2,1,0:T(8,128)S(1)} %copy-done.8), custom_call_target="tpu_custom_call" | custom-call | flops 1474560 | bytes 2359296 | tf_op jit(solution)/shard_map/pallas_call | solution.py:75
  6.5 7.3 %all-to-all-start = ((bf16[8,96,256]{2,1,0:T(8,128)(2,1)}), bf16[8,96,256]{2,1,0:T(8,128)(2,1)S(1)}, u32[]{:S(2)}, u32[]{:S(2)}) async-start(bf16[8,96,256]{2,1,0:T(8,128)(2,1)} %get-tuple-element.26), calls=%async_computation | async-start | bytes 786432 | tf_op jit(solution)/shard_map/all_to_all | solution.py:264
  13.7 1.6 %collective-permute-start.1 = (bf16[192,768]{1,0:T(8,128)(2,1)S(1)}, bf16[192,768]{1,0:T(8,128)(2,1)S(1)}, u32[]{:S(2)}, u32[]{:S(2)}) collective-permute-start(bf16[192,768]{1,0:T(8,128)(2,1)S(1)} %bitcast.4), channel_id=1, source_target_pairs={{0,2},{1,3},{2,0},{3,1},{4,6},{5,7},{6,4},{7,5},{8,10},{9,11},{10,... | collective-permute-start | bytes 884744 | tf_op jit(solution)/shard_map/ppermute | solution.py:241
  15.8 7.9 %collective-permute-done.1.refs_2_ = bf16[192,768]{1,0:T(8,128)(2,1)S(1)} collective-permute-done((bf16[192,768]{1,0:T(8,128)(2,1)S(1)}, bf16[192,768]{1,0:T(8,128)(2,1)S(1)}, u32[]{:S(2)}, u32[]{:S(2)}) %collective-permute-start.1) | collective-permute-done | bytes 294944 | tf_op jit(solution)/shard_map/ppermute | solution.py:241
  23.8 1.8 %shard_map.233 = (bf16[8,104,256]{2,1,0:T(8,128)(2,1)}, f32[4,96,256]{2,1,0:T(8,128)}, f32[4,96,256]{2,1,0:T(8,128)}) custom-call(s32[4]{0:T(128)S(1)} %copy-done.15, f32[2,4,96,256]{3,2,1,0:T(8,128)S(1)} %copy-done.2, f32[4,96,256]{2,1,0:T(8,128)S(1)} %copy-done.9, f32[4,96,256]{2,1,0:T(8,128)S(1)} %copy-done.10), custom_call_target="tpu_custom_call" | custom-call | flops 1966080 | bytes 3145728 | tf_op jit(solution)/shard_map/pallas_call | solution.py:75
  26.3 2.4 %collective-permute-done.3.refs_2_ = bf16[192,768]{1,0:T(8,128)(2,1)} collective-permute-done((bf16[192,768]{1,0:T(8,128)(2,1)}, bf16[192,768]{1,0:T(8,128)(2,1)}, u32[]{:S(2)}, u32[]{:S(2)}) %collective-permute-start.3) | collective-permute-done | bytes 294944 | tf_op jit(solution)/shard_map/ppermute | solution.py:241
  29.4 1.5 %collective-permute-start.5 = (bf16[8,96,256]{2,1,0:T(8,128)(2,1)S(1)}, bf16[8,96,256]{2,1,0:T(8,128)(2,1)S(1)}, u32[]{:S(2)}, u32[]{:S(2)}) collective-permute-start(bf16[8,96,256]{2,1,0:T(8,128)(2,1)S(1)} %all-to-all-done.refs_4_.refs_0_), channel_id=1, source_target_pairs={{0,2},{1,3},{2,0},{3,1},{4,6},{5,7},{6,4},{7,5},{8,10},{9,11},{10,... | collective-permute-start | bytes 1179656 | tf_op jit(solution)/shard_map/ppermute | solution.py:241
  30.9 5.7 %all-to-all-start.2 = ((bf16[8,104,256]{2,1,0:T(8,128)(2,1)}), bf16[8,104,256]{2,1,0:T(8,128)(2,1)S(1)}, u32[]{:S(2)}, u32[]{:S(2)}) async-start(bf16[8,104,256]{2,1,0:T(8,128)(2,1)} %get-tuple-element.27), calls=%async_computation.2 | async-start | bytes 851968 | tf_op jit(solution)/shard_map/all_to_all | solution.py:264
  36.6 2.5 %collective-permute-done.5.refs_6_.refs_2_ = bf16[8,96,256]{2,1,0:T(8,128)(2,1)S(1)} collective-permute-done((bf16[8,96,256]{2,1,0:T(8,128)(2,1)S(1)}, bf16[8,96,256]{2,1,0:T(8,128)(2,1)S(1)}, u32[]{:S(2)}, u32[]{:S(2)}) %collective-permute-start.5) | collective-permute-done | bytes 393248 | tf_op jit(solution)/shard_map/ppermute | solution.py:241
  39.6 1.1 %copy.26.refs_8_ = bf16[1,768,192]{2,1,0:T(8,128)(2,1)S(1)} copy(bf16[1,768,192]{1,2,0:T(8,128)(2,1)} %param.27) | data formatting | bytes 589824 | tf_op args[10]
  45.0 2.3 %all-to-all-done.2.refs_4_.refs_0_ = bf16[8,104,256]{2,1,0:T(8,128)(2,1)S(1)} async-done(((bf16[8,104,256]{2,1,0:T(8,128)(2,1)}), bf16[8,104,256]{2,1,0:T(8,128)(2,1)S(1)}, u32[]{:S(2)}, u32[]{:S(2)}) %all-to-all-start.2) | async-done | bytes 426016 | tf_op jit(solution)/shard_map/all_to_all | solution.py:264
  47.8 1.5 %collective-permute-start.8 = (f32[8,128]{1,0:T(8,128)S(1)}, f32[8,128]{1,0:T(8,128)S(1)}, u32[]{:S(2)}, u32[]{:S(2)}) collective-permute-start(f32[8,128]{1,0:T(8,128)S(1)} %get-tuple-element.31.refs_0_), channel_id=1, source_target_pairs={{0,2},{1,3},{2,0},{3,1},{4,6},{5,7},{6,4},{7,5},{8,10},{9,11},{10,... | collective-permute-start | bytes 12296 | tf_op jit(solution)/shard_map/ppermute | solution.py:241
  49.9 7.1 %collective-permute-done.8.refs_2_ = f32[8,128]{1,0:T(8,128)S(1)} collective-permute-done((f32[8,128]{1,0:T(8,128)S(1)}, f32[8,128]{1,0:T(8,128)S(1)}, u32[]{:S(2)}, u32[]{:S(2)}) %collective-permute-start.8) | collective-permute-done | bytes 4128 | tf_op jit(solution)/shard_map/ppermute | solution.py:241
  58.0 6.6 %all-to-all-start.1 = ((bf16[8,96,192]{2,1,0:T(8,128)(2,1)}), bf16[8,96,192]{2,1,0:T(8,128)(2,1)S(1)}, u32[]{:S(2)}, u32[]{:S(2)}) async-start(bf16[8,96,192]{2,1,0:T(8,128)(2,1)} %bitcast.2), calls=%async_computation.1 | async-start | bytes 786432 | tf_op jit(solution)/shard_map/all_to_all | solution.py:264
  64.7 1.6 %shard_map.237 = (f32[768,256]{1,0:T(8,128)S(1)}, f32[8,128]{1,0:T(8,128)S(1)}, f32[8,128]{1,0:T(8,128)S(1)}) custom-call(s32[4]{0:T(128)S(1)} %copy-done.15, bf16[192,768]{1,0:T(8,128)(2,1)} %bitcast.1.refs_0_, bf16[192,768]{1,0:T(8,128)(2,1)} %collective-permute-done.10.refs_1_, bf16[192,768]{1,0:T(8,128)(2,1)} %collective-permute-done.3.refs_2_, ...), custom_call_target="tpu_custom_call" | custom-call | flops 1610612736 | bytes 3932160 | tf_op jit(solution)/shard_map/pallas_call | solution.py:146
  66.5 1.5 %collective-permute-start.16 = (f32[8,128]{1,0:T(8,128)S(1)}, f32[8,128]{1,0:T(8,128)S(1)}, u32[]{:S(2)}, u32[]{:S(2)}) collective-permute-start(f32[8,128]{1,0:T(8,128)S(1)} %get-tuple-element.38.refs_0_), channel_id=1, source_target_pairs={{0,2},{1,3},{2,0},{3,1},{4,6},{5,7},{6,4},{7,5},{8,10},{9,11},{10,... | collective-permute-start | bytes 12296 | tf_op jit(solution)/shard_map/ppermute | solution.py:241
  68.2 1.9 %collective-permute-done.16.refs_2_ = f32[8,128]{1,0:T(8,128)S(1)} collective-permute-done((f32[8,128]{1,0:T(8,128)S(1)}, f32[8,128]{1,0:T(8,128)S(1)}, u32[]{:S(2)}, u32[]{:S(2)}) %collective-permute-start.16) | collective-permute-done | bytes 4128 | tf_op jit(solution)/shard_map/ppermute | solution.py:241
  71.9 5.0 %all-to-all-done.1.back = bf16[8,96,192]{2,1,0:T(8,128)(2,1)S(1)} async-done(((bf16[8,96,192]{2,1,0:T(8,128)(2,1)}), bf16[8,96,192]{2,1,0:T(8,128)(2,1)S(1)}, u32[]{:S(2)}, u32[]{:S(2)}) %all-to-all-start.1) | async-done | bytes 294944 | tf_op jit(solution)/shard_map/all_to_all | solution.py:264
  76.9 3.6 %all-to-all-start.3 = ((bf16[8,96,256]{2,1,0:T(8,128)(2,1)}), bf16[8,96,256]{2,1,0:T(8,128)(2,1)S(1)}, u32[]{:S(2)}, u32[]{:S(2)}) async-start(bf16[8,96,256]{2,1,0:T(8,128)(2,1)} %bitcast.3), calls=%async_computation.3 | async-start | bytes 786432 | tf_op jit(solution)/shard_map/all_to_all | solution.py:264
  82.6 1.7 %shard_map.240 = f32[1,2,192,768]{3,2,1,0:T(8,128)} custom-call(s32[4]{0:T(128)S(1)} %copy-done.14, bf16[8,96,256]{2,1,0:T(8,128)(2,1)S(1)} %all-to-all-done.refs_4_.refs_0_, bf16[8,96,256]{2,1,0:T(8,128)(2,1)S(1)} %copy-done.4, bf16[8,96,256]{2,1,0:T(8,128)(2,1)S(1)} %collective-permute-done.5.refs_6_.refs_2_, bf16[8,96,256]{2,1,0:T(8,128)(2,1)S(1)} %copy-done.6, ...), custom_call_target="tpu_custom_call" | custom-call | flops 452984832 | bytes 3538944 | tf_op jit(solution)/shard_map/pallas_call | solution.py:203
  84.2 1.3 %shard_map.236 = f32[4,96,192]{2,1,0:T(8,128)} custom-call(s32[4]{0:T(128)S(1)} %copy-done.14, f32[4,96,192]{2,1,0:T(8,128)S(1)} %copy-done.11, bf16[8,96,192]{2,1,0:T(8,128)(2,1)S(1)} %all-to-all-done.1.back), custom_call_target="tpu_custom_call" | custom-call | flops 147456 | bytes 884736 | tf_op jit(solution)/shard_map/pallas_call | solution.py:227
  85.6 2.5 %shard_map.241 = (f32[1,192,768]{2,1,0:T(8,128)}, f32[1,256,1024]{2,1,0:T(8,128)}) custom-call(s32[4]{0:T(128)S(1)} %copy-done.15, bf16[8,104,256]{2,1,0:T(8,128)(2,1)S(1)} %all-to-all-done.2.refs_4_.refs_0_, bf16[8,104,256]{2,1,0:T(8,128)(2,1)} %collective-permute-done.12.refs_5_.refs_1_, bf16[8,104,256]{2,1,0:T(8,128)(2,1)S(1)} %copy-done.20, ...), custom_call_target="tpu_custom_call" | custom-call | flops 1073741824 | bytes 5373952 | tf_op jit(solution)/shard_map/pallas_call | solution.py:203
  88.1 4.4 %all-to-all-done.3.back = bf16[8,96,256]{2,1,0:T(8,128)(2,1)S(1)} async-done(((bf16[8,96,256]{2,1,0:T(8,128)(2,1)}), bf16[8,96,256]{2,1,0:T(8,128)(2,1)S(1)}, u32[]{:S(2)}, u32[]{:S(2)}) %all-to-all-start.3) | async-done | bytes 393248 | tf_op jit(solution)/shard_map/all_to_all | solution.py:264
  92.4 1.3 %shard_map.239 = f32[4,96,256]{2,1,0:T(8,128)} custom-call(s32[4]{0:T(128)S(1)} %copy-done.15, f32[4,96,256]{2,1,0:T(8,128)S(1)} %copy-done.12, bf16[8,96,256]{2,1,0:T(8,128)(2,1)S(1)} %all-to-all-done.3.back), custom_call_target="tpu_custom_call" | custom-call | flops 196608 | bytes 1179648 | tf_op jit(solution)/shard_map/pallas_call | solution.py:227
  (87 shorter events, 16.8 us)
Async XLA Ops:
  6.5 22.9 %all-to-all-start = ((bf16[8,96,256]{2,1,0:T(8,128)(2,1)}), bf16[8,96,256]{2,1,0:T(8,128)(2,1)S(1)}, u32[]{:S(2)}, u32[]{:S(2)}) async-start(bf16[8,96,256]{2,1,0:T(8,128)(2,1)} %get-tuple-element.26), calls=%async_computation | async-start | bytes 786432 | tf_op jit(solution)/shard_map/all_to_all | solution.py:264
  13.7 10.0 %collective-permute-start.1 = (bf16[192,768]{1,0:T(8,128)(2,1)S(1)}, bf16[192,768]{1,0:T(8,128)(2,1)S(1)}, u32[]{:S(2)}, u32[]{:S(2)}) collective-permute-start(bf16[192,768]{1,0:T(8,128)(2,1)S(1)} %bitcast.4), channel_id=1, source_target_pairs={{0,2},{1,3},{2,0},{3,1},{4,6},{5,7},{6,4},{7,5},{8,10},{9,11},{10,... | collective-permute-start | bytes 884744 | tf_op jit(solution)/shard_map/ppermute | solution.py:241
  15.3 10.3 %collective-permute-start = (bf16[192,768]{1,0:T(8,128)(2,1)S(1)}, bf16[192,768]{1,0:T(8,128)(2,1)S(1)}, u32[]{:S(2)}, u32[]{:S(2)}) collective-permute-start(bf16[192,768]{1,0:T(8,128)(2,1)S(1)} %bitcast.5), channel_id=1, source_target_pairs={{0,1},{1,0},{2,3},{3,2},{4,5},{5,4},{6,7},{7,6},{8,9},{9,8},{10,11... | collective-permute-start | bytes 884744 | tf_op jit(solution)/shard_map/ppermute | solution.py:241
  15.3 26.0 %copy-start.14 = (s32[4]{0:T(128)S(1)}, s32[4]{0:T(128)}, u32[]{:S(2)}) copy-start(s32[4]{0:T(128)} %owner.14) | copy-start | bytes 52
  15.3 13.4 %collective-permute-start.3 = (bf16[192,768]{1,0:T(8,128)(2,1)}, bf16[192,768]{1,0:T(8,128)(2,1)}, u32[]{:S(2)}, u32[]{:S(2)}) collective-permute-start(bf16[192,768]{1,0:T(8,128)(2,1)} %bitcast.1.refs_0_), channel_id=1, source_target_pairs={{0,2},{1,3},{2,0},{3,1},{4,6},{5,7},{6,4},{7,5},{8,10},{9,11},{10,... | collective-permute-start | bytes 884744 | tf_op jit(solution)/shard_map/ppermute | solution.py:241
  23.7 5.0 %collective-permute-start.2 = (bf16[192,768]{1,0:T(8,128)(2,1)S(1)}, bf16[192,768]{1,0:T(8,128)(2,1)S(1)}, u32[]{:S(2)}, u32[]{:S(2)}) collective-permute-start(bf16[192,768]{1,0:T(8,128)(2,1)S(1)} %collective-permute-done.1.refs_2_), channel_id=1, source_target_pairs={{0,1},{1,0},{2,3},{3,2},{4,5},{5,4},{6,7},{7,6},{8,9},{9,8},{10,11... | collective-permute-start | bytes 884744 | tf_op jit(solution)/shard_map/ppermute | solution.py:241
  29.4 9.7 %collective-permute-start.5 = (bf16[8,96,256]{2,1,0:T(8,128)(2,1)S(1)}, bf16[8,96,256]{2,1,0:T(8,128)(2,1)S(1)}, u32[]{:S(2)}, u32[]{:S(2)}) collective-permute-start(bf16[8,96,256]{2,1,0:T(8,128)(2,1)S(1)} %all-to-all-done.refs_4_.refs_0_), channel_id=1, source_target_pairs={{0,2},{1,3},{2,0},{3,1},{4,6},{5,7},{6,4},{7,5},{8,10},{9,11},{10,... | collective-permute-start | bytes 1179656 | tf_op jit(solution)/shard_map/ppermute | solution.py:241
  30.9 16.3 %all-to-all-start.2 = ((bf16[8,104,256]{2,1,0:T(8,128)(2,1)}), bf16[8,104,256]{2,1,0:T(8,128)(2,1)S(1)}, u32[]{:S(2)}, u32[]{:S(2)}) async-start(bf16[8,104,256]{2,1,0:T(8,128)(2,1)} %get-tuple-element.27), calls=%async_computation.2 | async-start | bytes 851968 | tf_op jit(solution)/shard_map/all_to_all | solution.py:264
  36.6 4.1 %collective-permute-start.4 = (bf16[8,96,256]{2,1,0:T(8,128)(2,1)S(1)}, bf16[8,96,256]{2,1,0:T(8,128)(2,1)S(1)}, u32[]{:S(2)}, u32[]{:S(2)}) collective-permute-start(bf16[8,96,256]{2,1,0:T(8,128)(2,1)S(1)} %all-to-all-done.refs_4_.refs_0_), channel_id=1, source_target_pairs={{0,1},{1,0},{2,3},{3,2},{4,5},{5,4},{6,7},{7,6},{8,9},{9,8},{10,11... | collective-permute-start | bytes 1179656 | tf_op jit(solution)/shard_map/ppermute | solution.py:241
  39.1 2.2 %collective-permute-start.6 = (bf16[8,96,256]{2,1,0:T(8,128)(2,1)S(1)}, bf16[8,96,256]{2,1,0:T(8,128)(2,1)S(1)}, u32[]{:S(2)}, u32[]{:S(2)}) collective-permute-start(bf16[8,96,256]{2,1,0:T(8,128)(2,1)S(1)} %collective-permute-done.5.refs_6_.refs_2_), channel_id=1, source_target_pairs={{0,1},{1,0},{2,3},{3,2},{4,5},{5,4},{6,7},{7,6},{8,9},{9,8},{10,11... | collective-permute-start | bytes 1179656 | tf_op jit(solution)/shard_map/ppermute | solution.py:241
  39.1 5.9 %collective-permute-start.10 = (bf16[192,768]{1,0:T(8,128)(2,1)}, bf16[192,768]{1,0:T(8,128)(2,1)}, u32[]{:S(2)}, u32[]{:S(2)}) collective-permute-start(bf16[192,768]{1,0:T(8,128)(2,1)} %bitcast.1.refs_0_), channel_id=1, source_target_pairs={{0,1},{1,0},{2,3},{3,2},{4,5},{5,4},{6,7},{7,6},{8,9},{9,8},{10,11... | collective-permute-start | bytes 884744 | tf_op jit(solution)/shard_map/ppermute | solution.py:241
  39.6 5.4 %collective-permute-start.11 = (bf16[192,768]{1,0:T(8,128)(2,1)}, bf16[192,768]{1,0:T(8,128)(2,1)}, u32[]{:S(2)}, u32[]{:S(2)}) collective-permute-start(bf16[192,768]{1,0:T(8,128)(2,1)} %collective-permute-done.3.refs_2_), channel_id=1, source_target_pairs={{0,1},{1,0},{2,3},{3,2},{4,5},{5,4},{6,7},{7,6},{8,9},{9,8},{10,11... | collective-permute-start | bytes 884744 | tf_op jit(solution)/shard_map/ppermute | solution.py:241
  45.0 19.7 %copy-start.18 = (bf16[1,1024,256]{2,1,0:T(8,128)(2,1)S(1)}, bf16[1,1024,256]{2,1,0:T(8,128)(2,1)}, u32[]{:S(2)}) copy-start(bf16[1,1024,256]{2,1,0:T(8,128)(2,1)} %refs_8_.2) | copy-start | bytes 1572868
  47.2 10.7 %collective-permute-start.13 = (bf16[8,104,256]{2,1,0:T(8,128)(2,1)S(1)}, bf16[8,104,256]{2,1,0:T(8,128)(2,1)S(1)}, u32[]{:S(2)}, u32[]{:S(2)}) collective-permute-start(bf16[8,104,256]{2,1,0:T(8,128)(2,1)S(1)} %all-to-all-done.2.refs_4_.refs_0_), channel_id=1, source_target_pairs={{0,2},{1,3},{2,0},{3,1},{4,6},{5,7},{6,4},{7,5},{8,10},{9,11},{10,... | collective-permute-start | bytes 1277960 | tf_op jit(solution)/shard_map/ppermute | solution.py:241
  47.8 2.1 %collective-permute-start.7 = (f32[8,128]{1,0:T(8,128)S(1)}, f32[8,128]{1,0:T(8,128)S(1)}, u32[]{:S(2)}, u32[]{:S(2)}) collective-permute-start(f32[8,128]{1,0:T(8,128)S(1)} %get-tuple-element.31.refs_0_), channel_id=1, source_target_pairs={{0,1},{1,0},{2,3},{3,2},{4,5},{5,4},{6,7},{7,6},{8,9},{9,8},{10,11... | collective-permute-start | bytes 12296 | tf_op jit(solution)/shard_map/ppermute | solution.py:241
  47.8 9.3 %collective-permute-start.8 = (f32[8,128]{1,0:T(8,128)S(1)}, f32[8,128]{1,0:T(8,128)S(1)}, u32[]{:S(2)}, u32[]{:S(2)}) collective-permute-start(f32[8,128]{1,0:T(8,128)S(1)} %get-tuple-element.31.refs_0_), channel_id=1, source_target_pairs={{0,2},{1,3},{2,0},{3,1},{4,6},{5,7},{6,4},{7,5},{8,10},{9,11},{10,... | collective-permute-start | bytes 12296 | tf_op jit(solution)/shard_map/ppermute | solution.py:241
  49.3 7.8 %collective-permute-start.9 = (f32[8,128]{1,0:T(8,128)S(1)}, f32[8,128]{1,0:T(8,128)S(1)}, u32[]{:S(2)}, u32[]{:S(2)}) collective-permute-start(f32[8,128]{1,0:T(8,128)S(1)} %get-tuple-element.31.refs_0_), channel_id=1, source_target_pairs={{0,3},{1,2},{2,1},{3,0},{4,7},{5,6},{6,5},{7,4},{8,11},{9,10},{10,... | collective-permute-start | bytes 12296 | tf_op jit(solution)/shard_map/ppermute | solution.py:241
  49.6 15.0 %collective-permute-start.12 = (bf16[8,104,256]{2,1,0:T(8,128)(2,1)S(1)}, bf16[8,104,256]{2,1,0:T(8,128)(2,1)}, u32[]{:S(2)}, u32[]{:S(2)}) collective-permute-start(bf16[8,104,256]{2,1,0:T(8,128)(2,1)S(1)} %all-to-all-done.2.refs_4_.refs_0_), channel_id=1, source_target_pairs={{0,1},{1,0},{2,3},{3,2},{4,5},{5,4},{6,7},{7,6},{8,9},{9,8},{10,11... | collective-permute-start | bytes 1277960 | tf_op jit(solution)/shard_map/ppermute | solution.py:241
  57.9 6.7 %collective-permute-start.14 = (bf16[8,104,256]{2,1,0:T(8,128)(2,1)S(1)}, bf16[8,104,256]{2,1,0:T(8,128)(2,1)}, u32[]{:S(2)}, u32[]{:S(2)}) collective-permute-start(bf16[8,104,256]{2,1,0:T(8,128)(2,1)S(1)} %collective-permute-done.13.refs_6_.refs_2_), channel_id=1, source_target_pairs={{0,1},{1,0},{2,3},{3,2},{4,5},{5,4},{6,7},{7,6},{8,9},{9,8},{10,11... | collective-permute-start | bytes 1277960 | tf_op jit(solution)/shard_map/ppermute | solution.py:241
  58.0 18.9 %all-to-all-start.1 = ((bf16[8,96,192]{2,1,0:T(8,128)(2,1)}), bf16[8,96,192]{2,1,0:T(8,128)(2,1)S(1)}, u32[]{:S(2)}, u32[]{:S(2)}) async-start(bf16[8,96,192]{2,1,0:T(8,128)(2,1)} %bitcast.2), calls=%async_computation.1 | async-start | bytes 786432 | tf_op jit(solution)/shard_map/all_to_all | solution.py:264
  66.3 1.9 %collective-permute-start.15 = (f32[8,128]{1,0:T(8,128)S(1)}, f32[8,128]{1,0:T(8,128)S(1)}, u32[]{:S(2)}, u32[]{:S(2)}) collective-permute-start(f32[8,128]{1,0:T(8,128)S(1)} %get-tuple-element.38.refs_0_), channel_id=1, source_target_pairs={{0,1},{1,0},{2,3},{3,2},{4,5},{5,4},{6,7},{7,6},{8,9},{9,8},{10,11... | collective-permute-start | bytes 12296 | tf_op jit(solution)/shard_map/ppermute | solution.py:241
  66.5 3.6 %collective-permute-start.16 = (f32[8,128]{1,0:T(8,128)S(1)}, f32[8,128]{1,0:T(8,128)S(1)}, u32[]{:S(2)}, u32[]{:S(2)}) collective-permute-start(f32[8,128]{1,0:T(8,128)S(1)} %get-tuple-element.38.refs_0_), channel_id=1, source_target_pairs={{0,2},{1,3},{2,0},{3,1},{4,6},{5,7},{6,4},{7,5},{8,10},{9,11},{10,... | collective-permute-start | bytes 12296 | tf_op jit(solution)/shard_map/ppermute | solution.py:241
  68.0 3.0 %collective-permute-start.17 = (f32[8,128]{1,0:T(8,128)S(1)}, f32[8,128]{1,0:T(8,128)S(1)}, u32[]{:S(2)}, u32[]{:S(2)}) collective-permute-start(f32[8,128]{1,0:T(8,128)S(1)} %get-tuple-element.38.refs_0_), channel_id=1, source_target_pairs={{0,3},{1,2},{2,1},{3,0},{4,7},{5,6},{6,5},{7,4},{8,11},{9,10},{10,... | collective-permute-start | bytes 12296 | tf_op jit(solution)/shard_map/ppermute | solution.py:241
  76.9 15.5 %all-to-all-start.3 = ((bf16[8,96,256]{2,1,0:T(8,128)(2,1)}), bf16[8,96,256]{2,1,0:T(8,128)(2,1)S(1)}, u32[]{:S(2)}, u32[]{:S(2)}) async-start(bf16[8,96,256]{2,1,0:T(8,128)(2,1)} %bitcast.3), calls=%async_computation.3 | async-start | bytes 786432 | tf_op jit(solution)/shard_map/all_to_all | solution.py:264
  (26 other events, 145.6 us)

commit v4 on v3

--- a/solution.py
+++ b/solution.py
@@ -18,6 +18,7 @@
 f32 = jnp.float32
 LANES = 128
 VMEM = pl.BlockSpec(memory_space=pltpu.VMEM)
+BRIEF = pl.CostEstimate(flops=1024, bytes_accessed=1024, transcendentals=0)
 LIMIT = pltpu.CompilerParams(vmem_limit_bytes=16 << 20)
 SMEM = pl.BlockSpec(memory_space=pltpu.SMEM)
 
@@ -69,7 +70,7 @@
     lax.fori_loop(0, moment.shape[0], unit, 0, unroll=moment.shape[0] <= 4)
 
 
-def adam_part(owner, grads, moment, second, owners):
+def adam_part(owner, grads, moment, second, owners, params):
     rows, cols = moment.shape[1:]
     packed = jax.ShapeDtypeStruct((owners, *packed_shape(rows, cols)), bf16)
     return pl.pallas_call(
@@ -81,7 +82,7 @@
         ),
         in_specs=[SMEM, VMEM, VMEM, VMEM],
         out_specs=(VMEM, VMEM, VMEM),
-        compiler_params=LIMIT,
+        compiler_params=params,
         cost_estimate=pl.CostEstimate(
             flops=20 * moment.size, bytes_accessed=32 * moment.size, transcendentals=moment.size
         ),
@@ -150,11 +151,7 @@
         out_specs=(VMEM, VMEM, VMEM),
         scratch_shapes=[pltpu.VMEM((depth, depth), bf16), pltpu.VMEM((tensor, depth, cols), bf16)],
         compiler_params=LIMIT,
-        cost_estimate=pl.CostEstimate(
-            flops=2 * depth * cols * tensor * (depth + cols),
-            bytes_accessed=2 * depth * depth + 2 * depth * cols * tensor + 6 * depth * cols,
-            transcendentals=0,
-        ),
+        cost_estimate=BRIEF,
     )(owner, *left, *grad, root)
 
 
@@ -310,24 +307,22 @@
     owners = lax.axis_size("shard")
     rows = att_weight.shape[1]
     att_packed, att_moment_out, att_second_out = adam_part(
-        att_owner, att_grads, att_moment, att_second, owners
+        att_owner, att_grads, att_moment, att_second, owners, None
     )
     glu_packed, glu_moment_out, glu_second_out = adam_part(
-        glu_owner, glu_grads, glu_moment, glu_second, owners
+        glu_owner, glu_grads, glu_moment, glu_second, owners, LIMIT
     )
     att_root, att_root_far = spread_first(att_left_root[0])
-    glu_root, glu_root_far = spread_first(glu_left_root[0])
-    att_left = spread_rest(att_root, att_root_far)
-    glu_left = spread_rest(glu_root, glu_root_far)
-    att_near, att_far = spread_first(
-        after(over_shard(att_packed), *att_left[1:], glu_root_far, glu_packed)
-    )
+    att_near, att_far = spread_first(after(over_shard(att_packed), att_root_far, glu_packed))
+    att_left = spread_rest(*lax.optimization_barrier((att_root, att_root_far, att_near))[:2])
+    glu_root, glu_root_far = spread_first(after(glu_left_root[0], att_far))
     att_grad = spread_rest(att_near, att_far)
     att_done, att_norm, att_adam = shampoo_part(att_owner, att_left, att_grad, att_right_root, rows)
-    glu_near, glu_far = spread_first(after(over_shard(glu_packed), att_done, *glu_left[1:]))
     att_send = grafted(att_done, att_norm, att_adam, owners)
-    glu_grad = spread_rest(glu_near, after(glu_far, att_send))
+    glu_near, glu_far = spread_first(after(over_shard(glu_packed), att_send, glu_root_far))
+    glu_left = spread_rest(*lax.optimization_barrier((glu_root, glu_root_far, glu_near))[:2])
     att_back = over_shard(att_send)
+    glu_grad = spread_rest(glu_near, glu_far)
     glu_done, glu_norm, glu_adam = shampoo_part(glu_owner, glu_left, glu_grad, glu_right_root, rows)
     glu_back = over_shard(grafted(glu_done, glu_norm, glu_adam, owners))
     (att_stats_out,) = stats_part(att_owner, att_grad, (att_stats,), rows, att_weight.shape[2])

time: 95.1 us -> 85 us (0.89)
  waiting for transfers between devices: 35 us -> 25.9 us
  local copies, waits for them, and re-layouts: 11.4 us -> 2.46 us
  Pallas kernels: 14.6 us -> 22.1 us
    unnamed x57 -> x33, local copies, waits for them, and re-layouts: 11.4 us -> 2.46 us
    all_to_all x4, waiting for transfers between devices: 11.6 us -> 6.25 us  [over_shard(): lax.all_to_all(value, 'shard', split_axis=0, concat_axis=0, tiled=True)]
    pallas_call x2, Pallas kernels: 2.19 us -> 6.87 us  [shampoo_part(): pl.pallas_call(functools.partial(shampoo_kernel, rows, cols), out_shape=(...]
    ppermute x18, waiting for transfers between devices: 23.4 us -> 19.7 us  [flip(): return lax.ppermute(value, 'tensor', [(i, i ^ bits) for i in range(size)])]
    pallas_call x2, Pallas kernels: 4.14 us -> 6.21 us  [stats_part(): pl.pallas_call(functools.partial(stats_kernel, rows, cols, len(stats) ==...]
    ppermute x18, starting transfers between devices: 8.82 us -> 10.6 us  [flip(): return lax.ppermute(value, 'tensor', [(i, i ^ bits) for i in range(size)])]
    all_to_all x4, starting transfers between devices: 23.1 us -> 21.6 us  [over_shard(): lax.all_to_all(value, 'shard', split_axis=0, concat_axis=0, tiled=True)]
  transfers between devices with their start and end apart: 22 -> 22, of which waited for: 10 -> 10; matrix products, arithmetic and copies ran while one was open for 1% -> 1% of each run, Pallas kernels for 12% -> 22%
where the time goes in v4:
time: 85 us; the launch traced here: 83.6 us
  starting transfers between devices  32.2 us (38%)
  waiting for transfers between devices  25.9 us (30%)
  Pallas kernels  22.1 us (26%)
  local copies, waits for them, and re-layouts  2.46 us (3%)
  between operations  0.87 us (1%)
    all_to_all x4, starting transfers between devices, over_shard(): lax.all_to_all(value, 'shard', split_axis=0, concat_axis=0, tiled=True)  21.6 us
    ppermute x18, waiting for transfers between devices, flip(): return lax.ppermute(value, 'tensor', [(i, i ^ bits) for i in range(size)])  19.7 us
    ppermute x18, starting transfers between devices, flip(): return lax.ppermute(value, 'tensor', [(i, i ^ bits) for i in range(size)])  10.6 us
    pallas_call x2, Pallas kernels, shampoo_part(): pl.pallas_call(functools.partial(shampoo_kernel, rows, cols), out_shape=(...  6.87 us
    all_to_all x4, waiting for transfers between devices, over_shard(): lax.all_to_all(value, 'shard', split_axis=0, concat_axis=0, tiled=True)  6.25 us
    pallas_call x2, Pallas kernels, stats_part(): pl.pallas_call(functools.partial(stats_kernel, rows, cols, len(stats) ==...  6.21 us
    pallas_call x2, Pallas kernels, adam_part(): pl.pallas_call(adam_kernel, out_shape=(packed, jax.ShapeDtypeStruct(momen...  4.59 us
    pallas_call x2, Pallas kernels, weight_part(): pl.pallas_call(weight_kernel, out_shape=jax.ShapeDtypeStruct(weight.shape...  2.66 us
  transfers between devices with their start and end apart: 22, of which 10 were waited for; matrix products, arithmetic and copies ran while one was open for 1% of the time, Pallas kernels for 22%

profile of v4, /device:TPU:0, one launch (start us, length us, event | category | flops | bytes accessed | tf_op | source)
XLA Modules:
  0.0 83.6 jit_solution(4443700492663961948)
XLA Ops:
  0.7 2.8 %shard_map.232 = (bf16[8,96,256]{2,1,0:T(8,128)(2,1)}, f32[4,96,192]{2,1,0:T(8,128)}, f32[4,96,192]{2,1,0:T(8,128)}) custom-call(s32[4]{0:T(128)} %owner.14, f32[2,4,96,192]{3,2,1,0:T(8,128)} %grads.2, f32[4,96,192]{2,1,0:T(8,128)} %moment.2, f32[4,96,192]{2,1,0:T(8,128)} %second.2), custom_call_target="tpu_custom_call" | custom-call | flops 1474560 | bytes 2359296 | tf_op jit(solution)/shard_map/pallas_call | solution.py:76
  3.5 7.3 %all-to-all-start = ((bf16[8,96,256]{2,1,0:T(8,128)(2,1)}), bf16[8,96,256]{2,1,0:T(8,128)(2,1)S(1)}, u32[]{:S(2)}, u32[]{:S(2)}) async-start(bf16[8,96,256]{2,1,0:T(8,128)(2,1)} %get-tuple-element.30), calls=%async_computation | async-start | bytes 786432 | tf_op jit(solution)/shard_map/all_to_all | solution.py:261
  10.7 1.6 %collective-permute-start = (bf16[192,768]{1,0:T(8,128)(2,1)S(1)}, bf16[192,768]{1,0:T(8,128)(2,1)S(1)}, u32[]{:S(2)}, u32[]{:S(2)}) collective-permute-start(bf16[192,768]{1,0:T(8,128)(2,1)S(1)} %bitcast.4), channel_id=1, source_target_pairs={{0,2},{1,3},{2,0},{3,1},{4,6},{5,7},{6,4},{7,5},{8,10},{9,11},{10,... | collective-permute-start | bytes 884744 | tf_op jit(solution)/shard_map/ppermute | solution.py:238
  12.3 1.8 %shard_map.233 = (bf16[8,104,256]{2,1,0:T(8,128)(2,1)}, f32[4,96,256]{2,1,0:T(8,128)}, f32[4,96,256]{2,1,0:T(8,128)}) custom-call(s32[4]{0:T(128)S(1)} %copy-done.13, f32[2,4,96,256]{3,2,1,0:T(8,128)S(1)} %copy-done.1, f32[4,96,256]{2,1,0:T(8,128)S(1)} %copy-done.7, f32[4,96,256]{2,1,0:T(8,128)S(1)} %copy-done.8), custom_call_target="tpu_custom_call" | custom-call | flops 1966080 | bytes 3145728 | tf_op jit(solution)/shard_map/pallas_call | solution.py:76
  14.1 5.1 %collective-permute-done.refs_2_ = bf16[192,768]{1,0:T(8,128)(2,1)S(1)} collective-permute-done((bf16[192,768]{1,0:T(8,128)(2,1)S(1)}, bf16[192,768]{1,0:T(8,128)(2,1)S(1)}, u32[]{:S(2)}, u32[]{:S(2)}) %collective-permute-start) | collective-permute-done | bytes 294944 | tf_op jit(solution)/shard_map/ppermute | solution.py:238
  19.3 3.1 %all-to-all-done.refs_4_.refs_0_ = bf16[8,96,256]{2,1,0:T(8,128)(2,1)S(1)} async-done(((bf16[8,96,256]{2,1,0:T(8,128)(2,1)}), bf16[8,96,256]{2,1,0:T(8,128)(2,1)S(1)}, u32[]{:S(2)}, u32[]{:S(2)}) %all-to-all-start) | async-done | bytes 393248 | tf_op jit(solution)/shard_map/all_to_all | solution.py:261
  22.4 1.5 %collective-permute-start.4 = (bf16[8,96,256]{2,1,0:T(8,128)(2,1)S(1)}, bf16[8,96,256]{2,1,0:T(8,128)(2,1)S(1)}, u32[]{:S(2)}, u32[]{:S(2)}) collective-permute-start(bf16[8,96,256]{2,1,0:T(8,128)(2,1)S(1)} %all-to-all-done.refs_4_.refs_0_), channel_id=1, source_target_pairs={{0,2},{1,3},{2,0},{3,1},{4,6},{5,7},{6,4},{7,5},{8,10},{9,11},{10,... | collective-permute-start | bytes 1179656 | tf_op jit(solution)/shard_map/ppermute | solution.py:238
  23.9 3.6 %all-to-all-start.2 = ((bf16[8,104,256]{2,1,0:T(8,128)(2,1)}), bf16[8,104,256]{2,1,0:T(8,128)(2,1)S(1)}, u32[]{:S(2)}, u32[]{:S(2)}) async-start(bf16[8,104,256]{2,1,0:T(8,128)(2,1)} %get-tuple-element.31), calls=%async_computation.2 | async-start | bytes 851968 | tf_op jit(solution)/shard_map/all_to_all | solution.py:261
  27.6 2.8 %collective-permute-done.4.refs_6_.refs_2_ = bf16[8,96,256]{2,1,0:T(8,128)(2,1)S(1)} collective-permute-done((bf16[8,96,256]{2,1,0:T(8,128)(2,1)S(1)}, bf16[8,96,256]{2,1,0:T(8,128)(2,1)S(1)}, u32[]{:S(2)}, u32[]{:S(2)}) %collective-permute-start.4) | collective-permute-done | bytes 393248 | tf_op jit(solution)/shard_map/ppermute | solution.py:238
  30.9 1.5 %collective-permute-start.9 = (bf16[192,768]{1,0:T(8,128)(2,1)}, bf16[192,768]{1,0:T(8,128)(2,1)S(1)}, u32[]{:S(2)}, u32[]{:S(2)}) collective-permute-start(bf16[192,768]{1,0:T(8,128)(2,1)} %bitcast.2.refs_0_), channel_id=1, source_target_pairs={{0,2},{1,3},{2,0},{3,1},{4,6},{5,7},{6,4},{7,5},{8,10},{9,11},{10,... | collective-permute-start | bytes 884744 | tf_op jit(solution)/shard_map/ppermute | solution.py:238
  33.6 3.3 %shard_map.234 = (f32[768,192]{1,0:T(8,128)S(1)}, f32[8,128]{1,0:T(8,128)S(1)}, f32[8,128]{1,0:T(8,128)S(1)}) custom-call(s32[4]{0:T(128)S(1)} %copy-done.12, bf16[192,768]{1,0:T(8,128)(2,1)S(1)} %bitcast.6, bf16[192,768]{1,0:T(8,128)(2,1)} %collective-permute-done.1.refs_1_, bf16[192,768]{1,0:T(8,128)(2,1)S(1)} %collective-permute-done.refs_2_, ...), custom_call_target="tpu_custom_call" | custom-call | flops 1024 | bytes 1024 | tf_op jit(solution)/shard_map/pallas_call | solution.py:147
  38.9 2.0 %collective-permute-done.7.refs_2_ = f32[8,128]{1,0:T(8,128)S(1)} collective-permute-done((f32[8,128]{1,0:T(8,128)S(1)}, f32[8,128]{1,0:T(8,128)S(1)}, u32[]{:S(2)}, u32[]{:S(2)}) %collective-permute-start.7) | collective-permute-done | bytes 4128 | tf_op jit(solution)/shard_map/ppermute | solution.py:238
  43.2 6.2 %all-to-all-start.1 = ((bf16[8,96,192]{2,1,0:T(8,128)(2,1)}), bf16[8,96,192]{2,1,0:T(8,128)(2,1)S(1)}, u32[]{:S(2)}, u32[]{:S(2)}) async-start(bf16[8,96,192]{2,1,0:T(8,128)(2,1)} %bitcast.1), calls=%async_computation.1 | async-start | bytes 786432 | tf_op jit(solution)/shard_map/all_to_all | solution.py:261
  49.4 4.6 %collective-permute-done.13.refs_6_.refs_2_ = bf16[8,104,256]{2,1,0:T(8,128)(2,1)} collective-permute-done((bf16[8,104,256]{2,1,0:T(8,128)(2,1)S(1)}, bf16[8,104,256]{2,1,0:T(8,128)(2,1)}, u32[]{:S(2)}, u32[]{:S(2)}) %collective-permute-start.13) | collective-permute-done | bytes 426016 | tf_op jit(solution)/shard_map/ppermute | solution.py:238
  54.6 2.3 %collective-permute-done.10.refs_1_ = bf16[192,768]{1,0:T(8,128)(2,1)S(1)} collective-permute-done((bf16[192,768]{1,0:T(8,128)(2,1)}, bf16[192,768]{1,0:T(8,128)(2,1)S(1)}, u32[]{:S(2)}, u32[]{:S(2)}) %collective-permute-start.10) | collective-permute-done | bytes 294944 | tf_op jit(solution)/shard_map/ppermute | solution.py:238
  57.0 3.5 %shard_map.237 = (f32[768,256]{1,0:T(8,128)S(1)}, f32[8,128]{1,0:T(8,128)S(1)}, f32[8,128]{1,0:T(8,128)S(1)}) custom-call(s32[4]{0:T(128)S(1)} %copy-done.13, bf16[192,768]{1,0:T(8,128)(2,1)} %bitcast.2.refs_0_, bf16[192,768]{1,0:T(8,128)(2,1)S(1)} %collective-permute-done.10.refs_1_, bf16[192,768]{1,0:T(8,128)(2,1)S(1)} %collective-permute-done.9.refs_2_, ...), custom_call_target="tpu_custom_call" | custom-call | flops 1024 | bytes 1024 | tf_op jit(solution)/shard_map/pallas_call | solution.py:147
  62.4 1.9 %collective-permute-done.16.refs_2_ = f32[8,128]{1,0:T(8,128)S(1)} collective-permute-done((f32[8,128]{1,0:T(8,128)S(1)}, f32[8,128]{1,0:T(8,128)S(1)}, u32[]{:S(2)}, u32[]{:S(2)}) %collective-permute-start.16) | collective-permute-done | bytes 4128 | tf_op jit(solution)/shard_map/ppermute | solution.py:238
  65.8 4.5 %all-to-all-start.3 = ((bf16[8,96,256]{2,1,0:T(8,128)(2,1)}), bf16[8,96,256]{2,1,0:T(8,128)(2,1)S(1)}, u32[]{:S(2)}, u32[]{:S(2)}) async-start(bf16[8,96,256]{2,1,0:T(8,128)(2,1)} %bitcast.3), calls=%async_computation.3 | async-start | bytes 786432 | tf_op jit(solution)/shard_map/all_to_all | solution.py:261
  70.3 1.3 %copy-done = f32[1,2,192,768]{3,2,1,0:T(8,128)S(1)} copy-done((f32[1,2,192,768]{3,2,1,0:T(8,128)S(1)}, f32[1,2,192,768]{3,2,1,0:T(8,128)}, u32[]{:S(2)}) %copy-start) | copy-done | bytes 1179672
  71.5 2.7 %shard_map.240 = f32[1,2,192,768]{3,2,1,0:T(8,128)} custom-call(s32[4]{0:T(128)S(1)} %copy-done.12, bf16[8,96,256]{2,1,0:T(8,128)(2,1)S(1)} %all-to-all-done.refs_4_.refs_0_, bf16[8,96,256]{2,1,0:T(8,128)(2,1)S(1)} %collective-permute-done.3.refs_5_.refs_1_, bf16[8,96,256]{2,1,0:T(8,128)(2,1)S(1)} %collective-permute-done.4.refs_6_.refs_2_, ...), custom_call_target="tpu_custom_call" | custom-call | flops 452984832 | bytes 3538944 | tf_op jit(solution)/shard_map/pallas_call | solution.py:200
  74.3 1.3 %shard_map.236 = f32[4,96,192]{2,1,0:T(8,128)} custom-call(s32[4]{0:T(128)S(1)} %copy-done.12, f32[4,96,192]{2,1,0:T(8,128)S(1)} %copy-done.9, bf16[8,96,192]{2,1,0:T(8,128)(2,1)S(1)} %all-to-all-done.1.back), custom_call_target="tpu_custom_call" | custom-call | flops 147456 | bytes 884736 | tf_op jit(solution)/shard_map/pallas_call | solution.py:224
  75.6 3.5 %shard_map.241 = (f32[1,192,768]{2,1,0:T(8,128)}, f32[1,256,1024]{2,1,0:T(8,128)}) custom-call(s32[4]{0:T(128)S(1)} %copy-done.13, bf16[8,104,256]{2,1,0:T(8,128)(2,1)S(1)} %all-to-all-done.2.refs_4_.refs_0_, bf16[8,104,256]{2,1,0:T(8,128)(2,1)S(1)} %copy-done.4, bf16[8,104,256]{2,1,0:T(8,128)(2,1)} %collective-permute-done.13.refs_6_.refs_2_, ...), custom_call_target="tpu_custom_call" | custom-call | flops 1073741824 | bytes 5373952 | tf_op jit(solution)/shard_map/pallas_call | solution.py:200
  79.1 3.1 %all-to-all-done.3.back = bf16[8,96,256]{2,1,0:T(8,128)(2,1)S(1)} async-done(((bf16[8,96,256]{2,1,0:T(8,128)(2,1)}), bf16[8,96,256]{2,1,0:T(8,128)(2,1)S(1)}, u32[]{:S(2)}, u32[]{:S(2)}) %all-to-all-start.3) | async-done | bytes 393248 | tf_op jit(solution)/shard_map/all_to_all | solution.py:261
  82.2 1.3 %shard_map.239 = f32[4,96,256]{2,1,0:T(8,128)} custom-call(s32[4]{0:T(128)S(1)} %copy-done.13, f32[4,96,256]{2,1,0:T(8,128)S(1)} %copy-done.10, bf16[8,96,256]{2,1,0:T(8,128)(2,1)S(1)} %all-to-all-done.3.back), custom_call_target="tpu_custom_call" | custom-call | flops 196608 | bytes 1179648 | tf_op jit(solution)/shard_map/pallas_call | solution.py:224
  (63 shorter events, 9.9 us)
Async XLA Ops:
  3.5 18.9 %all-to-all-start = ((bf16[8,96,256]{2,1,0:T(8,128)(2,1)}), bf16[8,96,256]{2,1,0:T(8,128)(2,1)S(1)}, u32[]{:S(2)}, u32[]{:S(2)}) async-start(bf16[8,96,256]{2,1,0:T(8,128)(2,1)} %get-tuple-element.30), calls=%async_computation | async-start | bytes 786432 | tf_op jit(solution)/shard_map/all_to_all | solution.py:261
  10.7 22.9 %copy-start.12 = (s32[4]{0:T(128)S(1)}, s32[4]{0:T(128)}, u32[]{:S(2)}) copy-start(s32[4]{0:T(128)} %owner.14) | copy-start | bytes 52
  10.7 8.5 %collective-permute-start = (bf16[192,768]{1,0:T(8,128)(2,1)S(1)}, bf16[192,768]{1,0:T(8,128)(2,1)S(1)}, u32[]{:S(2)}, u32[]{:S(2)}) collective-permute-start(bf16[192,768]{1,0:T(8,128)(2,1)S(1)} %bitcast.4), channel_id=1, source_target_pairs={{0,2},{1,3},{2,0},{3,1},{4,6},{5,7},{6,4},{7,5},{8,10},{9,11},{10,... | collective-permute-start | bytes 884744 | tf_op jit(solution)/shard_map/ppermute | solution.py:238
  22.4 8.0 %collective-permute-start.4 = (bf16[8,96,256]{2,1,0:T(8,128)(2,1)S(1)}, bf16[8,96,256]{2,1,0:T(8,128)(2,1)S(1)}, u32[]{:S(2)}, u32[]{:S(2)}) collective-permute-start(bf16[8,96,256]{2,1,0:T(8,128)(2,1)S(1)} %all-to-all-done.refs_4_.refs_0_), channel_id=1, source_target_pairs={{0,2},{1,3},{2,0},{3,1},{4,6},{5,7},{6,4},{7,5},{8,10},{9,11},{10,... | collective-permute-start | bytes 1179656 | tf_op jit(solution)/shard_map/ppermute | solution.py:238
  23.9 18.2 %all-to-all-start.2 = ((bf16[8,104,256]{2,1,0:T(8,128)(2,1)}), bf16[8,104,256]{2,1,0:T(8,128)(2,1)S(1)}, u32[]{:S(2)}, u32[]{:S(2)}) async-start(bf16[8,104,256]{2,1,0:T(8,128)(2,1)} %get-tuple-element.31), calls=%async_computation.2 | async-start | bytes 851968 | tf_op jit(solution)/shard_map/all_to_all | solution.py:261
  27.6 6.1 %collective-permute-start.3 = (bf16[8,96,256]{2,1,0:T(8,128)(2,1)S(1)}, bf16[8,96,256]{2,1,0:T(8,128)(2,1)S(1)}, u32[]{:S(2)}, u32[]{:S(2)}) collective-permute-start(bf16[8,96,256]{2,1,0:T(8,128)(2,1)S(1)} %all-to-all-done.refs_4_.refs_0_), channel_id=1, source_target_pairs={{0,1},{1,0},{2,3},{3,2},{4,5},{5,4},{6,7},{7,6},{8,9},{9,8},{10,11... | collective-permute-start | bytes 1179656 | tf_op jit(solution)/shard_map/ppermute | solution.py:238
  30.4 3.2 %collective-permute-start.5 = (bf16[8,96,256]{2,1,0:T(8,128)(2,1)S(1)}, bf16[8,96,256]{2,1,0:T(8,128)(2,1)S(1)}, u32[]{:S(2)}, u32[]{:S(2)}) collective-permute-start(bf16[8,96,256]{2,1,0:T(8,128)(2,1)S(1)} %collective-permute-done.4.refs_6_.refs_2_), channel_id=1, source_target_pairs={{0,1},{1,0},{2,3},{3,2},{4,5},{5,4},{6,7},{7,6},{8,9},{9,8},{10,11... | collective-permute-start | bytes 1179656 | tf_op jit(solution)/shard_map/ppermute | solution.py:238
  30.4 3.2 %collective-permute-start.1 = (bf16[192,768]{1,0:T(8,128)(2,1)S(1)}, bf16[192,768]{1,0:T(8,128)(2,1)}, u32[]{:S(2)}, u32[]{:S(2)}) collective-permute-start(bf16[192,768]{1,0:T(8,128)(2,1)S(1)} %bitcast.5), channel_id=1, source_target_pairs={{0,1},{1,0},{2,3},{3,2},{4,5},{5,4},{6,7},{7,6},{8,9},{9,8},{10,11... | collective-permute-start | bytes 884744 | tf_op jit(solution)/shard_map/ppermute | solution.py:238
  30.9 2.7 %collective-permute-start.2 = (bf16[192,768]{1,0:T(8,128)(2,1)S(1)}, bf16[192,768]{1,0:T(8,128)(2,1)}, u32[]{:S(2)}, u32[]{:S(2)}) collective-permute-start(bf16[192,768]{1,0:T(8,128)(2,1)S(1)} %collective-permute-done.refs_2_), channel_id=1, source_target_pairs={{0,1},{1,0},{2,3},{3,2},{4,5},{5,4},{6,7},{7,6},{8,9},{9,8},{10,11... | collective-permute-start | bytes 884744 | tf_op jit(solution)/shard_map/ppermute | solution.py:238
  30.9 11.2 %collective-permute-start.9 = (bf16[192,768]{1,0:T(8,128)(2,1)}, bf16[192,768]{1,0:T(8,128)(2,1)S(1)}, u32[]{:S(2)}, u32[]{:S(2)}) collective-permute-start(bf16[192,768]{1,0:T(8,128)(2,1)} %bitcast.2.refs_0_), channel_id=1, source_target_pairs={{0,2},{1,3},{2,0},{3,1},{4,6},{5,7},{6,4},{7,5},{8,10},{9,11},{10,... | collective-permute-start | bytes 884744 | tf_op jit(solution)/shard_map/ppermute | solution.py:238
  37.0 19.9 %copy-start.2 = (bf16[1,1024,256]{2,1,0:T(8,128)(2,1)S(1)}, bf16[1,1024,256]{2,1,0:T(8,128)(2,1)}, u32[]{:S(2)}) copy-start(bf16[1,1024,256]{2,1,0:T(8,128)(2,1)} %refs_8_.2) | copy-start | bytes 1572868
  37.0 1.9 %collective-permute-start.6 = (f32[8,128]{1,0:T(8,128)S(1)}, f32[8,128]{1,0:T(8,128)S(1)}, u32[]{:S(2)}, u32[]{:S(2)}) collective-permute-start(f32[8,128]{1,0:T(8,128)S(1)} %get-tuple-element.37.refs_0_), channel_id=1, source_target_pairs={{0,1},{1,0},{2,3},{3,2},{4,5},{5,4},{6,7},{7,6},{8,9},{9,8},{10,11... | collective-permute-start | bytes 12296 | tf_op jit(solution)/shard_map/ppermute | solution.py:238
  37.3 3.6 %collective-permute-start.7 = (f32[8,128]{1,0:T(8,128)S(1)}, f32[8,128]{1,0:T(8,128)S(1)}, u32[]{:S(2)}, u32[]{:S(2)}) collective-permute-start(f32[8,128]{1,0:T(8,128)S(1)} %get-tuple-element.37.refs_0_), channel_id=1, source_target_pairs={{0,2},{1,3},{2,0},{3,1},{4,6},{5,7},{6,4},{7,5},{8,10},{9,11},{10,... | collective-permute-start | bytes 12296 | tf_op jit(solution)/shard_map/ppermute | solution.py:238
  38.2 3.0 %collective-permute-start.8 = (f32[8,128]{1,0:T(8,128)S(1)}, f32[8,128]{1,0:T(8,128)S(1)}, u32[]{:S(2)}, u32[]{:S(2)}) collective-permute-start(f32[8,128]{1,0:T(8,128)S(1)} %get-tuple-element.37.refs_0_), channel_id=1, source_target_pairs={{0,3},{1,2},{2,1},{3,0},{4,7},{5,6},{6,5},{7,4},{8,11},{9,10},{10,... | collective-permute-start | bytes 12296 | tf_op jit(solution)/shard_map/ppermute | solution.py:238
  42.1 11.9 %collective-permute-start.13 = (bf16[8,104,256]{2,1,0:T(8,128)(2,1)S(1)}, bf16[8,104,256]{2,1,0:T(8,128)(2,1)}, u32[]{:S(2)}, u32[]{:S(2)}) collective-permute-start(bf16[8,104,256]{2,1,0:T(8,128)(2,1)S(1)} %all-to-all-done.2.refs_4_.refs_0_), channel_id=1, source_target_pairs={{0,2},{1,3},{2,0},{3,1},{4,6},{5,7},{6,4},{7,5},{8,10},{9,11},{10,... | collective-permute-start | bytes 1277960 | tf_op jit(solution)/shard_map/ppermute | solution.py:238
  43.2 22.5 %all-to-all-start.1 = ((bf16[8,96,192]{2,1,0:T(8,128)(2,1)}), bf16[8,96,192]{2,1,0:T(8,128)(2,1)S(1)}, u32[]{:S(2)}, u32[]{:S(2)}) async-start(bf16[8,96,192]{2,1,0:T(8,128)(2,1)} %bitcast.1), calls=%async_computation.1 | async-start | bytes 786432 | tf_op jit(solution)/shard_map/all_to_all | solution.py:261
  49.4 7.5 %collective-permute-start.12 = (bf16[8,104,256]{2,1,0:T(8,128)(2,1)S(1)}, bf16[8,104,256]{2,1,0:T(8,128)(2,1)S(1)}, u32[]{:S(2)}, u32[]{:S(2)}) collective-permute-start(bf16[8,104,256]{2,1,0:T(8,128)(2,1)S(1)} %all-to-all-done.2.refs_4_.refs_0_), channel_id=1, source_target_pairs={{0,1},{1,0},{2,3},{3,2},{4,5},{5,4},{6,7},{7,6},{8,9},{9,8},{10,11... | collective-permute-start | bytes 1277960 | tf_op jit(solution)/shard_map/ppermute | solution.py:238
  54.1 2.8 %collective-permute-start.14 = (bf16[8,104,256]{2,1,0:T(8,128)(2,1)}, bf16[8,104,256]{2,1,0:T(8,128)(2,1)S(1)}, u32[]{:S(2)}, u32[]{:S(2)}) collective-permute-start(bf16[8,104,256]{2,1,0:T(8,128)(2,1)} %collective-permute-done.13.refs_6_.refs_2_), channel_id=1, source_target_pairs={{0,1},{1,0},{2,3},{3,2},{4,5},{5,4},{6,7},{7,6},{8,9},{9,8},{10,11... | collective-permute-start | bytes 1277960 | tf_op jit(solution)/shard_map/ppermute | solution.py:238
  54.1 2.8 %collective-permute-start.10 = (bf16[192,768]{1,0:T(8,128)(2,1)}, bf16[192,768]{1,0:T(8,128)(2,1)S(1)}, u32[]{:S(2)}, u32[]{:S(2)}) collective-permute-start(bf16[192,768]{1,0:T(8,128)(2,1)} %bitcast.2.refs_0_), channel_id=1, source_target_pairs={{0,1},{1,0},{2,3},{3,2},{4,5},{5,4},{6,7},{7,6},{8,9},{9,8},{10,11... | collective-permute-start | bytes 884744 | tf_op jit(solution)/shard_map/ppermute | solution.py:238
  54.6 2.3 %collective-permute-start.11 = (bf16[192,768]{1,0:T(8,128)(2,1)S(1)}, bf16[192,768]{1,0:T(8,128)(2,1)S(1)}, u32[]{:S(2)}, u32[]{:S(2)}) collective-permute-start(bf16[192,768]{1,0:T(8,128)(2,1)S(1)} %collective-permute-done.9.refs_2_), channel_id=1, source_target_pairs={{0,1},{1,0},{2,3},{3,2},{4,5},{5,4},{6,7},{7,6},{8,9},{9,8},{10,11... | collective-permute-start | bytes 884744 | tf_op jit(solution)/shard_map/ppermute | solution.py:238
  60.5 1.9 %collective-permute-start.15 = (f32[8,128]{1,0:T(8,128)S(1)}, f32[8,128]{1,0:T(8,128)S(1)}, u32[]{:S(2)}, u32[]{:S(2)}) collective-permute-start(f32[8,128]{1,0:T(8,128)S(1)} %get-tuple-element.46.refs_0_), channel_id=1, source_target_pairs={{0,1},{1,0},{2,3},{3,2},{4,5},{5,4},{6,7},{7,6},{8,9},{9,8},{10,11... | collective-permute-start | bytes 12296 | tf_op jit(solution)/shard_map/ppermute | solution.py:238
  60.7 3.6 %collective-permute-start.16 = (f32[8,128]{1,0:T(8,128)S(1)}, f32[8,128]{1,0:T(8,128)S(1)}, u32[]{:S(2)}, u32[]{:S(2)}) collective-permute-start(f32[8,128]{1,0:T(8,128)S(1)} %get-tuple-element.46.refs_0_), channel_id=1, source_target_pairs={{0,2},{1,3},{2,0},{3,1},{4,6},{5,7},{6,4},{7,5},{8,10},{9,11},{10,... | collective-permute-start | bytes 12296 | tf_op jit(solution)/shard_map/ppermute | solution.py:238
  61.8 3.0 %collective-permute-start.17 = (f32[8,128]{1,0:T(8,128)S(1)}, f32[8,128]{1,0:T(8,128)S(1)}, u32[]{:S(2)}, u32[]{:S(2)}) collective-permute-start(f32[8,128]{1,0:T(8,128)S(1)} %get-tuple-element.46.refs_0_), channel_id=1, source_target_pairs={{0,3},{1,2},{2,1},{3,0},{4,7},{5,6},{6,5},{7,4},{8,11},{9,10},{10,... | collective-permute-start | bytes 12296 | tf_op jit(solution)/shard_map/ppermute | solution.py:238
  65.8 16.5 %all-to-all-start.3 = ((bf16[8,96,256]{2,1,0:T(8,128)(2,1)}), bf16[8,96,256]{2,1,0:T(8,128)(2,1)S(1)}, u32[]{:S(2)}, u32[]{:S(2)}) async-start(bf16[8,96,256]{2,1,0:T(8,128)(2,1)} %bitcast.3), calls=%async_computation.3 | async-start | bytes 786432 | tf_op jit(solution)/shard_map/all_to_all | solution.py:261
  (14 other events, 85.2 us)

commit v5 on v4

--- a/solution.py
+++ b/solution.py
@@ -32,14 +32,16 @@
     return (rows, lanes) if lanes > cols else (round_up(rows + 3, 8), cols)
 
 
-def pieces(total, shape):
-    full = jnp.broadcast_to(total, shape)
-    high = full.astype(bf16).astype(f32)
-    middle = (full - high).astype(bf16).astype(f32)
-    low = full - high - middle
+def pieces(totals, shape):
     row = lax.broadcasted_iota(jnp.int32, shape, 0)
     column = lax.broadcasted_iota(jnp.int32, shape, 1)
-    value = jnp.where(row == 0, high, jnp.where(row == 1, middle, jnp.where(row == 2, low, 0.0)))
+    value = jnp.zeros(shape, f32)
+    for n, total in enumerate(totals):
+        rest = jnp.broadcast_to(total, shape)
+        for m in range(3):
+            piece = rest.astype(bf16).astype(f32)
+            value = jnp.where(row == 3 * n + m, piece, value)
+            rest = rest - piece
     return jnp.where(column == 0, value, 0.0).astype(bf16)
 
 
@@ -61,10 +63,10 @@
         slot = owner[u]
         if packed_cols > cols:
             packed[slot, :, :cols] = summed.astype(bf16)
-            packed[slot, :, cols:] = pieces(total, (packed_rows, packed_cols - cols))
+            packed[slot, :, cols:] = pieces((total,), (packed_rows, packed_cols - cols))
         else:
             packed[slot, :rows, :] = summed.astype(bf16)
-            packed[slot, rows:, :] = pieces(total, (packed_rows - rows, packed_cols))
+            packed[slot, rows:, :] = pieces((total,), (packed_rows - rows, packed_cols))
         return carry
 
     lax.fori_loop(0, moment.shape[0], unit, 0, unroll=moment.shape[0] <= 4)
@@ -104,7 +106,7 @@
 
 def shampoo_kernel(rows, cols, owner, *refs):
     tensor = lax.axis_size("tensor")
-    left, grad, (root, out, norm, adam, whole, half) = refs[:tensor], refs[tensor : 2 * tensor], refs[2 * tensor :]
+    left, grad, (root, *outs, whole, half) = refs[:tensor], refs[tensor : 2 * tensor], refs[2 * tensor :]
     part = lax.axis_index("tensor")
 
     @pl.when(holds(owner))
@@ -113,8 +115,8 @@
         for i in range(tensor):
             place = pl.multiple_of((part ^ i) * depth, depth)
             whole[pl.ds(place, depth), :] = left[i][...]
-        total = jnp.zeros(out.shape, f32)
-        adam_sq = jnp.zeros((), f32)
+        total = jnp.zeros((whole.shape[0], cols), f32)
+        adam_sq = jnp.zeros((1, 1), f32)
         for k in range(tensor):
             columns = block(grad[k], rows, cols)
             half[k] = jnp.dot(whole[...], columns, preferred_element_type=f32).astype(bf16)
@@ -122,33 +124,54 @@
                 extra = grad[k][:, :, cols:]
             else:
                 extra = grad[k][:, rows:, :]
-            adam_sq = adam_sq + jnp.sum(extra.astype(f32))
+            extra = extra.astype(f32).reshape(-1, extra.shape[-1])
+            adam_sq = adam_sq + jnp.sum(extra, axis=(0, 1), keepdims=True)
         for k in range(tensor):
-            place = pl.multiple_of((part ^ k) * cols, cols)
-            total = total + jnp.dot(
-                half[k], root[0, pl.ds(place, cols), :], preferred_element_type=f32
+            span = slice(k * cols, (k + 1) * cols)
+            if spare(cols):
+                sides, right = (((1,), (1,)), ((), ())), root[0, :, span]
+            else:
+                sides, right = (((1,), (0,)), ((), ())), root[0, span, :]
+            total = total + lax.dot_general(
+                half[part ^ k], right, sides, preferred_element_type=f32
             )
-        out[...] = total
-        norm[...] = jnp.full(norm.shape, jnp.sum(total * total), f32)
-        adam[...] = jnp.full(adam.shape, adam_sq, f32)
+        norm = jnp.sum(total * total, axis=(0, 1), keepdims=True)
+        if len(outs) == 1:
+            out = outs[0]
+            owners, high, wide = out.shape
+            out[:, :, :cols] = total.astype(bf16).reshape(owners, high, cols)
+            extra = pieces((norm, adam_sq), (high, wide - cols))
+            out[:, :, cols:] = jnp.broadcast_to(extra[None], (owners, *extra.shape))
+        else:
+            for ref, value in zip(outs, (total, norm, adam_sq)):
+                ref[...] = jnp.broadcast_to(value, ref.shape)
 
     @pl.when(jnp.logical_not(holds(owner)))
     def _():
-        out[...] = jnp.zeros_like(out)
-        norm[...] = jnp.zeros_like(norm)
-        adam[...] = jnp.zeros_like(adam)
+        for ref in outs:
+            ref[...] = jnp.zeros_like(ref)
+
+
+def spare(cols):
+    return round_up(cols, LANES) > cols
 
 
 def shampoo_part(owner, left, grad, root, rows):
     cols = root.shape[2]
     depth = left[0].shape[1]
+    if spare(cols):
+        root = jnp.swapaxes(root, 1, 2)
     tensor = len(left)
     small = jax.ShapeDtypeStruct((8, LANES), f32)
+    if spare(cols):
+        shapes = (jax.ShapeDtypeStruct((depth // rows, rows, round_up(cols, LANES)), bf16),)
+    else:
+        shapes = (jax.ShapeDtypeStruct((depth, cols), f32), small, small)
     return pl.pallas_call(
         functools.partial(shampoo_kernel, rows, cols),
-        out_shape=(jax.ShapeDtypeStruct((depth, cols), f32), small, small),
+        out_shape=shapes,
         in_specs=[SMEM] + [VMEM] * (2 * tensor + 1),
-        out_specs=(VMEM, VMEM, VMEM),
+        out_specs=(VMEM,) * len(shapes),
         scratch_shapes=[pltpu.VMEM((depth, depth), bf16), pltpu.VMEM((tensor, depth, cols), bf16)],
         compiler_params=LIMIT,
         cost_estimate=BRIEF,
@@ -212,25 +235,72 @@
     )(owner, *grad, *stats)
 
 
-def weight_kernel(owner, weight, back, out):
+def weight_kernel(owner, weight, back, *refs):
+    *norm, out = refs
+    cols = weight.shape[2]
+
     def unit(u, carry):
-        out[u] = weight[u] - learn_rate * back[owner[u]].astype(f32)
+        update = back[owner[u], :, :cols].astype(f32)
+        if norm:
+            adam, *norms = norm
+            total = norms[0][u]
+            for other in norms[1:]:
+                total = total + other[u]
+            update = jnp.sqrt(adam[u] / (total + graft_eps))[:1, :1] * update
+        out[u] = weight[u] - learn_rate * update
         return carry
 
     lax.fori_loop(0, weight.shape[0], unit, 0, unroll=weight.shape[0] <= 4)
 
 
-def weight_part(owner, weight, back):
+def weight_part(owner, weight, back, *norm):
     return pl.pallas_call(
         weight_kernel,
         out_shape=jax.ShapeDtypeStruct(weight.shape, f32),
-        in_specs=[SMEM, VMEM, VMEM],
+        in_specs=[SMEM] + [VMEM] * (2 + len(norm)),
         out_specs=VMEM,
         compiler_params=LIMIT,
         cost_estimate=pl.CostEstimate(
             flops=2 * weight.size, bytes_accessed=12 * weight.size, transcendentals=0
         ),
-    )(owner, weight, back)
+    )(owner, weight, back, *norm)
+
+
+def extra_kernel(cols, owner, back, norm, adam):
+    def unit(u, carry):
+        extra = back[owner[u], :, cols:].astype(f32)
+        row = lax.broadcasted_iota(jnp.int32, extra.shape, 0)
+        for ref, first in ((norm, 0), (adam, 3)):
+            mine = jnp.where((row >= first) & (row < first + 3), extra, 0.0)
+            total = jnp.sum(mine, axis=(0, 1), keepdims=True)
+            ref[u] = jnp.broadcast_to(total, ref.shape[1:])
+        return carry
+
+    lax.fori_loop(0, norm.shape[0], unit, 0, unroll=norm.shape[0] <= 4)
+
+
+def extra_part(owner, back, cols):
+    small = jax.ShapeDtypeStruct((owner.shape[0], 8, LANES), f32)
+    norm, adam = pl.pallas_call(
+        functools.partial(extra_kernel, cols),
+        out_shape=(small, small),
+        in_specs=[SMEM, VMEM],
+        out_specs=(VMEM, VMEM),
+        compiler_params=LIMIT,
+        cost_estimate=BRIEF,
+    )(owner, back)
+    return adam, *all_norms(norm)
+
+
+def all_norms(norm):
+    return [norm] + [flip(norm, k) for k in range(1, lax.axis_size("tensor"))]
+
+
+def back_part(owner, weight, done, owners):
+    if len(done) == 1:
+        back = over_shard(done[0])
+        return weight_part(owner, weight, back, *extra_part(owner, back, weight.shape[2]))
+    return weight_part(owner, weight, over_shard(grafted(*done, owners)))
 
 
 def flip(value, bits):
@@ -271,7 +341,7 @@
 
 
 def grafted(done, norm, adam, owners):
-    norms = [norm] + [flip(norm, k) for k in range(1, lax.axis_size("tensor"))]
+    norms = all_norms(norm)
     out = pl.pallas_call(
         scale_kernel,
         out_shape=jax.ShapeDtypeStruct(done.shape, bf16),
@@ -317,20 +387,17 @@
     att_left = spread_rest(*lax.optimization_barrier((att_root, att_root_far, att_near))[:2])
     glu_root, glu_root_far = spread_first(after(glu_left_root[0], att_far))
     att_grad = spread_rest(att_near, att_far)
-    att_done, att_norm, att_adam = shampoo_part(att_owner, att_left, att_grad, att_right_root, rows)
-    att_send = grafted(att_done, att_norm, att_adam, owners)
-    glu_near, glu_far = spread_first(after(over_shard(glu_packed), att_send, glu_root_far))
+    att_done = shampoo_part(att_owner, att_left, att_grad, att_right_root, rows)
+    glu_near, glu_far = spread_first(after(over_shard(glu_packed), glu_root_far, *att_done))
     glu_left = spread_rest(*lax.optimization_barrier((glu_root, glu_root_far, glu_near))[:2])
-    att_back = over_shard(att_send)
-    glu_grad = spread_rest(glu_near, glu_far)
-    glu_done, glu_norm, glu_adam = shampoo_part(glu_owner, glu_left, glu_grad, glu_right_root, rows)
-    glu_back = over_shard(grafted(glu_done, glu_norm, glu_adam, owners))
     (att_stats_out,) = stats_part(att_owner, att_grad, (att_stats,), rows, att_weight.shape[2])
+    glu_grad = spread_rest(glu_near, after(glu_far, att_stats_out, *glu_left[1:]))
+    glu_done = shampoo_part(glu_owner, glu_left, glu_grad, glu_right_root, rows)
     glu_left_out, glu_right_out = stats_part(
         glu_owner, glu_grad, (glu_left_stat, glu_right_stat), rows, glu_weight.shape[2]
     )
-    att_weight_out = weight_part(att_owner, att_weight, att_back)
-    glu_weight_out = weight_part(glu_owner, glu_weight, glu_back)
+    att_weight_out = back_part(att_owner, att_weight, att_done, owners)
+    glu_weight_out = back_part(glu_owner, glu_weight, glu_done, owners)
     return (
         att_weight_out,
         att_moment_out,

time: 85 us -> 83.8 us (0.986); the launches traced: 83.6 us -> 83.3 us
  starting transfers between devices: 32.2 us -> 37.6 us
  Pallas kernels: 22.1 us -> 19.1 us
  waiting for transfers between devices: 25.9 us -> 24.5 us
  local copies, waits for them, and re-layouts: 2.46 us -> 1.32 us
    all_to_all x4, starting transfers between devices: 21.6 us -> 26 us  [over_shard(): lax.all_to_all(value, 'shard', split_axis=0, concat_axis=0, tiled=True)]
    ppermute x18, waiting for transfers between devices: 19.7 us -> 16 us  [flip(): return lax.ppermute(value, 'tensor', [(i, i ^ bits) for i in range(size)])]
    all_to_all x4, waiting for transfers between devices: 6.25 us -> 8.5 us  [over_shard(): lax.all_to_all(value, 'shard', split_axis=0, concat_axis=0, tiled=True)]
    pallas_call x2, Pallas kernels: 6.21 us -> 4.54 us  [stats_part(): pl.pallas_call(functools.partial(stats_kernel, rows, cols, len(stats) ==...]
    unnamed x33 -> x26, local copies, waits for them, and re-layouts: 2.46 us -> 1.32 us
    ppermute x18, starting transfers between devices: 10.6 us -> 11.6 us  [flip(): return lax.ppermute(value, 'tensor', [(i, i ^ bits) for i in range(size)])]
    pallas_call x2 -> x1, Pallas kernels: 1.78 us -> 0.87 us  [grafted(): pl.pallas_call(scale_kernel, out_shape=jax.ShapeDtypeStruct(done.shape, b...]
    pallas_call x2 -> x3, Pallas kernels: 6.87 us -> 6.34 us  [the longest x2 5.5 us: shampoo_part(): pl.pallas_call(functools.partial(shampoo_kernel, rows, cols), out_shape=s...]
  transfers between devices with their start and end apart: 22 -> 22, of which waited for: 10 -> 12; matrix products, arithmetic and copies ran while one was open for 1% -> 0% of each run, Pallas kernels for 22% -> 18%
where the time goes in v5:
time: 83.8 us; the launch traced here: 83.3 us
  starting transfers between devices  37.6 us (45%)
  waiting for transfers between devices  24.5 us (29%)
  Pallas kernels  19.1 us (23%)
  local copies, waits for them, and re-layouts  1.32 us (2%)
    all_to_all x4, starting transfers between devices, over_shard(): lax.all_to_all(value, 'shard', split_axis=0, concat_axis=0, tiled=True)  26 us
    ppermute x18, waiting for transfers between devices, flip(): return lax.ppermute(value, 'tensor', [(i, i ^ bits) for i in range(size)])  16 us
    ppermute x18, starting transfers between devices, flip(): return lax.ppermute(value, 'tensor', [(i, i ^ bits) for i in range(size)])  11.6 us
    all_to_all x4, waiting for transfers between devices, over_shard(): lax.all_to_all(value, 'shard', split_axis=0, concat_axis=0, tiled=True)  8.5 us
    pallas_call x2, Pallas kernels, shampoo_part(): pl.pallas_call(functools.partial(shampoo_kernel, rows, cols), out_shape=s...  5.5 us
    pallas_call x2, Pallas kernels, adam_part(): pl.pallas_call(adam_kernel, out_shape=(packed, jax.ShapeDtypeStruct(momen...  4.58 us
    pallas_call x2, Pallas kernels, stats_part(): pl.pallas_call(functools.partial(stats_kernel, rows, cols, len(stats) ==...  4.54 us
    pallas_call x2, Pallas kernels, weight_part(): pl.pallas_call(weight_kernel, out_shape=jax.ShapeDtypeStruct(weight.shape...  2.72 us
  transfers between devices with their start and end apart: 22, of which 12 were waited for; matrix products, arithmetic and copies ran while one was open for 0% of the time, Pallas kernels for 18%

profile of v5, /device:TPU:0, one launch (start us, length us, event | category | flops | bytes accessed | tf_op | source)
XLA Modules:
  0.0 83.3 jit_solution(7181887791824813382)
XLA Ops:
  0.7 2.8 %shard_map.232 = (bf16[8,96,256]{2,1,0:T(8,128)(2,1)}, f32[4,96,192]{2,1,0:T(8,128)}, f32[4,96,192]{2,1,0:T(8,128)}) custom-call(s32[4]{0:T(128)} %owner.14, f32[2,4,96,192]{3,2,1,0:T(8,128)} %grads.2, f32[4,96,192]{2,1,0:T(8,128)} %moment.2, f32[4,96,192]{2,1,0:T(8,128)} %second.2), custom_call_target="tpu_custom_call" | custom-call | flops 1474560 | bytes 2359296 | tf_op jit(solution)/shard_map/pallas_call | solution.py:78
  3.5 7.3 %all-to-all-start = ((bf16[8,96,256]{2,1,0:T(8,128)(2,1)}), bf16[8,96,256]{2,1,0:T(8,128)(2,1)S(1)}, u32[]{:S(2)}, u32[]{:S(2)}) async-start(bf16[8,96,256]{2,1,0:T(8,128)(2,1)} %get-tuple-element.30), calls=%async_computation | async-start | bytes 786432 | tf_op jit(solution)/shard_map/all_to_all | solution.py:331
  10.7 1.6 %collective-permute-start = (bf16[192,768]{1,0:T(8,128)(2,1)S(1)}, bf16[192,768]{1,0:T(8,128)(2,1)S(1)}, u32[]{:S(2)}, u32[]{:S(2)}) collective-permute-start(bf16[192,768]{1,0:T(8,128)(2,1)S(1)} %bitcast.4), channel_id=1, source_target_pairs={{0,2},{1,3},{2,0},{3,1},{4,6},{5,7},{6,4},{7,5},{8,10},{9,11},{10,... | collective-permute-start | bytes 884744 | tf_op jit(solution)/shard_map/ppermute | solution.py:308
  12.3 1.8 %shard_map.233 = (bf16[8,104,256]{2,1,0:T(8,128)(2,1)}, f32[4,96,256]{2,1,0:T(8,128)}, f32[4,96,256]{2,1,0:T(8,128)}) custom-call(s32[4]{0:T(128)S(1)} %copy-done.10, f32[2,4,96,256]{3,2,1,0:T(8,128)S(1)} %copy-done.1, f32[4,96,256]{2,1,0:T(8,128)S(1)} %copy-done.3, f32[4,96,256]{2,1,0:T(8,128)S(1)} %copy-done.4), custom_call_target="tpu_custom_call" | custom-call | flops 1966080 | bytes 3145728 | tf_op jit(solution)/shard_map/pallas_call | solution.py:78
  14.2 5.1 %collective-permute-done.refs_2_ = bf16[192,768]{1,0:T(8,128)(2,1)S(1)} collective-permute-done((bf16[192,768]{1,0:T(8,128)(2,1)S(1)}, bf16[192,768]{1,0:T(8,128)(2,1)S(1)}, u32[]{:S(2)}, u32[]{:S(2)}) %collective-permute-start) | collective-permute-done | bytes 294944 | tf_op jit(solution)/shard_map/ppermute | solution.py:308
  19.3 3.1 %all-to-all-done.refs_4_.refs_0_ = bf16[8,96,256]{2,1,0:T(8,128)(2,1)S(1)} async-done(((bf16[8,96,256]{2,1,0:T(8,128)(2,1)}), bf16[8,96,256]{2,1,0:T(8,128)(2,1)S(1)}, u32[]{:S(2)}, u32[]{:S(2)}) %all-to-all-start) | async-done | bytes 393248 | tf_op jit(solution)/shard_map/all_to_all | solution.py:331
  22.4 1.5 %collective-permute-start.4 = (bf16[8,96,256]{2,1,0:T(8,128)(2,1)S(1)}, bf16[8,96,256]{2,1,0:T(8,128)(2,1)S(1)}, u32[]{:S(2)}, u32[]{:S(2)}) collective-permute-start(bf16[8,96,256]{2,1,0:T(8,128)(2,1)S(1)} %all-to-all-done.refs_4_.refs_0_), channel_id=1, source_target_pairs={{0,2},{1,3},{2,0},{3,1},{4,6},{5,7},{6,4},{7,5},{8,10},{9,11},{10,... | collective-permute-start | bytes 1179656 | tf_op jit(solution)/shard_map/ppermute | solution.py:308
  23.9 3.6 %all-to-all-start.2 = ((bf16[8,104,256]{2,1,0:T(8,128)(2,1)}), bf16[8,104,256]{2,1,0:T(8,128)(2,1)S(1)}, u32[]{:S(2)}, u32[]{:S(2)}) async-start(bf16[8,104,256]{2,1,0:T(8,128)(2,1)} %get-tuple-element.31), calls=%async_computation.2 | async-start | bytes 851968 | tf_op jit(solution)/shard_map/all_to_all | solution.py:331
  27.6 2.8 %collective-permute-done.4.refs_6_.refs_2_ = bf16[8,96,256]{2,1,0:T(8,128)(2,1)S(1)} collective-permute-done((bf16[8,96,256]{2,1,0:T(8,128)(2,1)S(1)}, bf16[8,96,256]{2,1,0:T(8,128)(2,1)S(1)}, u32[]{:S(2)}, u32[]{:S(2)}) %collective-permute-start.4) | collective-permute-done | bytes 393248 | tf_op jit(solution)/shard_map/ppermute | solution.py:308
  30.9 1.5 %collective-permute-start.9 = (bf16[192,768]{1,0:T(8,128)(2,1)}, bf16[192,768]{1,0:T(8,128)(2,1)}, u32[]{:S(2)}, u32[]{:S(2)}) collective-permute-start(bf16[192,768]{1,0:T(8,128)(2,1)} %bitcast.2.refs_0_), channel_id=1, source_target_pairs={{0,2},{1,3},{2,0},{3,1},{4,6},{5,7},{6,4},{7,5},{8,10},{9,11},{10,... | collective-permute-start | bytes 884744 | tf_op jit(solution)/shard_map/ppermute | solution.py:308
  33.0 4.3 %shard_map.234 = bf16[8,96,256]{2,1,0:T(8,128)(2,1)} custom-call(s32[4]{0:T(128)S(1)} %copy-done.9, bf16[192,768]{1,0:T(8,128)(2,1)S(1)} %bitcast.6, bf16[192,768]{1,0:T(8,128)(2,1)S(1)} %collective-permute-done.1.refs_1_, bf16[192,768]{1,0:T(8,128)(2,1)S(1)} %collective-permute-done.refs_2_, bf16[192,768]{1,0:T(8,128)(2,1)S(1)} %collective-permute-done.2.refs_3_, ...), custom_call_target="tpu_custom_call" | custom-call | flops 1024 | bytes 1024 | tf_op jit(solution)/shard_map/pallas_call | solution.py:170
  37.3 2.3 %all-to-all-done.2.refs_4_.refs_0_ = bf16[8,104,256]{2,1,0:T(8,128)(2,1)S(1)} async-done(((bf16[8,104,256]{2,1,0:T(8,128)(2,1)}), bf16[8,104,256]{2,1,0:T(8,128)(2,1)S(1)}, u32[]{:S(2)}, u32[]{:S(2)}) %all-to-all-start.2) | async-done | bytes 426016 | tf_op jit(solution)/shard_map/all_to_all | solution.py:331
  40.7 1.5 %collective-permute-start.13 = (bf16[8,104,256]{2,1,0:T(8,128)(2,1)S(1)}, bf16[8,104,256]{2,1,0:T(8,128)(2,1)S(1)}, u32[]{:S(2)}, u32[]{:S(2)}) collective-permute-start(bf16[8,104,256]{2,1,0:T(8,128)(2,1)S(1)} %all-to-all-done.2.refs_4_.refs_0_), channel_id=1, source_target_pairs={{0,2},{1,3},{2,0},{3,1},{4,6},{5,7},{6,4},{7,5},{8,10},{9,11},{10,... | collective-permute-start | bytes 1277960 | tf_op jit(solution)/shard_map/ppermute | solution.py:308
  42.7 6.3 %all-to-all-start.1 = ((bf16[8,96,256]{2,1,0:T(8,128)(2,1)}), bf16[8,96,256]{2,1,0:T(8,128)(2,1)S(1)}, u32[]{:S(2)}, u32[]{:S(2)}) async-start(bf16[8,96,256]{2,1,0:T(8,128)(2,1)} %shard_map.234), calls=%async_computation.1 | async-start | bytes 786432 | tf_op jit(solution)/shard_map/all_to_all | solution.py:331
  50.3 2.7 %shard_map.237 = f32[1,2,192,768]{3,2,1,0:T(8,128)} custom-call(s32[4]{0:T(128)S(1)} %copy-done.9, bf16[8,96,256]{2,1,0:T(8,128)(2,1)S(1)} %all-to-all-done.refs_4_.refs_0_, bf16[8,96,256]{2,1,0:T(8,128)(2,1)S(1)} %collective-permute-done.3.refs_5_.refs_1_, bf16[8,96,256]{2,1,0:T(8,128)(2,1)S(1)} %collective-permute-done.4.refs_6_.refs_2_, ...), custom_call_target="tpu_custom_call" | custom-call | flops 452984832 | bytes 3538944 | tf_op jit(solution)/shard_map/pallas_call | solution.py:223
  53.6 1.4 %collective-permute-done.14.refs_7_.refs_3_ = bf16[8,104,256]{2,1,0:T(8,128)(2,1)S(1)} collective-permute-done((bf16[8,104,256]{2,1,0:T(8,128)(2,1)S(1)}, bf16[8,104,256]{2,1,0:T(8,128)(2,1)S(1)}, u32[]{:S(2)}, u32[]{:S(2)}) %collective-permute-start.14) | collective-permute-done | bytes 426016 | tf_op jit(solution)/shard_map/ppermute | solution.py:308
  58.2 2.1 %collective-permute-done.16.refs_2_ = f32[8,128]{1,0:T(8,128)S(1)} collective-permute-done((f32[8,128]{1,0:T(8,128)S(1)}, f32[8,128]{1,0:T(8,128)S(1)}, u32[]{:S(2)}, u32[]{:S(2)}) %collective-permute-start.16) | collective-permute-done | bytes 4128 | tf_op jit(solution)/shard_map/ppermute | solution.py:308
  61.2 8.8 %all-to-all-start.3 = ((bf16[8,96,256]{2,1,0:T(8,128)(2,1)}), bf16[8,96,256]{2,1,0:T(8,128)(2,1)S(1)}, u32[]{:S(2)}, u32[]{:S(2)}) async-start(bf16[8,96,256]{2,1,0:T(8,128)(2,1)} %bitcast.3), calls=%async_computation.3 | async-start | bytes 786432 | tf_op jit(solution)/shard_map/all_to_all | solution.py:331
  70.9 1.5 %collective-permute-start.7 = (f32[4,8,128]{2,1,0:T(8,128)S(1)}, f32[4,8,128]{2,1,0:T(8,128)S(1)}, u32[]{:S(2)}, u32[]{:S(2)}) collective-permute-start(f32[4,8,128]{2,1,0:T(8,128)S(1)} %get-tuple-element.36.refs_1_), channel_id=1, source_target_pairs={{0,2},{1,3},{2,0},{3,1},{4,6},{5,7},{6,4},{7,5},{8,10},{9,11},{10,... | collective-permute-start | bytes 49160 | tf_op jit(solution)/shard_map/ppermute | solution.py:308
  72.8 1.9 %collective-permute-done.7.refs_3_ = f32[4,8,128]{2,1,0:T(8,128)S(1)} collective-permute-done((f32[4,8,128]{2,1,0:T(8,128)S(1)}, f32[4,8,128]{2,1,0:T(8,128)S(1)}, u32[]{:S(2)}, u32[]{:S(2)}) %collective-permute-start.7) | collective-permute-done | bytes 16416 | tf_op jit(solution)/shard_map/ppermute | solution.py:308
  75.6 1.4 %shard_map.236 = f32[4,96,192]{2,1,0:T(8,128)} custom-call(s32[4]{0:T(128)S(1)} %copy-done.9, f32[4,96,192]{2,1,0:T(8,128)S(1)} %copy-done.5, bf16[8,96,256]{2,1,0:T(8,128)(2,1)S(1)} %all-to-all-done.1.back, f32[4,8,128]{2,1,0:T(8,128)S(1)} %get-tuple-element.35.refs_0_, f32[4,8,128]{2,1,0:T(8,128)S(1)} %get-tuple-element.36.refs_1_, ...), custom_call_target="tpu_custom_call" | custom-call | flops 147456 | bytes 884736 | tf_op jit(solution)/shard_map/pallas_call | solution.py:257
  77.0 1.8 %shard_map.241 = (f32[1,192,768]{2,1,0:T(8,128)}, f32[1,256,1024]{2,1,0:T(8,128)}) custom-call(s32[4]{0:T(128)S(1)} %copy-done.10, bf16[8,104,256]{2,1,0:T(8,128)(2,1)S(1)} %all-to-all-done.2.refs_4_.refs_0_, bf16[8,104,256]{2,1,0:T(8,128)(2,1)S(1)} %collective-permute-done.12.refs_5_.refs_1_, ...), custom_call_target="tpu_custom_call" | custom-call | flops 1073741824 | bytes 5373952 | tf_op jit(solution)/shard_map/pallas_call | solution.py:223
  78.9 3.1 %all-to-all-done.3.back = bf16[8,96,256]{2,1,0:T(8,128)(2,1)S(1)} async-done(((bf16[8,96,256]{2,1,0:T(8,128)(2,1)}), bf16[8,96,256]{2,1,0:T(8,128)(2,1)S(1)}, u32[]{:S(2)}, u32[]{:S(2)}) %all-to-all-start.3) | async-done | bytes 393248 | tf_op jit(solution)/shard_map/all_to_all | solution.py:331
  81.9 1.3 %shard_map.240 = f32[4,96,256]{2,1,0:T(8,128)} custom-call(s32[4]{0:T(128)S(1)} %copy-done.10, f32[4,96,256]{2,1,0:T(8,128)S(1)} %copy-done.6, bf16[8,96,256]{2,1,0:T(8,128)(2,1)S(1)} %all-to-all-done.3.back), custom_call_target="tpu_custom_call" | custom-call | flops 196608 | bytes 1179648 | tf_op jit(solution)/shard_map/pallas_call | solution.py:257
  (56 shorter events, 10.7 us)
Async XLA Ops:
  3.5 18.9 %all-to-all-start = ((bf16[8,96,256]{2,1,0:T(8,128)(2,1)}), bf16[8,96,256]{2,1,0:T(8,128)(2,1)S(1)}, u32[]{:S(2)}, u32[]{:S(2)}) async-start(bf16[8,96,256]{2,1,0:T(8,128)(2,1)} %get-tuple-element.30), calls=%async_computation | async-start | bytes 786432 | tf_op jit(solution)/shard_map/all_to_all | solution.py:331
  10.7 22.3 %copy-start.8 = (bf16[1,768,192]{1,2,0:T(8,128)(2,1)S(1)}, bf16[1,768,192]{1,2,0:T(8,128)(2,1)}, u32[]{:S(2)}) copy-start(bf16[1,768,192]{1,2,0:T(8,128)(2,1)} %param.27) | copy-start | bytes 884740
  10.7 22.3 %copy-start.9 = (s32[4]{0:T(128)S(1)}, s32[4]{0:T(128)}, u32[]{:S(2)}) copy-start(s32[4]{0:T(128)} %owner.14) | copy-start | bytes 52
  10.7 8.5 %collective-permute-start = (bf16[192,768]{1,0:T(8,128)(2,1)S(1)}, bf16[192,768]{1,0:T(8,128)(2,1)S(1)}, u32[]{:S(2)}, u32[]{:S(2)}) collective-permute-start(bf16[192,768]{1,0:T(8,128)(2,1)S(1)} %bitcast.4), channel_id=1, source_target_pairs={{0,2},{1,3},{2,0},{3,1},{4,6},{5,7},{6,4},{7,5},{8,10},{9,11},{10,... | collective-permute-start | bytes 884744 | tf_op jit(solution)/shard_map/ppermute | solution.py:308
  22.4 8.0 %collective-permute-start.4 = (bf16[8,96,256]{2,1,0:T(8,128)(2,1)S(1)}, bf16[8,96,256]{2,1,0:T(8,128)(2,1)S(1)}, u32[]{:S(2)}, u32[]{:S(2)}) collective-permute-start(bf16[8,96,256]{2,1,0:T(8,128)(2,1)S(1)} %all-to-all-done.refs_4_.refs_0_), channel_id=1, source_target_pairs={{0,2},{1,3},{2,0},{3,1},{4,6},{5,7},{6,4},{7,5},{8,10},{9,11},{10,... | collective-permute-start | bytes 1179656 | tf_op jit(solution)/shard_map/ppermute | solution.py:308
  23.9 15.6 %all-to-all-start.2 = ((bf16[8,104,256]{2,1,0:T(8,128)(2,1)}), bf16[8,104,256]{2,1,0:T(8,128)(2,1)S(1)}, u32[]{:S(2)}, u32[]{:S(2)}) async-start(bf16[8,104,256]{2,1,0:T(8,128)(2,1)} %get-tuple-element.31), calls=%async_computation.2 | async-start | bytes 851968 | tf_op jit(solution)/shard_map/all_to_all | solution.py:331
  27.6 5.4 %collective-permute-start.3 = (bf16[8,96,256]{2,1,0:T(8,128)(2,1)S(1)}, bf16[8,96,256]{2,1,0:T(8,128)(2,1)S(1)}, u32[]{:S(2)}, u32[]{:S(2)}) collective-permute-start(bf16[8,96,256]{2,1,0:T(8,128)(2,1)S(1)} %all-to-all-done.refs_4_.refs_0_), channel_id=1, source_target_pairs={{0,1},{1,0},{2,3},{3,2},{4,5},{5,4},{6,7},{7,6},{8,9},{9,8},{10,11... | collective-permute-start | bytes 1179656 | tf_op jit(solution)/shard_map/ppermute | solution.py:308
  30.4 2.6 %collective-permute-start.5 = (bf16[8,96,256]{2,1,0:T(8,128)(2,1)S(1)}, bf16[8,96,256]{2,1,0:T(8,128)(2,1)S(1)}, u32[]{:S(2)}, u32[]{:S(2)}) collective-permute-start(bf16[8,96,256]{2,1,0:T(8,128)(2,1)S(1)} %collective-permute-done.4.refs_6_.refs_2_), channel_id=1, source_target_pairs={{0,1},{1,0},{2,3},{3,2},{4,5},{5,4},{6,7},{7,6},{8,9},{9,8},{10,11... | collective-permute-start | bytes 1179656 | tf_op jit(solution)/shard_map/ppermute | solution.py:308
  30.4 2.1 %collective-permute-start.1 = (bf16[192,768]{1,0:T(8,128)(2,1)S(1)}, bf16[192,768]{1,0:T(8,128)(2,1)S(1)}, u32[]{:S(2)}, u32[]{:S(2)}) collective-permute-start(bf16[192,768]{1,0:T(8,128)(2,1)S(1)} %bitcast.5), channel_id=1, source_target_pairs={{0,1},{1,0},{2,3},{3,2},{4,5},{5,4},{6,7},{7,6},{8,9},{9,8},{10,11... | collective-permute-start | bytes 884744 | tf_op jit(solution)/shard_map/ppermute | solution.py:308
  30.9 2.1 %collective-permute-start.2 = (bf16[192,768]{1,0:T(8,128)(2,1)S(1)}, bf16[192,768]{1,0:T(8,128)(2,1)S(1)}, u32[]{:S(2)}, u32[]{:S(2)}) collective-permute-start(bf16[192,768]{1,0:T(8,128)(2,1)S(1)} %collective-permute-done.refs_2_), channel_id=1, source_target_pairs={{0,1},{1,0},{2,3},{3,2},{4,5},{5,4},{6,7},{7,6},{8,9},{9,8},{10,11... | collective-permute-start | bytes 884744 | tf_op jit(solution)/shard_map/ppermute | solution.py:308
  30.9 9.7 %collective-permute-start.9 = (bf16[192,768]{1,0:T(8,128)(2,1)}, bf16[192,768]{1,0:T(8,128)(2,1)}, u32[]{:S(2)}, u32[]{:S(2)}) collective-permute-start(bf16[192,768]{1,0:T(8,128)(2,1)} %bitcast.2.refs_0_), channel_id=1, source_target_pairs={{0,2},{1,3},{2,0},{3,1},{4,6},{5,7},{6,4},{7,5},{8,10},{9,11},{10,... | collective-permute-start | bytes 884744 | tf_op jit(solution)/shard_map/ppermute | solution.py:308
  40.7 12.4 %collective-permute-start.13 = (bf16[8,104,256]{2,1,0:T(8,128)(2,1)S(1)}, bf16[8,104,256]{2,1,0:T(8,128)(2,1)S(1)}, u32[]{:S(2)}, u32[]{:S(2)}) collective-permute-start(bf16[8,104,256]{2,1,0:T(8,128)(2,1)S(1)} %all-to-all-done.2.refs_4_.refs_0_), channel_id=1, source_target_pairs={{0,2},{1,3},{2,0},{3,1},{4,6},{5,7},{6,4},{7,5},{8,10},{9,11},{10,... | collective-permute-start | bytes 1277960 | tf_op jit(solution)/shard_map/ppermute | solution.py:308
  42.2 10.8 %collective-permute-start.10 = (bf16[192,768]{1,0:T(8,128)(2,1)}, bf16[192,768]{1,0:T(8,128)(2,1)S(1)}, u32[]{:S(2)}, u32[]{:S(2)}) collective-permute-start(bf16[192,768]{1,0:T(8,128)(2,1)} %bitcast.2.refs_0_), channel_id=1, source_target_pairs={{0,1},{1,0},{2,3},{3,2},{4,5},{5,4},{6,7},{7,6},{8,9},{9,8},{10,11... | collective-permute-start | bytes 884744 | tf_op jit(solution)/shard_map/ppermute | solution.py:308
  42.2 10.8 %collective-permute-start.11 = (bf16[192,768]{1,0:T(8,128)(2,1)}, bf16[192,768]{1,0:T(8,128)(2,1)}, u32[]{:S(2)}, u32[]{:S(2)}) collective-permute-start(bf16[192,768]{1,0:T(8,128)(2,1)} %collective-permute-done.9.refs_2_), channel_id=1, source_target_pairs={{0,1},{1,0},{2,3},{3,2},{4,5},{5,4},{6,7},{7,6},{8,9},{9,8},{10,11... | collective-permute-start | bytes 884744 | tf_op jit(solution)/shard_map/ppermute | solution.py:308
  42.7 18.5 %all-to-all-start.1 = ((bf16[8,96,256]{2,1,0:T(8,128)(2,1)}), bf16[8,96,256]{2,1,0:T(8,128)(2,1)S(1)}, u32[]{:S(2)}, u32[]{:S(2)}) async-start(bf16[8,96,256]{2,1,0:T(8,128)(2,1)} %shard_map.234), calls=%async_computation.1 | async-start | bytes 786432 | tf_op jit(solution)/shard_map/all_to_all | solution.py:331
  49.0 4.6 %collective-permute-start.12 = (bf16[8,104,256]{2,1,0:T(8,128)(2,1)S(1)}, bf16[8,104,256]{2,1,0:T(8,128)(2,1)S(1)}, u32[]{:S(2)}, u32[]{:S(2)}) collective-permute-start(bf16[8,104,256]{2,1,0:T(8,128)(2,1)S(1)} %all-to-all-done.2.refs_4_.refs_0_), channel_id=1, source_target_pairs={{0,1},{1,0},{2,3},{3,2},{4,5},{5,4},{6,7},{7,6},{8,9},{9,8},{10,11... | collective-permute-start | bytes 1277960 | tf_op jit(solution)/shard_map/ppermute | solution.py:308
  53.0 2.0 %collective-permute-start.14 = (bf16[8,104,256]{2,1,0:T(8,128)(2,1)S(1)}, bf16[8,104,256]{2,1,0:T(8,128)(2,1)S(1)}, u32[]{:S(2)}, u32[]{:S(2)}) collective-permute-start(bf16[8,104,256]{2,1,0:T(8,128)(2,1)S(1)} %collective-permute-done.13.refs_6_.refs_2_), channel_id=1, source_target_pairs={{0,1},{1,0},{2,3},{3,2},{4,5},{5,4},{6,7},{7,6},{8,9},{9,8},{10,11... | collective-permute-start | bytes 1277960 | tf_op jit(solution)/shard_map/ppermute | solution.py:308
  56.2 1.9 %collective-permute-start.15 = (f32[8,128]{1,0:T(8,128)S(1)}, f32[8,128]{1,0:T(8,128)S(1)}, u32[]{:S(2)}, u32[]{:S(2)}) collective-permute-start(f32[8,128]{1,0:T(8,128)S(1)} %get-tuple-element.46.refs_0_), channel_id=1, source_target_pairs={{0,1},{1,0},{2,3},{3,2},{4,5},{5,4},{6,7},{7,6},{8,9},{9,8},{10,11... | collective-permute-start | bytes 12296 | tf_op jit(solution)/shard_map/ppermute | solution.py:308
  56.7 3.6 %collective-permute-start.16 = (f32[8,128]{1,0:T(8,128)S(1)}, f32[8,128]{1,0:T(8,128)S(1)}, u32[]{:S(2)}, u32[]{:S(2)}) collective-permute-start(f32[8,128]{1,0:T(8,128)S(1)} %get-tuple-element.46.refs_0_), channel_id=1, source_target_pairs={{0,2},{1,3},{2,0},{3,1},{4,6},{5,7},{6,4},{7,5},{8,10},{9,11},{10,... | collective-permute-start | bytes 12296 | tf_op jit(solution)/shard_map/ppermute | solution.py:308
  57.2 3.1 %collective-permute-start.17 = (f32[8,128]{1,0:T(8,128)S(1)}, f32[8,128]{1,0:T(8,128)S(1)}, u32[]{:S(2)}, u32[]{:S(2)}) collective-permute-start(f32[8,128]{1,0:T(8,128)S(1)} %get-tuple-element.46.refs_0_), channel_id=1, source_target_pairs={{0,3},{1,2},{2,1},{3,0},{4,7},{5,6},{6,5},{7,4},{8,11},{9,10},{10,... | collective-permute-start | bytes 12296 | tf_op jit(solution)/shard_map/ppermute | solution.py:308
  61.2 20.8 %all-to-all-start.3 = ((bf16[8,96,256]{2,1,0:T(8,128)(2,1)}), bf16[8,96,256]{2,1,0:T(8,128)(2,1)S(1)}, u32[]{:S(2)}, u32[]{:S(2)}) async-start(bf16[8,96,256]{2,1,0:T(8,128)(2,1)} %bitcast.3), calls=%async_computation.3 | async-start | bytes 786432 | tf_op jit(solution)/shard_map/all_to_all | solution.py:331
  70.9 1.9 %collective-permute-start.6 = (f32[4,8,128]{2,1,0:T(8,128)S(1)}, f32[4,8,128]{2,1,0:T(8,128)S(1)}, u32[]{:S(2)}, u32[]{:S(2)}) collective-permute-start(f32[4,8,128]{2,1,0:T(8,128)S(1)} %get-tuple-element.36.refs_1_), channel_id=1, source_target_pairs={{0,1},{1,0},{2,3},{3,2},{4,5},{5,4},{6,7},{7,6},{8,9},{9,8},{10,11... | collective-permute-start | bytes 49160 | tf_op jit(solution)/shard_map/ppermute | solution.py:308
  70.9 3.8 %collective-permute-start.7 = (f32[4,8,128]{2,1,0:T(8,128)S(1)}, f32[4,8,128]{2,1,0:T(8,128)S(1)}, u32[]{:S(2)}, u32[]{:S(2)}) collective-permute-start(f32[4,8,128]{2,1,0:T(8,128)S(1)} %get-tuple-element.36.refs_1_), channel_id=1, source_target_pairs={{0,2},{1,3},{2,0},{3,1},{4,6},{5,7},{6,4},{7,5},{8,10},{9,11},{10,... | collective-permute-start | bytes 49160 | tf_op jit(solution)/shard_map/ppermute | solution.py:308
  72.5 3.2 %collective-permute-start.8 = (f32[4,8,128]{2,1,0:T(8,128)S(1)}, f32[4,8,128]{2,1,0:T(8,128)S(1)}, u32[]{:S(2)}, u32[]{:S(2)}) collective-permute-start(f32[4,8,128]{2,1,0:T(8,128)S(1)} %get-tuple-element.36.refs_1_), channel_id=1, source_target_pairs={{0,3},{1,2},{2,1},{3,0},{4,7},{5,6},{6,5},{7,4},{8,11},{9,10},{10,... | collective-permute-start | bytes 49160 | tf_op jit(solution)/shard_map/ppermute | solution.py:308
  (11 other events, 97.0 us)

commit v6 on v5

--- a/solution.py
+++ b/solution.py
@@ -27,9 +27,15 @@
     return -(-value // step) * step
 
 
-def packed_shape(rows, cols):
+def folds(rows, cols):
+    return cols == LANES + LANES // 2 and rows % 32 == 0
+
+
+def packed_shape(rows, cols, totals):
     lanes = round_up(cols, LANES)
-    return (rows, lanes) if lanes > cols else (round_up(rows + 3, 8), cols)
+    if folds(rows, cols):
+        return (rows + rows // 2 + round_up(3 * totals, 8), LANES)
+    return (rows, lanes) if lanes > cols else (round_up(rows + 3 * totals, 8), cols)
 
 
 def pieces(totals, shape):
@@ -45,9 +51,49 @@
     return jnp.where(column == 0, value, 0.0).astype(bf16)
 
 
+def pack(ref, value, totals):
+    rows, cols = value.shape
+    high, wide = ref.shape
+    if folds(rows, cols):
+        half, side = rows // 2, value[:, LANES:]
+        ref[:rows, :] = value[:, :LANES].astype(bf16)
+        ref[rows : rows + half, :] = jnp.concatenate([side[:half], side[half:]], axis=1).astype(bf16)
+        if totals:
+            ref[rows + half :, :] = pieces(totals, (high - rows - half, wide))
+    elif wide > cols:
+        ref[:, :cols] = value.astype(bf16)
+        ref[:, cols:] = pieces(totals, (high, wide - cols))
+    else:
+        ref[:rows, :] = value.astype(bf16)
+        if totals:
+            ref[rows:, :] = pieces(totals, (high - rows, wide))
+
+
+def unpack(ref, rows, cols, start=0, count=None):
+    count = ref.shape[0] if count is None else count
+    span = pl.ds(start, count)
+    if not folds(rows, cols):
+        return ref[span, :rows, :cols].reshape(count * rows, cols)
+    side = ref[span, rows : rows + rows // 2, :]
+    side = jnp.concatenate([side[:, :, : LANES // 2], side[:, :, LANES // 2 :]], axis=1)
+    return jnp.concatenate([ref[span, :rows, :], side], axis=2).reshape(count * rows, cols)
+
+
+def unpack_total(ref, rows, cols, n, start=0, count=None):
+    count = ref.shape[0] if count is None else count
+    span = pl.ds(start, count)
+    if folds(rows, cols):
+        extra = ref[span, rows + rows // 2 :, :]
+    elif ref.shape[2] > cols:
+        extra = ref[span, :, cols:]
+    else:
+        extra = ref[span, rows:, :]
+    row = lax.broadcasted_iota(jnp.int32, extra.shape, 1)
+    mine = jnp.where((row >= 3 * n) & (row < 3 * n + 3), extra.astype(f32), 0.0)
+    return jnp.sum(jnp.sum(mine, axis=0), axis=(0, 1), keepdims=True)
+
+
 def adam_kernel(owner, grads, moment, second, packed, moment_out, second_out):
-    rows, cols = moment.shape[1:]
-    packed_rows, packed_cols = packed.shape[1:]
     packed[...] = jnp.zeros_like(packed)
 
     def unit(u, carry):
@@ -60,13 +106,7 @@
         moment_out[u] = moment_new
         second_out[u] = second_new
         total = jnp.sum(direction * direction, axis=(0, 1), keepdims=True)
-        slot = owner[u]
-        if packed_cols > cols:
-            packed[slot, :, :cols] = summed.astype(bf16)
-            packed[slot, :, cols:] = pieces((total,), (packed_rows, packed_cols - cols))
-        else:
-            packed[slot, :rows, :] = summed.astype(bf16)
-            packed[slot, rows:, :] = pieces((total,), (packed_rows - rows, packed_cols))
+        pack(packed.at[owner[u]], summed, (total,))
         return carry
 
     lax.fori_loop(0, moment.shape[0], unit, 0, unroll=moment.shape[0] <= 4)
@@ -74,11 +114,10 @@
 
 def adam_part(owner, grads, moment, second, owners, params):
     rows, cols = moment.shape[1:]
-    packed = jax.ShapeDtypeStruct((owners, *packed_shape(rows, cols)), bf16)
     return pl.pallas_call(
         adam_kernel,
         out_shape=(
-            packed,
+            jax.ShapeDtypeStruct((owners, *packed_shape(rows, cols, 1)), bf16),
             jax.ShapeDtypeStruct(moment.shape, f32),
             jax.ShapeDtypeStruct(second.shape, f32),
         ),
@@ -99,49 +138,35 @@
     return found
 
 
-def block(ref, rows, cols, start=0, count=None):
-    count = ref.shape[0] if count is None else count
-    return ref[pl.ds(start, count), :rows, :cols].reshape(count * rows, cols)
-
-
-def shampoo_kernel(rows, cols, owner, *refs):
+def shampoo_kernel(rows, cols, turned, embed, owner, *refs):
     tensor = lax.axis_size("tensor")
-    left, grad, (root, *outs, whole, half) = refs[:tensor], refs[tensor : 2 * tensor], refs[2 * tensor :]
+    left, grad = refs[:tensor], refs[tensor : 2 * tensor]
+    root, *outs, whole, blocks, done = refs[2 * tensor :]
     part = lax.axis_index("tensor")
 
     @pl.when(holds(owner))
     def _():
         depth = left[0].shape[0]
-        for i in range(tensor):
-            place = pl.multiple_of((part ^ i) * depth, depth)
-            whole[pl.ds(place, depth), :] = left[i][...]
-        total = jnp.zeros((whole.shape[0], cols), f32)
         adam_sq = jnp.zeros((1, 1), f32)
         for k in range(tensor):
-            columns = block(grad[k], rows, cols)
-            half[k] = jnp.dot(whole[...], columns, preferred_element_type=f32).astype(bf16)
-            if grad[k].shape[2] > cols:
-                extra = grad[k][:, :, cols:]
-            else:
-                extra = grad[k][:, rows:, :]
-            extra = extra.astype(f32).reshape(-1, extra.shape[-1])
-            adam_sq = adam_sq + jnp.sum(extra, axis=(0, 1), keepdims=True)
+            whole[pl.ds(pl.multiple_of((part ^ k) * depth, depth), depth), :] = left[k][...]
+            blocks[part ^ k] = unpack(grad[k], rows, cols)
+            adam_sq = adam_sq + unpack_total(grad[k], rows, cols, 0)
+        half = jnp.zeros((whole.shape[0], cols), f32)
         for k in range(tensor):
             span = slice(k * cols, (k + 1) * cols)
-            if spare(cols):
+            if turned:
                 sides, right = (((1,), (1,)), ((), ())), root[0, :, span]
             else:
                 sides, right = (((1,), (0,)), ((), ())), root[0, span, :]
-            total = total + lax.dot_general(
-                half[part ^ k], right, sides, preferred_element_type=f32
-            )
+            half = half + lax.dot_general(blocks[k], right, sides, preferred_element_type=f32)
+        total = jnp.dot(whole[...], half.astype(bf16), preferred_element_type=f32)
         norm = jnp.sum(total * total, axis=(0, 1), keepdims=True)
-        if len(outs) == 1:
-            out = outs[0]
-            owners, high, wide = out.shape
-            out[:, :, :cols] = total.astype(bf16).reshape(owners, high, cols)
-            extra = pieces((norm, adam_sq), (high, wide - cols))
-            out[:, :, cols:] = jnp.broadcast_to(extra[None], (owners, *extra.shape))
+        if embed:
+            done[...] = total
+            for slot in range(outs[0].shape[0]):
+                value = done[slot * rows : (slot + 1) * rows, :]
+                pack(outs[0].at[slot], value, (norm, adam_sq))
         else:
             for ref, value in zip(outs, (total, norm, adam_sq)):
                 ref[...] = jnp.broadcast_to(value, ref.shape)
@@ -152,27 +177,28 @@
             ref[...] = jnp.zeros_like(ref)
 
 
-def spare(cols):
-    return round_up(cols, LANES) > cols
-
-
-def shampoo_part(owner, left, grad, root, rows):
+def shampoo_part(owner, left, grad, root, rows, embed):
     cols = root.shape[2]
     depth = left[0].shape[1]
-    if spare(cols):
+    tensor = len(left)
+    turned = cols % LANES != 0
+    if turned:
         root = jnp.swapaxes(root, 1, 2)
-    tensor = len(left)
-    small = jax.ShapeDtypeStruct((8, LANES), f32)
-    if spare(cols):
-        shapes = (jax.ShapeDtypeStruct((depth // rows, rows, round_up(cols, LANES)), bf16),)
+    if embed:
+        shapes = (jax.ShapeDtypeStruct((depth // rows, *packed_shape(rows, cols, 2)), bf16),)
     else:
+        small = jax.ShapeDtypeStruct((8, LANES), f32)
         shapes = (jax.ShapeDtypeStruct((depth, cols), f32), small, small)
     return pl.pallas_call(
-        functools.partial(shampoo_kernel, rows, cols),
+        functools.partial(shampoo_kernel, rows, cols, turned, embed),
         out_shape=shapes,
         in_specs=[SMEM] + [VMEM] * (2 * tensor + 1),
         out_specs=(VMEM,) * len(shapes),
-        scratch_shapes=[pltpu.VMEM((depth, depth), bf16), pltpu.VMEM((tensor, depth, cols), bf16)],
+        scratch_shapes=[
+            pltpu.VMEM((depth, depth), bf16),
+            pltpu.VMEM((tensor, depth, cols), bf16),
+            pltpu.VMEM((depth, cols) if embed else (8, LANES), f32),
+        ],
         compiler_params=LIMIT,
         cost_estimate=BRIEF,
     )(owner, *left, *grad, root)
@@ -194,11 +220,11 @@
     def _():
         high = left.shape[0]
         total = jnp.zeros(left.shape, f32)
-        mine = block(grad[0], rows, cols)
+        mine = unpack(grad[0], rows, cols)
         for k in range(tensor):
-            columns = block(grad[k], rows, cols)
+            columns = unpack(grad[k], rows, cols)
             slots = high // rows
-            band = block(grad[k], rows, cols, part * slots, slots)
+            band = unpack(grad[k], rows, cols, part * slots, slots)
             total = total + lax.dot_general(
                 band, columns, (((1,), (1,)), ((), ())), preferred_element_type=f32
             )
@@ -237,10 +263,10 @@
 
 def weight_kernel(owner, weight, back, *refs):
     *norm, out = refs
-    cols = weight.shape[2]
+    rows, cols = weight.shape[1:]
 
     def unit(u, carry):
-        update = back[owner[u], :, :cols].astype(f32)
+        update = unpack(back, rows, cols, owner[u], 1).astype(f32)
         if norm:
             adam, *norms = norm
             total = norms[0][u]
@@ -266,23 +292,20 @@
     )(owner, weight, back, *norm)
 
 
-def extra_kernel(cols, owner, back, norm, adam):
+def totals_kernel(rows, cols, owner, back, norm, adam):
     def unit(u, carry):
-        extra = back[owner[u], :, cols:].astype(f32)
-        row = lax.broadcasted_iota(jnp.int32, extra.shape, 0)
-        for ref, first in ((norm, 0), (adam, 3)):
-            mine = jnp.where((row >= first) & (row < first + 3), extra, 0.0)
-            total = jnp.sum(mine, axis=(0, 1), keepdims=True)
+        for n, ref in enumerate((norm, adam)):
+            total = unpack_total(back, rows, cols, n, owner[u], 1)
             ref[u] = jnp.broadcast_to(total, ref.shape[1:])
         return carry
 
     lax.fori_loop(0, norm.shape[0], unit, 0, unroll=norm.shape[0] <= 4)
 
 
-def extra_part(owner, back, cols):
+def totals_part(owner, back, rows, cols):
     small = jax.ShapeDtypeStruct((owner.shape[0], 8, LANES), f32)
     norm, adam = pl.pallas_call(
-        functools.partial(extra_kernel, cols),
+        functools.partial(totals_kernel, rows, cols),
         out_shape=(small, small),
         in_specs=[SMEM, VMEM],
         out_specs=(VMEM, VMEM),
@@ -294,13 +317,6 @@
 
 def all_norms(norm):
     return [norm] + [flip(norm, k) for k in range(1, lax.axis_size("tensor"))]
-
-
-def back_part(owner, weight, done, owners):
-    if len(done) == 1:
-        back = over_shard(done[0])
-        return weight_part(owner, weight, back, *extra_part(owner, back, weight.shape[2]))
-    return weight_part(owner, weight, over_shard(grafted(*done, owners)))
 
 
 def flip(value, bits):
@@ -337,14 +353,17 @@
     for other in norm[1:]:
         total = total + other[...]
     scale = jnp.sqrt(adam[...] / (total + graft_eps))[:1, :1]
-    out[...] = (scale * done[...]).astype(bf16)
+    rows = done.shape[0] // out.shape[0]
+    for slot in range(out.shape[0]):
+        pack(out.at[slot], scale * done[slot * rows : (slot + 1) * rows, :], ())
 
 
 def grafted(done, norm, adam, owners):
+    depth, cols = done.shape
     norms = all_norms(norm)
-    out = pl.pallas_call(
+    return pl.pallas_call(
         scale_kernel,
-        out_shape=jax.ShapeDtypeStruct(done.shape, bf16),
+        out_shape=jax.ShapeDtypeStruct((owners, *packed_shape(depth // owners, cols, 0)), bf16),
         in_specs=[VMEM] * (2 + len(norms)),
         out_specs=VMEM,
         compiler_params=LIMIT,
@@ -352,7 +371,6 @@
             flops=done.size, bytes_accessed=6 * done.size, transcendentals=0
         ),
     )(done, adam, *norms)
-    return out.reshape(owners, -1, done.shape[1])
 
 
 def per_device(
@@ -377,27 +395,30 @@
     owners = lax.axis_size("shard")
     rows = att_weight.shape[1]
     att_packed, att_moment_out, att_second_out = adam_part(
-        att_owner, att_grads, att_moment, att_second, owners, None
+        att_owner, att_grads, att_moment, att_second, owners, LIMIT
     )
     glu_packed, glu_moment_out, glu_second_out = adam_part(
-        glu_owner, glu_grads, glu_moment, glu_second, owners, LIMIT
-    )
-    att_root, att_root_far = spread_first(att_left_root[0])
-    att_near, att_far = spread_first(after(over_shard(att_packed), att_root_far, glu_packed))
+        glu_owner, glu_grads, glu_moment, glu_second, owners, None
+    )
+    glu_root, glu_root_far = spread_first(glu_left_root[0])
+    glu_near, glu_far = spread_first(after(over_shard(glu_packed), glu_root_far, att_packed))
+    glu_left = spread_rest(*lax.optimization_barrier((glu_root, glu_root_far, glu_near))[:2])
+    att_root, att_root_far = spread_first(after(att_left_root[0], glu_far))
+    glu_grad = spread_rest(glu_near, glu_far)
+    (glu_done,) = shampoo_part(glu_owner, glu_left, glu_grad, glu_right_root, rows, True)
+    att_near, att_far = spread_first(after(over_shard(att_packed), glu_done))
     att_left = spread_rest(*lax.optimization_barrier((att_root, att_root_far, att_near))[:2])
-    glu_root, glu_root_far = spread_first(after(glu_left_root[0], att_far))
-    att_grad = spread_rest(att_near, att_far)
-    att_done = shampoo_part(att_owner, att_left, att_grad, att_right_root, rows)
-    glu_near, glu_far = spread_first(after(over_shard(glu_packed), glu_root_far, *att_done))
-    glu_left = spread_rest(*lax.optimization_barrier((glu_root, glu_root_far, glu_near))[:2])
-    (att_stats_out,) = stats_part(att_owner, att_grad, (att_stats,), rows, att_weight.shape[2])
-    glu_grad = spread_rest(glu_near, after(glu_far, att_stats_out, *glu_left[1:]))
-    glu_done = shampoo_part(glu_owner, glu_left, glu_grad, glu_right_root, rows)
     glu_left_out, glu_right_out = stats_part(
         glu_owner, glu_grad, (glu_left_stat, glu_right_stat), rows, glu_weight.shape[2]
     )
-    att_weight_out = back_part(att_owner, att_weight, att_done, owners)
-    glu_weight_out = back_part(glu_owner, glu_weight, glu_done, owners)
+    glu_back = over_shard(glu_done)
+    att_grad = spread_rest(att_near, after(att_far, glu_left_out, *att_left[1:]))
+    att_done = shampoo_part(att_owner, att_left, att_grad, att_right_root, rows, False)
+    (att_stats_out,) = stats_part(att_owner, att_grad, (att_stats,), rows, att_weight.shape[2])
+    att_back = over_shard(grafted(*att_done, owners))
+    glu_totals = totals_part(glu_owner, glu_back, rows, glu_weight.shape[2])
+    glu_weight_out = weight_part(glu_owner, glu_weight, glu_back, *glu_totals)
+    att_weight_out = weight_part(att_owner, att_weight, att_back)
     return (
         att_weight_out,
         att_moment_out,

time: 83.8 us -> 80.4 us (0.959)
  starting transfers between devices: 37.6 us -> 32.7 us
  waiting for transfers between devices: 24.5 us -> 20.7 us
  local copies, waits for them, and re-layouts: 1.32 us -> 5.06 us
  Pallas kernels: 19.1 us -> 20.9 us
    all_to_all x4, starting transfers between devices: 26 us -> 21.6 us  [over_shard(): lax.all_to_all(value, 'shard', split_axis=0, concat_axis=0, tiled=True)]
    unnamed x26 -> x32, local copies, waits for them, and re-layouts: 1.32 us -> 5.06 us
    all_to_all x4, waiting for transfers between devices: 8.5 us -> 5.84 us  [over_shard(): lax.all_to_all(value, 'shard', split_axis=0, concat_axis=0, tiled=True)]
    pallas_call x2, Pallas kernels: 4.54 us -> 5.78 us  [stats_part(): pl.pallas_call(functools.partial(stats_kernel, rows, cols, len(stats) ==...]
    ppermute x18, waiting for transfers between devices: 16 us -> 14.9 us  [flip(): return lax.ppermute(value, 'tensor', [(i, i ^ bits) for i in range(size)])]
  transfers between devices with their start and end apart: 22 -> 22, of which waited for: 12 -> 10; matrix products, arithmetic and copies ran while one was open for 0% -> 0% of each run, Pallas kernels for 18% -> 21%
where the time goes in v6:
time: 80.4 us; the launch traced here: 80.1 us
  starting transfers between devices  32.7 us (41%)
  Pallas kernels  20.9 us (26%)
  waiting for transfers between devices  20.7 us (26%)
  local copies, waits for them, and re-layouts  5.06 us (6%)
  between operations  0.82 us (1%)
    all_to_all x4, starting transfers between devices, over_shard(): lax.all_to_all(value, 'shard', split_axis=0, concat_axis=0, tiled=True)  21.6 us
    ppermute x18, waiting for transfers between devices, flip(): return lax.ppermute(value, 'tensor', [(i, i ^ bits) for i in range(size)])  14.9 us
    ppermute x18, starting transfers between devices, flip(): return lax.ppermute(value, 'tensor', [(i, i ^ bits) for i in range(size)])  11.1 us
    pallas_call x2, Pallas kernels, shampoo_part(): pl.pallas_call(functools.partial(shampoo_kernel, rows, cols, turned, embe...  6.23 us
    all_to_all x4, waiting for transfers between devices, over_shard(): lax.all_to_all(value, 'shard', split_axis=0, concat_axis=0, tiled=True)  5.84 us
    pallas_call x2, Pallas kernels, stats_part(): pl.pallas_call(functools.partial(stats_kernel, rows, cols, len(stats) ==...  5.78 us
    unnamed x32, local copies, waits for them, and re-layouts  5.06 us
    pallas_call x2, Pallas kernels, adam_part(): pl.pallas_call(adam_kernel, out_shape=(jax.ShapeDtypeStruct((owners, *pac...  4.52 us
  transfers between devices with their start and end apart: 22, of which 10 were waited for; matrix products, arithmetic and copies ran while one was open for 0% of the time, Pallas kernels for 21%

profile of v6, /device:TPU:0, one launch (start us, length us, event | category | flops | bytes accessed | tf_op | source)
XLA Modules:
  0.0 80.1 jit_solution(17602596211516422992)
XLA Ops:
  0.7 2.7 %shard_map.232 = (bf16[8,104,256]{2,1,0:T(8,128)(2,1)}, f32[4,96,256]{2,1,0:T(8,128)}, f32[4,96,256]{2,1,0:T(8,128)}) custom-call(s32[4]{0:T(128)} %owner.16, f32[2,4,96,256]{3,2,1,0:T(8,128)} %grads.2, f32[4,96,256]{2,1,0:T(8,128)} %moment.2, f32[4,96,256]{2,1,0:T(8,128)} %second.2), custom_call_target="tpu_custom_call" | custom-call | flops 1966080 | bytes 3145728 | tf_op jit(solution)/shard_map/pallas_call | solution.py:117
  3.4 7.3 %all-to-all-start = ((bf16[8,104,256]{2,1,0:T(8,128)(2,1)}), bf16[8,104,256]{2,1,0:T(8,128)(2,1)S(1)}, u32[]{:S(2)}, u32[]{:S(2)}) async-start(bf16[8,104,256]{2,1,0:T(8,128)(2,1)} %get-tuple-element.30), calls=%async_computation | async-start | bytes 851968 | tf_op jit(solution)/shard_map/all_to_all | solution.py:347
  10.7 1.6 %collective-permute-start = (bf16[192,768]{1,0:T(8,128)(2,1)S(1)}, bf16[192,768]{1,0:T(8,128)(2,1)}, u32[]{:S(2)}, u32[]{:S(2)}) collective-permute-start(bf16[192,768]{1,0:T(8,128)(2,1)S(1)} %bitcast.3), channel_id=1, source_target_pairs={{0,2},{1,3},{2,0},{3,1},{4,6},{5,7},{6,4},{7,5},{8,10},{9,11},{10,... | collective-permute-start | bytes 884744 | tf_op jit(solution)/shard_map/ppermute | solution.py:324
  12.3 1.8 %shard_map.233 = (bf16[8,152,128]{2,1,0:T(8,128)(2,1)}, f32[4,96,192]{2,1,0:T(8,128)}, f32[4,96,192]{2,1,0:T(8,128)}) custom-call(s32[4]{0:T(128)S(1)} %copy-done.13, f32[2,4,96,192]{3,2,1,0:T(8,128)S(1)} %copy-done.1, f32[4,96,192]{2,1,0:T(8,128)S(1)} %copy-done.5, f32[4,96,192]{2,1,0:T(8,128)S(1)} %copy-done.6), custom_call_target="tpu_custom_call" | custom-call | flops 1474560 | bytes 2359296 | tf_op jit(solution)/shard_map/pallas_call | solution.py:117
  14.1 5.3 %collective-permute-done.refs_2_ = bf16[192,768]{1,0:T(8,128)(2,1)} collective-permute-done((bf16[192,768]{1,0:T(8,128)(2,1)S(1)}, bf16[192,768]{1,0:T(8,128)(2,1)}, u32[]{:S(2)}, u32[]{:S(2)}) %collective-permute-start) | collective-permute-done | bytes 294944 | tf_op jit(solution)/shard_map/ppermute | solution.py:324
  19.4 3.7 %all-to-all-done.refs_4_.refs_0_ = bf16[8,104,256]{2,1,0:T(8,128)(2,1)S(1)} async-done(((bf16[8,104,256]{2,1,0:T(8,128)(2,1)}), bf16[8,104,256]{2,1,0:T(8,128)(2,1)S(1)}, u32[]{:S(2)}, u32[]{:S(2)}) %all-to-all-start) | async-done | bytes 426016 | tf_op jit(solution)/shard_map/all_to_all | solution.py:347
  23.1 1.5 %collective-permute-start.1 = (bf16[8,104,256]{2,1,0:T(8,128)(2,1)S(1)}, bf16[8,104,256]{2,1,0:T(8,128)(2,1)S(1)}, u32[]{:S(2)}, u32[]{:S(2)}) collective-permute-start(bf16[8,104,256]{2,1,0:T(8,128)(2,1)S(1)} %all-to-all-done.refs_4_.refs_0_), channel_id=1, source_target_pairs={{0,2},{1,3},{2,0},{3,1},{4,6},{5,7},{6,4},{7,5},{8,10},{9,11},{10,... | collective-permute-start | bytes 1277960 | tf_op jit(solution)/shard_map/ppermute | solution.py:324
  24.6 3.6 %all-to-all-start.1 = ((bf16[8,152,128]{2,1,0:T(8,128)(2,1)}), bf16[8,152,128]{2,1,0:T(8,128)(2,1)S(1)}, u32[]{:S(2)}, u32[]{:S(2)}) async-start(bf16[8,152,128]{2,1,0:T(8,128)(2,1)} %get-tuple-element.31), calls=%async_computation.1 | async-start | bytes 622592 | tf_op jit(solution)/shard_map/all_to_all | solution.py:347
  28.2 3.4 %collective-permute-done.1.refs_6_.refs_2_ = bf16[8,104,256]{2,1,0:T(8,128)(2,1)S(1)} collective-permute-done((bf16[8,104,256]{2,1,0:T(8,128)(2,1)S(1)}, bf16[8,104,256]{2,1,0:T(8,128)(2,1)S(1)}, u32[]{:S(2)}, u32[]{:S(2)}) %collective-permute-start.1) | collective-permute-done | bytes 426016 | tf_op jit(solution)/shard_map/ppermute | solution.py:324
  32.1 1.5 %collective-permute-start.2 = (bf16[192,768]{1,0:T(8,128)(2,1)}, bf16[192,768]{1,0:T(8,128)(2,1)}, u32[]{:S(2)}, u32[]{:S(2)}) collective-permute-start(bf16[192,768]{1,0:T(8,128)(2,1)} %bitcast.6), channel_id=1, source_target_pairs={{0,2},{1,3},{2,0},{3,1},{4,6},{5,7},{6,4},{7,5},{8,10},{9,11},{10,... | collective-permute-start | bytes 884744 | tf_op jit(solution)/shard_map/ppermute | solution.py:324
  34.5 3.4 %shard_map.234 = bf16[8,104,256]{2,1,0:T(8,128)(2,1)} custom-call(s32[4]{0:T(128)S(1)} %copy-done.12, bf16[192,768]{1,0:T(8,128)(2,1)S(1)} %bitcast.5, bf16[192,768]{1,0:T(8,128)(2,1)S(1)} %collective-permute-done.3.refs_1_, bf16[192,768]{1,0:T(8,128)(2,1)} %collective-permute-done.refs_2_, bf16[192,768]{1,0:T(8,128)(2,1)S(1)} %collective-permute-done.4.refs_3_, ...), custom_call_target="tpu_custom_call" | custom-call | flops 1024 | bytes 1024 | tf_op jit(solution)/shard_map/pallas_call | solution.py:192
  38.6 5.0 %all-to-all-start.3 = ((bf16[8,104,256]{2,1,0:T(8,128)(2,1)}), bf16[8,104,256]{2,1,0:T(8,128)(2,1)S(1)}, u32[]{:S(2)}, u32[]{:S(2)}) async-start(bf16[8,104,256]{2,1,0:T(8,128)(2,1)} %shard_map.234), calls=%async_computation.3 | async-start | bytes 851968 | tf_op jit(solution)/shard_map/all_to_all | solution.py:347
  43.7 1.5 %collective-permute-start.10 = (bf16[8,152,128]{2,1,0:T(8,128)(2,1)S(1)}, bf16[8,152,128]{2,1,0:T(8,128)(2,1)S(1)}, u32[]{:S(2)}, u32[]{:S(2)}) collective-permute-start(bf16[8,152,128]{2,1,0:T(8,128)(2,1)S(1)} %all-to-all-done.1.refs_4_.refs_0_), channel_id=1, source_target_pairs={{0,2},{1,3},{2,0},{3,1},{4,6},{5,7},{6,4},{7,5},{8,10},{9,11},{10,... | collective-permute-start | bytes 933896 | tf_op jit(solution)/shard_map/ppermute | solution.py:324
  49.1 2.9 %shard_map.235 = (f32[1,192,768]{2,1,0:T(8,128)}, f32[1,256,1024]{2,1,0:T(8,128)}) custom-call(s32[4]{0:T(128)S(1)} %copy-done.12, bf16[8,104,256]{2,1,0:T(8,128)(2,1)S(1)} %all-to-all-done.refs_4_.refs_0_, bf16[8,104,256]{2,1,0:T(8,128)(2,1)S(1)} %collective-permute-done.5.refs_5_.refs_1_, bf16[8,104,256]{2,1,0:T(8,128)(2,1)S(1)} %collective-permute-done.1.refs_6_.refs_2_, ...), custom_call_target="tpu_custom_call" | custom-call | flops 1073741824 | bytes 5373952 | tf_op jit(solution)/shard_map/pallas_call | solution.py:249
  52.8 1.6 %collective-permute-done.11.refs_7_.refs_3_ = bf16[8,152,128]{2,1,0:T(8,128)(2,1)S(1)} collective-permute-done((bf16[8,152,128]{2,1,0:T(8,128)(2,1)S(1)}, bf16[8,152,128]{2,1,0:T(8,128)(2,1)S(1)}, u32[]{:S(2)}, u32[]{:S(2)}) %collective-permute-start.11) | collective-permute-done | bytes 311328 | tf_op jit(solution)/shard_map/ppermute | solution.py:324
  55.3 2.8 %shard_map.236 = (f32[768,192]{1,0:T(8,128)S(1)}, f32[8,128]{1,0:T(8,128)S(1)}, f32[8,128]{1,0:T(8,128)S(1)}) custom-call(s32[4]{0:T(128)S(1)} %copy-done.13, bf16[192,768]{1,0:T(8,128)(2,1)S(1)} %bitcast.8, bf16[192,768]{1,0:T(8,128)(2,1)S(1)} %collective-permute-done.7.refs_1_, bf16[192,768]{1,0:T(8,128)(2,1)} %collective-permute-done.2.refs_2_, ...), custom_call_target="tpu_custom_call" | custom-call | flops 1024 | bytes 1024 | tf_op jit(solution)/shard_map/pallas_call | solution.py:192
  58.2 1.3 %collective-permute-start.14 = (f32[8,128]{1,0:T(8,128)S(1)}, f32[8,128]{1,0:T(8,128)S(1)}, u32[]{:S(2)}, u32[]{:S(2)}) collective-permute-start(f32[8,128]{1,0:T(8,128)S(1)} %get-tuple-element.43.refs_0_), channel_id=1, source_target_pairs={{0,3},{1,2},{2,1},{3,0},{4,7},{5,6},{6,5},{7,4},{8,11},{9,10},{10,... | collective-permute-start | bytes 12296 | tf_op jit(solution)/shard_map/ppermute | solution.py:324
  61.3 1.8 %collective-permute-done.13.refs_2_ = f32[8,128]{1,0:T(8,128)S(1)} collective-permute-done((f32[8,128]{1,0:T(8,128)S(1)}, f32[8,128]{1,0:T(8,128)S(1)}, u32[]{:S(2)}, u32[]{:S(2)}) %collective-permute-start.13) | collective-permute-done | bytes 4128 | tf_op jit(solution)/shard_map/ppermute | solution.py:324
  64.0 5.7 %all-to-all-start.2 = ((bf16[8,144,128]{2,1,0:T(8,128)(2,1)}), bf16[8,144,128]{2,1,0:T(8,128)(2,1)S(1)}, u32[]{:S(2)}, u32[]{:S(2)}) async-start(bf16[8,144,128]{2,1,0:T(8,128)(2,1)} %shard_map.237), calls=%async_computation.2 | async-start | bytes 589824 | tf_op jit(solution)/shard_map/all_to_all | solution.py:347
  71.1 1.3 %collective-permute-start.15 = (f32[4,8,128]{2,1,0:T(8,128)S(1)}, f32[4,8,128]{2,1,0:T(8,128)S(1)}, u32[]{:S(2)}, u32[]{:S(2)}) collective-permute-start(f32[4,8,128]{2,1,0:T(8,128)S(1)} %get-tuple-element.47.refs_1_), channel_id=1, source_target_pairs={{0,1},{1,0},{2,3},{3,2},{4,5},{5,4},{6,7},{7,6},{8,9},{9,8},{10,11... | collective-permute-start | bytes 49160 | tf_op jit(solution)/shard_map/ppermute | solution.py:324
  72.4 2.8 %shard_map.241 = f32[1,2,192,768]{3,2,1,0:T(8,128)} custom-call(s32[4]{0:T(128)S(1)} %copy-done.13, bf16[8,152,128]{2,1,0:T(8,128)(2,1)S(1)} %all-to-all-done.1.refs_4_.refs_0_, bf16[8,152,128]{2,1,0:T(8,128)(2,1)S(1)} %collective-permute-done.9.refs_5_.refs_1_, bf16[8,152,128]{2,1,0:T(8,128)(2,1)S(1)} %collective-permute-done.10.refs_6_.refs_2_, ...), custom_call_target="tpu_custom_call" | custom-call | flops 452984832 | bytes 3538944 | tf_op jit(solution)/shard_map/pallas_call | solution.py:249
  75.2 1.4 %shard_map.240 = f32[4,96,256]{2,1,0:T(8,128)} custom-call(s32[4]{0:T(128)S(1)} %copy-done.12, f32[4,96,256]{2,1,0:T(8,128)S(1)} %copy-done.7, bf16[8,104,256]{2,1,0:T(8,128)(2,1)S(1)} %all-to-all-done.3.back, f32[4,8,128]{2,1,0:T(8,128)S(1)} %get-tuple-element.46.refs_0_, f32[4,8,128]{2,1,0:T(8,128)S(1)} %get-tuple-element.47.refs_1_, ...), custom_call_target="tpu_custom_call" | custom-call | flops 196608 | bytes 1179648 | tf_op jit(solution)/shard_map/pallas_call | solution.py:283
  76.6 2.1 %all-to-all-done.2.back = bf16[8,144,128]{2,1,0:T(8,128)(2,1)S(1)} async-done(((bf16[8,144,128]{2,1,0:T(8,128)(2,1)}), bf16[8,144,128]{2,1,0:T(8,128)(2,1)S(1)}, u32[]{:S(2)}, u32[]{:S(2)}) %all-to-all-start.2) | async-done | bytes 294944 | tf_op jit(solution)/shard_map/all_to_all | solution.py:347
  78.7 1.4 %shard_map.238 = f32[4,96,192]{2,1,0:T(8,128)} custom-call(s32[4]{0:T(128)S(1)} %copy-done.13, f32[4,96,192]{2,1,0:T(8,128)S(1)} %copy-done.8, bf16[8,144,128]{2,1,0:T(8,128)(2,1)S(1)} %all-to-all-done.2.back), custom_call_target="tpu_custom_call" | custom-call | flops 147456 | bytes 884736 | tf_op jit(solution)/shard_map/pallas_call | solution.py:283
  (62 shorter events, 11.7 us)
Async XLA Ops:
  3.4 19.6 %all-to-all-start = ((bf16[8,104,256]{2,1,0:T(8,128)(2,1)}), bf16[8,104,256]{2,1,0:T(8,128)(2,1)S(1)}, u32[]{:S(2)}, u32[]{:S(2)}) async-start(bf16[8,104,256]{2,1,0:T(8,128)(2,1)} %get-tuple-element.30), calls=%async_computation | async-start | bytes 851968 | tf_op jit(solution)/shard_map/all_to_all | solution.py:347
  10.7 23.8 %copy-start.2 = (bf16[1,1024,256]{2,1,0:T(8,128)(2,1)S(1)}, bf16[1,1024,256]{2,1,0:T(8,128)(2,1)}, u32[]{:S(2)}) copy-start(bf16[1,1024,256]{2,1,0:T(8,128)(2,1)} %refs_8_.1) | copy-start | bytes 1572868
  10.7 23.8 %copy-start.12 = (s32[4]{0:T(128)S(1)}, s32[4]{0:T(128)}, u32[]{:S(2)}) copy-start(s32[4]{0:T(128)} %owner.16) | copy-start | bytes 52
  10.7 8.6 %collective-permute-start = (bf16[192,768]{1,0:T(8,128)(2,1)S(1)}, bf16[192,768]{1,0:T(8,128)(2,1)}, u32[]{:S(2)}, u32[]{:S(2)}) collective-permute-start(bf16[192,768]{1,0:T(8,128)(2,1)S(1)} %bitcast.3), channel_id=1, source_target_pairs={{0,2},{1,3},{2,0},{3,1},{4,6},{5,7},{6,4},{7,5},{8,10},{9,11},{10,... | collective-permute-start | bytes 884744 | tf_op jit(solution)/shard_map/ppermute | solution.py:324
  23.1 8.6 %collective-permute-start.1 = (bf16[8,104,256]{2,1,0:T(8,128)(2,1)S(1)}, bf16[8,104,256]{2,1,0:T(8,128)(2,1)S(1)}, u32[]{:S(2)}, u32[]{:S(2)}) collective-permute-start(bf16[8,104,256]{2,1,0:T(8,128)(2,1)S(1)} %all-to-all-done.refs_4_.refs_0_), channel_id=1, source_target_pairs={{0,2},{1,3},{2,0},{3,1},{4,6},{5,7},{6,4},{7,5},{8,10},{9,11},{10,... | collective-permute-start | bytes 1277960 | tf_op jit(solution)/shard_map/ppermute | solution.py:324
  24.6 14.1 %all-to-all-start.1 = ((bf16[8,152,128]{2,1,0:T(8,128)(2,1)}), bf16[8,152,128]{2,1,0:T(8,128)(2,1)S(1)}, u32[]{:S(2)}, u32[]{:S(2)}) async-start(bf16[8,152,128]{2,1,0:T(8,128)(2,1)} %get-tuple-element.31), calls=%async_computation.1 | async-start | bytes 622592 | tf_op jit(solution)/shard_map/all_to_all | solution.py:347
  28.2 6.2 %collective-permute-start.5 = (bf16[8,104,256]{2,1,0:T(8,128)(2,1)S(1)}, bf16[8,104,256]{2,1,0:T(8,128)(2,1)S(1)}, u32[]{:S(2)}, u32[]{:S(2)}) collective-permute-start(bf16[8,104,256]{2,1,0:T(8,128)(2,1)S(1)} %all-to-all-done.refs_4_.refs_0_), channel_id=1, source_target_pairs={{0,1},{1,0},{2,3},{3,2},{4,5},{5,4},{6,7},{7,6},{8,9},{9,8},{10,11... | collective-permute-start | bytes 1277960 | tf_op jit(solution)/shard_map/ppermute | solution.py:324
  31.6 2.8 %collective-permute-start.6 = (bf16[8,104,256]{2,1,0:T(8,128)(2,1)S(1)}, bf16[8,104,256]{2,1,0:T(8,128)(2,1)S(1)}, u32[]{:S(2)}, u32[]{:S(2)}) collective-permute-start(bf16[8,104,256]{2,1,0:T(8,128)(2,1)S(1)} %collective-permute-done.1.refs_6_.refs_2_), channel_id=1, source_target_pairs={{0,1},{1,0},{2,3},{3,2},{4,5},{5,4},{6,7},{7,6},{8,9},{9,8},{10,11... | collective-permute-start | bytes 1277960 | tf_op jit(solution)/shard_map/ppermute | solution.py:324
  31.6 2.6 %collective-permute-start.3 = (bf16[192,768]{1,0:T(8,128)(2,1)S(1)}, bf16[192,768]{1,0:T(8,128)(2,1)S(1)}, u32[]{:S(2)}, u32[]{:S(2)}) collective-permute-start(bf16[192,768]{1,0:T(8,128)(2,1)S(1)} %bitcast.4), channel_id=1, source_target_pairs={{0,1},{1,0},{2,3},{3,2},{4,5},{5,4},{6,7},{7,6},{8,9},{9,8},{10,11... | collective-permute-start | bytes 884744 | tf_op jit(solution)/shard_map/ppermute | solution.py:324
  32.1 2.3 %collective-permute-start.4 = (bf16[192,768]{1,0:T(8,128)(2,1)}, bf16[192,768]{1,0:T(8,128)(2,1)S(1)}, u32[]{:S(2)}, u32[]{:S(2)}) collective-permute-start(bf16[192,768]{1,0:T(8,128)(2,1)} %collective-permute-done.refs_2_), channel_id=1, source_target_pairs={{0,1},{1,0},{2,3},{3,2},{4,5},{5,4},{6,7},{7,6},{8,9},{9,8},{10,11... | collective-permute-start | bytes 884744 | tf_op jit(solution)/shard_map/ppermute | solution.py:324
  32.1 13.0 %collective-permute-start.2 = (bf16[192,768]{1,0:T(8,128)(2,1)}, bf16[192,768]{1,0:T(8,128)(2,1)}, u32[]{:S(2)}, u32[]{:S(2)}) collective-permute-start(bf16[192,768]{1,0:T(8,128)(2,1)} %bitcast.6), channel_id=1, source_target_pairs={{0,2},{1,3},{2,0},{3,1},{4,6},{5,7},{6,4},{7,5},{8,10},{9,11},{10,... | collective-permute-start | bytes 884744 | tf_op jit(solution)/shard_map/ppermute | solution.py:324
  38.6 25.4 %all-to-all-start.3 = ((bf16[8,104,256]{2,1,0:T(8,128)(2,1)}), bf16[8,104,256]{2,1,0:T(8,128)(2,1)S(1)}, u32[]{:S(2)}, u32[]{:S(2)}) async-start(bf16[8,104,256]{2,1,0:T(8,128)(2,1)} %shard_map.234), calls=%async_computation.3 | async-start | bytes 851968 | tf_op jit(solution)/shard_map/all_to_all | solution.py:347
  43.7 9.1 %collective-permute-start.10 = (bf16[8,152,128]{2,1,0:T(8,128)(2,1)S(1)}, bf16[8,152,128]{2,1,0:T(8,128)(2,1)S(1)}, u32[]{:S(2)}, u32[]{:S(2)}) collective-permute-start(bf16[8,152,128]{2,1,0:T(8,128)(2,1)S(1)} %all-to-all-done.1.refs_4_.refs_0_), channel_id=1, source_target_pairs={{0,2},{1,3},{2,0},{3,1},{4,6},{5,7},{6,4},{7,5},{8,10},{9,11},{10,... | collective-permute-start | bytes 933896 | tf_op jit(solution)/shard_map/ppermute | solution.py:324
  45.2 6.8 %collective-permute-start.7 = (bf16[192,768]{1,0:T(8,128)(2,1)S(1)}, bf16[192,768]{1,0:T(8,128)(2,1)S(1)}, u32[]{:S(2)}, u32[]{:S(2)}) collective-permute-start(bf16[192,768]{1,0:T(8,128)(2,1)S(1)} %bitcast.7), channel_id=1, source_target_pairs={{0,1},{1,0},{2,3},{3,2},{4,5},{5,4},{6,7},{7,6},{8,9},{9,8},{10,11... | collective-permute-start | bytes 884744 | tf_op jit(solution)/shard_map/ppermute | solution.py:324
  45.2 6.8 %collective-permute-start.8 = (bf16[192,768]{1,0:T(8,128)(2,1)}, bf16[192,768]{1,0:T(8,128)(2,1)S(1)}, u32[]{:S(2)}, u32[]{:S(2)}) collective-permute-start(bf16[192,768]{1,0:T(8,128)(2,1)} %collective-permute-done.2.refs_2_), channel_id=1, source_target_pairs={{0,1},{1,0},{2,3},{3,2},{4,5},{5,4},{6,7},{7,6},{8,9},{9,8},{10,11... | collective-permute-start | bytes 884744 | tf_op jit(solution)/shard_map/ppermute | solution.py:324
  45.7 7.1 %collective-permute-start.9 = (bf16[8,152,128]{2,1,0:T(8,128)(2,1)S(1)}, bf16[8,152,128]{2,1,0:T(8,128)(2,1)S(1)}, u32[]{:S(2)}, u32[]{:S(2)}) collective-permute-start(bf16[8,152,128]{2,1,0:T(8,128)(2,1)S(1)} %all-to-all-done.1.refs_4_.refs_0_), channel_id=1, source_target_pairs={{0,1},{1,0},{2,3},{3,2},{4,5},{5,4},{6,7},{7,6},{8,9},{9,8},{10,11... | collective-permute-start | bytes 933896 | tf_op jit(solution)/shard_map/ppermute | solution.py:324
  52.8 1.6 %collective-permute-start.11 = (bf16[8,152,128]{2,1,0:T(8,128)(2,1)S(1)}, bf16[8,152,128]{2,1,0:T(8,128)(2,1)S(1)}, u32[]{:S(2)}, u32[]{:S(2)}) collective-permute-start(bf16[8,152,128]{2,1,0:T(8,128)(2,1)S(1)} %collective-permute-done.10.refs_6_.refs_2_), channel_id=1, source_target_pairs={{0,1},{1,0},{2,3},{3,2},{4,5},{5,4},{6,7},{7,6},{8,9},{9,8},{10,11... | collective-permute-start | bytes 933896 | tf_op jit(solution)/shard_map/ppermute | solution.py:324
  58.2 3.1 %collective-permute-start.14 = (f32[8,128]{1,0:T(8,128)S(1)}, f32[8,128]{1,0:T(8,128)S(1)}, u32[]{:S(2)}, u32[]{:S(2)}) collective-permute-start(f32[8,128]{1,0:T(8,128)S(1)} %get-tuple-element.43.refs_0_), channel_id=1, source_target_pairs={{0,3},{1,2},{2,1},{3,0},{4,7},{5,6},{6,5},{7,4},{8,11},{9,10},{10,... | collective-permute-start | bytes 12296 | tf_op jit(solution)/shard_map/ppermute | solution.py:324
  59.5 3.6 %collective-permute-start.13 = (f32[8,128]{1,0:T(8,128)S(1)}, f32[8,128]{1,0:T(8,128)S(1)}, u32[]{:S(2)}, u32[]{:S(2)}) collective-permute-start(f32[8,128]{1,0:T(8,128)S(1)} %get-tuple-element.43.refs_0_), channel_id=1, source_target_pairs={{0,2},{1,3},{2,0},{3,1},{4,6},{5,7},{6,4},{7,5},{8,10},{9,11},{10,... | collective-permute-start | bytes 12296 | tf_op jit(solution)/shard_map/ppermute | solution.py:324
  60.0 3.1 %collective-permute-start.12 = (f32[8,128]{1,0:T(8,128)S(1)}, f32[8,128]{1,0:T(8,128)S(1)}, u32[]{:S(2)}, u32[]{:S(2)}) collective-permute-start(f32[8,128]{1,0:T(8,128)S(1)} %get-tuple-element.43.refs_0_), channel_id=1, source_target_pairs={{0,1},{1,0},{2,3},{3,2},{4,5},{5,4},{6,7},{7,6},{8,9},{9,8},{10,11... | collective-permute-start | bytes 12296 | tf_op jit(solution)/shard_map/ppermute | solution.py:324
  64.0 14.7 %all-to-all-start.2 = ((bf16[8,144,128]{2,1,0:T(8,128)(2,1)}), bf16[8,144,128]{2,1,0:T(8,128)(2,1)S(1)}, u32[]{:S(2)}, u32[]{:S(2)}) async-start(bf16[8,144,128]{2,1,0:T(8,128)(2,1)} %shard_map.237), calls=%async_computation.2 | async-start | bytes 589824 | tf_op jit(solution)/shard_map/all_to_all | solution.py:347
  70.4 4.8 %collective-permute-start.17 = (f32[4,8,128]{2,1,0:T(8,128)S(1)}, f32[4,8,128]{2,1,0:T(8,128)S(1)}, u32[]{:S(2)}, u32[]{:S(2)}) collective-permute-start(f32[4,8,128]{2,1,0:T(8,128)S(1)} %get-tuple-element.47.refs_1_), channel_id=1, source_target_pairs={{0,3},{1,2},{2,1},{3,0},{4,7},{5,6},{6,5},{7,4},{8,11},{9,10},{10,... | collective-permute-start | bytes 49160 | tf_op jit(solution)/shard_map/ppermute | solution.py:324
  70.5 4.7 %collective-permute-start.16 = (f32[4,8,128]{2,1,0:T(8,128)S(1)}, f32[4,8,128]{2,1,0:T(8,128)S(1)}, u32[]{:S(2)}, u32[]{:S(2)}) collective-permute-start(f32[4,8,128]{2,1,0:T(8,128)S(1)} %get-tuple-element.47.refs_1_), channel_id=1, source_target_pairs={{0,2},{1,3},{2,0},{3,1},{4,6},{5,7},{6,4},{7,5},{8,10},{9,11},{10,... | collective-permute-start | bytes 49160 | tf_op jit(solution)/shard_map/ppermute | solution.py:324
  71.1 4.1 %collective-permute-start.15 = (f32[4,8,128]{2,1,0:T(8,128)S(1)}, f32[4,8,128]{2,1,0:T(8,128)S(1)}, u32[]{:S(2)}, u32[]{:S(2)}) collective-permute-start(f32[4,8,128]{2,1,0:T(8,128)S(1)} %get-tuple-element.47.refs_1_), channel_id=1, source_target_pairs={{0,1},{1,0},{2,3},{3,2},{4,5},{5,4},{6,7},{7,6},{8,9},{9,8},{10,11... | collective-permute-start | bytes 49160 | tf_op jit(solution)/shard_map/ppermute | solution.py:324
  (14 other events, 97.2 us)
